TPU v7x, 32 devices: a whole 2x2x4 slice. The times are simulated.
32 devices in a mesh: dp: 4 (over z), seq: 8 (over y, x, core).
Axes of the slice: x: 2, y: 2, z: 4, core: 2. Of those that a mesh axis runs over, the one named last changes fastest.
Arguments:
- tokens: bfloat16 [4, 1024, 896], P('dp', 'seq'), may hold values from -6 to 6
- retrieved: bfloat16 [4, 16, 2, 128, 896], P('dp', 'seq'), may hold values from -6 to 6
- span_doc: int32 [4, 16], P('dp', 'seq'), may hold values from 0 to 3
- neigh_doc: int32 [4, 16, 2], P('dp', 'seq'), may hold values from 0 to 3
- cotangent: bfloat16 [4, 1024, 896], P('dp', 'seq'), may hold values from -6 to 6
- dec_gain: bfloat16 [2, 2, 896], P(None, None, ('dp', 'seq')), may hold values from 0.5 to 1.5
- dec_qkv: bfloat16 [2, 896, 2688], P(None, ('dp', 'seq')), may hold values from -0.1875 to 0.1875
- dec_out: bfloat16 [2, 896, 896], P(None, ('dp', 'seq')), may hold values from -1.5 to 1.5
- dec_in: bfloat16 [2, 896, 3584], P(None, ('dp', 'seq')), may hold values from -0.1875 to 0.1875
- dec_down: bfloat16 [2, 3584, 896], P(None, ('dp', 'seq')), may hold values from -0.09375 to 0.09375
- cca_gain: bfloat16 [896], P(('dp', 'seq')), may hold values from 0.5 to 1.5
- cca_q: bfloat16 [896, 896], P(('dp', 'seq')), may hold values from -0.1875 to 0.1875
- cca_kv: bfloat16 [896, 1792], P(('dp', 'seq')), may hold values from -0.1875 to 0.1875
- cca_out: bfloat16 [896, 896], P(('dp', 'seq')), may hold values from -1.5 to 1.5
- enc_gain: bfloat16 [2, 896], P(None, ('dp', 'seq')), may hold values from 0.5 to 1.5
- enc_in: bfloat16 [2, 896, 3584], P(None, ('dp', 'seq')), may hold values from -0.1875 to 0.1875
- enc_down: bfloat16 [2, 3584, 896], P(None, ('dp', 'seq')), may hold values from -0.09375 to 0.09375
- enc_final: bfloat16 [896], P(('dp', 'seq')), may hold values from 0.5 to 1.5
Outputs:
- result: bfloat16 [4, 1024, 896], P('dp', 'seq')
- tokens_grad: float32 [4, 1024, 896], P('dp', 'seq')
- dec_gain_grad: float32 [2, 2, 896], P(None, None, ('dp', 'seq'))
- dec_qkv_grad: float32 [2, 896, 2688], P(None, ('dp', 'seq'))
- dec_out_grad: float32 [2, 896, 896], P(None, ('dp', 'seq'))
- dec_in_grad: float32 [2, 896, 3584], P(None, ('dp', 'seq'))
- dec_down_grad: float32 [2, 3584, 896], P(None, None, ('dp', 'seq'))
- cca_gain_grad: float32 [896], P(('dp', 'seq'))
- cca_q_grad: float32 [896, 896], P(('dp', 'seq'))
- cca_kv_grad: float32 [896, 1792], P(('dp', 'seq'))
- cca_out_grad: float32 [896, 896], P(('dp', 'seq'))
- enc_gain_grad: float32 [2, 896], P(None, ('dp', 'seq'))
- enc_in_grad: float32 [2, 896, 3584], P(None, ('dp', 'seq'))
- enc_down_grad: float32 [2, 3584, 896], P(None, None, ('dp', 'seq'))
- enc_final_grad: float32 [896], P(('dp', 'seq'))
All inputs are finite; a program needn't handle non-finite values.
Results may differ from a plain program's by a relative error of at most 0.023.
Values may be sent and summed in bfloat16 or wider, within the bound.
A program may use at most 768 MiB of HBM per device.

v0:
```python
import jax
import jax.numpy as jnp
from jax import lax
from jax.sharding import PartitionSpec as P

D = 896
HEADS = 14
HEAD = 64
SPAN = 64
NEIGH = 2
RET = 128
ENC_LAYERS = 2
DEC_LAYERS = 2


EPSILON = 1e-06
SCORE_SCALE = 0.125
MASKED_SCORE = -1000000000.0


def shifted(x, axis, by):
    count = lax.axis_size(axis)
    pairs = [(i, i + by) for i in range(count) if 0 <= i + by < count]
    return lax.ppermute(x, axis, pairs)


def normed(values, norm_gain):
    return values * lax.rsqrt(jnp.mean(values * values, -1, keepdims=True) + EPSILON) * norm_gain


def gelu_exact(values):
    return jax.nn.gelu(values, approximate=False)


def project(values, weight):
    return jnp.dot(values, weight, preferred_element_type=jnp.float32)


def back_project(upstream, weight):
    return lax.dot_general(
        upstream,
        weight,
        (((upstream.ndim - 1,), (1,)), ((), ())),
        preferred_element_type=jnp.float32,
    )


def slab_term(left, right):
    flat_left = left.reshape(-1, left.shape[-1])
    flat_right = right.reshape(-1, right.shape[-1])
    return lax.dot_general(
        flat_left, flat_right, (((0,), (0,)), ((), ())), preferred_element_type=jnp.float32
    )


def norm_back(stream, norm_gain, upstream):
    _, pullback = jax.vjp(normed, stream, norm_gain)
    return pullback(upstream)


def split_heads(values):
    return values.reshape(values.shape[:-1] + (HEADS, HEAD))


def softmax_parts(scores):
    row_peak = jnp.max(scores, -1, keepdims=True)
    powers = jnp.exp(scores - row_peak)
    row_total = jnp.sum(powers, -1, keepdims=True)
    return (powers / row_total, (row_peak + jnp.log(row_total))[..., 0])


def feed_forward(stream, norm_gain, weight_in, weight_down):
    inputs = normed(stream, norm_gain).astype(jnp.bfloat16)
    hidden_pre = project(inputs, weight_in)
    hidden = gelu_exact(hidden_pre).astype(jnp.bfloat16)
    return (stream + project(hidden, weight_down), (stream, inputs, hidden_pre, hidden))


def feed_back(stored, norm_gain, weight_in, weight_down, upstream):
    stream, inputs, hidden_pre, hidden = stored
    grad_low = upstream.astype(jnp.bfloat16)
    grad_hidden = back_project(grad_low, weight_down)
    _, gelu_pull = jax.vjp(gelu_exact, hidden_pre)
    grad_pre = gelu_pull(grad_hidden)[0].astype(jnp.bfloat16)
    stream_grad, gain_grad = norm_back(stream, norm_gain, back_project(grad_pre, weight_in))
    return (upstream + stream_grad, gain_grad, ((inputs, grad_pre), (grad_low, hidden)))


def score_table(queries, keys_all, offset):
    raw_scores = (
        jnp.einsum("bqhd,bkhd->bhqk", queries, keys_all, preferred_element_type=jnp.float32)
        * SCORE_SCALE
    )
    key_place = jnp.arange(keys_all.shape[1])
    query_place = offset + jnp.arange(queries.shape[1])
    return jnp.where(key_place[None, :] <= query_place[:, None], raw_scores, MASKED_SCORE)


def self_forward(stream, norm_gain, weight_qkv, weight_out, offset):
    inputs = normed(stream, norm_gain).astype(jnp.bfloat16)
    joined = project(inputs, weight_qkv).astype(jnp.bfloat16)
    keys_vals = lax.all_gather(joined[..., D:], "seq", axis=1, tiled=True)
    queries = split_heads(joined[..., :D])
    scores = score_table(queries, split_heads(keys_vals[..., :D]), offset)
    attn_probs, log_total = softmax_parts(scores)
    attn_mixed = jnp.einsum(
        "bhqk,bkhd->bqhd",
        attn_probs.astype(jnp.bfloat16),
        split_heads(keys_vals[..., D:]),
        preferred_element_type=jnp.float32,
    )
    attn_mixed = attn_mixed.astype(jnp.bfloat16).reshape(stream.shape)
    return (
        stream + project(attn_mixed, weight_out),
        (stream, inputs, joined, keys_vals, log_total, attn_mixed),
    )


def self_back(stored, norm_gain, weight_qkv, weight_out, offset, upstream):
    stream, inputs, joined, keys_vals, log_total, attn_mixed = stored
    grad_low = upstream.astype(jnp.bfloat16)
    grad_mixed = split_heads(back_project(grad_low, weight_out).astype(jnp.bfloat16))
    queries = split_heads(joined[..., :D])
    keys_all = split_heads(keys_vals[..., :D])
    vals_all = split_heads(keys_vals[..., D:])
    scores = score_table(queries, keys_all, offset)
    attn_probs = jnp.exp(scores - log_total[..., None])
    grad_probs = jnp.einsum(
        "bqhd,bkhd->bhqk", grad_mixed, vals_all, preferred_element_type=jnp.float32
    )
    row_delta = jnp.sum(attn_probs * grad_probs, -1)
    grad_scores = (attn_probs * (grad_probs - row_delta[..., None])).astype(jnp.bfloat16)
    grad_queries = (
        jnp.einsum("bhqk,bkhd->bqhd", grad_scores, keys_all, preferred_element_type=jnp.float32)
        * SCORE_SCALE
    )
    seqs_here = queries.shape[0]
    grad_vals = jnp.einsum(
        "bhqk,bqhd->bkhd",
        attn_probs.astype(jnp.bfloat16),
        grad_mixed,
        preferred_element_type=jnp.float32,
    )
    grad_keys = (
        jnp.einsum("bhqk,bqhd->bkhd", grad_scores, queries, preferred_element_type=jnp.float32)
        * SCORE_SCALE
    )
    length = grad_keys.shape[1]
    grad_pairs = jnp.concatenate(
        [grad_keys.reshape(seqs_here, length, D), grad_vals.reshape(seqs_here, length, D)], -1
    )
    own_pairs = lax.psum_scatter(
        grad_pairs.astype(jnp.bfloat16), "seq", scatter_dimension=1, tiled=True
    ).astype(jnp.float32)
    grad_joined = jnp.concatenate([grad_queries.reshape(stream.shape), own_pairs], -1).astype(
        jnp.bfloat16
    )
    stream_grad, gain_grad = norm_back(stream, norm_gain, back_project(grad_joined, weight_qkv))
    return (upstream + stream_grad, gain_grad, ((inputs, grad_joined), (attn_mixed, grad_low)))


def cross_scores(queries, keys_vals, prior_flag):
    raw_scores = (
        jnp.einsum(
            "bcqhd,bckhd->bchqk",
            queries,
            split_heads(keys_vals[..., :D]),
            preferred_element_type=jnp.float32,
        )
        * SCORE_SCALE
    )
    allowed = jnp.repeat(prior_flag, RET, axis=2) > 0.5
    return jnp.where(allowed[:, :, None, None, :], raw_scores, MASKED_SCORE)


def row_gate(prior_flag):
    return jnp.repeat(jnp.max(prior_flag, -1).astype(jnp.float32), SPAN, axis=1)[..., None]


def cross_forward(stream, encoded, keep_flag, norm_gain, weight_q, weight_kv, weight_out):
    seqs_here = stream.shape[0]
    spans_here = encoded.shape[1]
    last_enc, last_flag = shifted((encoded[:, -1], keep_flag[:, -1]), "seq", 1)
    prior_enc = jnp.concatenate([last_enc[:, None], encoded[:, :-1]], 1)
    prior_flag = jnp.concatenate([last_flag[:, None], keep_flag[:, :-1]], 1)
    inputs = normed(stream, norm_gain).astype(jnp.bfloat16)
    queries = (
        project(inputs, weight_q)
        .astype(jnp.bfloat16)
        .reshape(seqs_here, spans_here, SPAN, HEADS, HEAD)
    )
    keys_vals = (
        project(prior_enc, weight_kv)
        .astype(jnp.bfloat16)
        .reshape(seqs_here, spans_here, NEIGH * RET, 2 * D)
    )
    scores = cross_scores(queries, keys_vals, prior_flag)
    attn_probs, log_total = softmax_parts(scores)
    attn_mixed = jnp.einsum(
        "bchqk,bckhd->bcqhd",
        attn_probs.astype(jnp.bfloat16),
        split_heads(keys_vals[..., D:]),
        preferred_element_type=jnp.float32,
    )
    attn_mixed = attn_mixed.astype(jnp.bfloat16).reshape(stream.shape)
    branch = row_gate(prior_flag) * project(attn_mixed, weight_out)
    return (
        stream + branch,
        (stream, inputs, prior_enc, prior_flag, queries, keys_vals, log_total, attn_mixed),
    )


def cross_back(stored, norm_gain, weight_q, weight_kv, weight_out, upstream):
    stream, inputs, prior_enc, prior_flag, queries, keys_vals, log_total, attn_mixed = stored
    grad_low = (upstream * row_gate(prior_flag)).astype(jnp.bfloat16)
    grad_mixed = back_project(grad_low, weight_out).astype(jnp.bfloat16).reshape(queries.shape)
    scores = cross_scores(queries, keys_vals, prior_flag)
    attn_probs = jnp.exp(scores - log_total[..., None])
    keys_part = split_heads(keys_vals[..., :D])
    vals_part = split_heads(keys_vals[..., D:])
    grad_vals = jnp.einsum(
        "bchqk,bcqhd->bckhd",
        attn_probs.astype(jnp.bfloat16),
        grad_mixed,
        preferred_element_type=jnp.float32,
    )
    grad_probs = jnp.einsum(
        "bcqhd,bckhd->bchqk", grad_mixed, vals_part, preferred_element_type=jnp.float32
    )
    grad_scores = attn_probs * (grad_probs - jnp.sum(attn_probs * grad_probs, -1, keepdims=True))
    grad_scores = grad_scores.astype(jnp.bfloat16)
    grad_queries = (
        jnp.einsum("bchqk,bckhd->bcqhd", grad_scores, keys_part, preferred_element_type=jnp.float32)
        * SCORE_SCALE
    )
    grad_keys = (
        jnp.einsum("bchqk,bcqhd->bckhd", grad_scores, queries, preferred_element_type=jnp.float32)
        * SCORE_SCALE
    )
    pair_shape = keys_vals.shape[:-1] + (D,)
    grad_pairs = jnp.concatenate([grad_keys.reshape(pair_shape), grad_vals.reshape(pair_shape)], -1)
    grad_pairs = grad_pairs.astype(jnp.bfloat16)
    grad_prior = back_project(grad_pairs, weight_kv).reshape(prior_enc.shape)
    query_low = grad_queries.reshape(stream.shape).astype(jnp.bfloat16)
    stream_grad, gain_grad = norm_back(stream, norm_gain, back_project(query_low, weight_q))
    from_next = shifted(grad_prior[:, 0].astype(jnp.bfloat16), "seq", -1).astype(jnp.float32)
    encoded_grad = jnp.concatenate([grad_prior[:, 1:], from_next[:, None]], 1)
    pairs = ((inputs, query_low), (prior_enc, grad_pairs), (attn_mixed, grad_low))
    return (upstream + stream_grad, gain_grad, pairs, encoded_grad)


def encode(retrieved, enc_gain, enc_in, enc_down, enc_final):
    stream = retrieved.astype(jnp.float32)
    stored = []
    for layer_idx in range(ENC_LAYERS):
        stream, layer_store = feed_forward(
            stream, enc_gain[layer_idx], enc_in[layer_idx], enc_down[layer_idx]
        )
        stored.append(layer_store)
    return (normed(stream, enc_final).astype(jnp.bfloat16), (stream, stored))


def encode_back(retrieved, enc_weights, encoded_grad):
    enc_gain, enc_in, enc_down, enc_final = enc_weights
    _, (stream, stored) = encode(retrieved, enc_gain, enc_in, enc_down, enc_final)
    upstream, final_grad = norm_back(stream, enc_final, encoded_grad)
    gain_list = [None] * ENC_LAYERS
    pair_list = [None] * ENC_LAYERS
    for layer_idx in reversed(range(ENC_LAYERS)):
        upstream, gain_list[layer_idx], pair_list[layer_idx] = feed_back(
            stored[layer_idx], enc_gain[layer_idx], enc_in[layer_idx], enc_down[layer_idx], upstream
        )
    return (gain_list, pair_list, final_grad)


def on_device(
    tokens,
    retrieved,
    span_doc,
    neigh_doc,
    cotangent,
    dec_gain,
    dec_qkv,
    dec_out,
    dec_in,
    dec_down,
    cca_gain,
    cca_q,
    cca_kv,
    cca_out,
    enc_gain,
    enc_in,
    enc_down,
    enc_final,
):
    offset = lax.axis_index("seq") * tokens.shape[1]
    enc_weights = (
        lax.all_gather(enc_gain, ("dp", "seq"), axis=1, tiled=True),
        lax.all_gather(enc_in, ("dp", "seq"), axis=1, tiled=True),
        lax.all_gather(enc_down, ("dp", "seq"), axis=1, tiled=True),
        lax.all_gather(enc_final, ("dp", "seq"), axis=0, tiled=True),
    )
    encoded, _ = encode(retrieved, enc_weights[0], enc_weights[1], enc_weights[2], enc_weights[3])
    keep_flag = (neigh_doc != span_doc[..., None]).astype(jnp.bfloat16)
    dec_weights = (
        lax.all_gather(dec_gain, ("dp", "seq"), axis=2, tiled=True),
        lax.all_gather(dec_qkv, ("dp", "seq"), axis=1, tiled=True),
        lax.all_gather(dec_out, ("dp", "seq"), axis=1, tiled=True),
        lax.all_gather(dec_in, ("dp", "seq"), axis=1, tiled=True),
        lax.all_gather(dec_down, ("dp", "seq"), axis=1, tiled=True),
        lax.all_gather(cca_gain, ("dp", "seq"), axis=0, tiled=True),
        lax.all_gather(cca_q, ("dp", "seq"), axis=0, tiled=True),
        lax.all_gather(cca_kv, ("dp", "seq"), axis=0, tiled=True),
        lax.all_gather(cca_out, ("dp", "seq"), axis=0, tiled=True),
    )
    norm_gains, qkv_all, out_all, in_all, down_all, cross_gain, cross_q, cross_kv, cross_out = (
        dec_weights
    )
    stream = tokens.astype(jnp.float32)
    attn_stores, ffn_stores = ([], [])
    stream, attn_store = self_forward(stream, norm_gains[0, 0], qkv_all[0], out_all[0], offset)
    attn_stores.append(attn_store)
    stream, cross_store = cross_forward(
        stream, encoded, keep_flag, cross_gain, cross_q, cross_kv, cross_out
    )
    stream, ffn_store = feed_forward(stream, norm_gains[0, 1], in_all[0], down_all[0])
    ffn_stores.append(ffn_store)
    layer_idx = 1
    stream, attn_store = self_forward(
        stream, norm_gains[layer_idx, 0], qkv_all[layer_idx], out_all[layer_idx], offset
    )
    attn_stores.append(attn_store)
    stream, ffn_store = feed_forward(
        stream, norm_gains[layer_idx, 1], in_all[layer_idx], down_all[layer_idx]
    )
    ffn_stores.append(ffn_store)
    result = stream.astype(jnp.bfloat16)
    upstream = cotangent.astype(jnp.float32)
    attn_gain_g = [None] * DEC_LAYERS
    ffn_gain_g = [None] * DEC_LAYERS
    attn_pairs = [None] * DEC_LAYERS
    ffn_pairs = [None] * DEC_LAYERS
    for layer_idx in reversed(range(1, DEC_LAYERS)):
        upstream, ffn_gain_g[layer_idx], ffn_pairs[layer_idx] = feed_back(
            ffn_stores[layer_idx],
            norm_gains[layer_idx, 1],
            in_all[layer_idx],
            down_all[layer_idx],
            upstream,
        )
        upstream, attn_gain_g[layer_idx], attn_pairs[layer_idx] = self_back(
            attn_stores[layer_idx],
            norm_gains[layer_idx, 0],
            qkv_all[layer_idx],
            out_all[layer_idx],
            offset,
            upstream,
        )
    upstream, ffn_gain_g[0], ffn_pairs[0] = feed_back(
        ffn_stores[0], norm_gains[0, 1], in_all[0], down_all[0], upstream
    )
    upstream, cross_gain_g, cross_pairs, encoded_grad = cross_back(
        cross_store, cross_gain, cross_q, cross_kv, cross_out, upstream
    )
    upstream, attn_gain_g[0], attn_pairs[0] = self_back(
        attn_stores[0], norm_gains[0, 0], qkv_all[0], out_all[0], offset, upstream
    )
    enc_gain_g, enc_pairs, final_gain_g = encode_back(retrieved, enc_weights, encoded_grad)
    pair_list = []
    for layer_idx in range(DEC_LAYERS):
        pair_list = pair_list + list(attn_pairs[layer_idx]) + list(ffn_pairs[layer_idx])
    pair_list = pair_list + list(cross_pairs)
    for layer_idx in range(ENC_LAYERS):
        pair_list = pair_list + list(enc_pairs[layer_idx])
    gain_list = []
    for layer_idx in range(DEC_LAYERS):
        gain_list = gain_list + [attn_gain_g[layer_idx], ffn_gain_g[layer_idx]]
    gain_list = gain_list + [cross_gain_g] + list(enc_gain_g) + [final_gain_g]

    def term():
        blocks = [slab_term(left, right) for left, right in pair_list]
        blocks = blocks + [vector[:, None] for vector in gain_list]
        return jnp.concatenate(blocks, 1)

    owned = lax.psum_scatter(term(), ("dp", "seq"), scatter_dimension=0, tiled=True)
    pieces = []
    cursor = 0
    for left, right in pair_list:
        width = right.shape[-1]
        pieces.append(owned[:, cursor : cursor + width])
        cursor = cursor + width
    gain_cols = owned[:, cursor:]
    dec_qkv_g = jnp.stack([pieces[4 * idx] for idx in range(DEC_LAYERS)])
    dec_out_g = jnp.stack([pieces[4 * idx + 1] for idx in range(DEC_LAYERS)])
    dec_in_g = jnp.stack([pieces[4 * idx + 2] for idx in range(DEC_LAYERS)])
    dec_down_g = jnp.stack([pieces[4 * idx + 3].T for idx in range(DEC_LAYERS)])
    base = 4 * DEC_LAYERS
    cross_q_g = pieces[base]
    cross_kv_g = pieces[base + 1]
    cross_out_g = pieces[base + 2]
    base = base + 3
    enc_in_g = jnp.stack([pieces[base + 2 * idx] for idx in range(ENC_LAYERS)])
    enc_down_g = jnp.stack([pieces[base + 2 * idx + 1].T for idx in range(ENC_LAYERS)])
    dec_gain_g = jnp.stack(
        [jnp.stack([gain_cols[:, 2 * idx], gain_cols[:, 2 * idx + 1]]) for idx in range(DEC_LAYERS)]
    )
    cross_gain_out = gain_cols[:, 2 * DEC_LAYERS]
    enc_gain_out = jnp.stack([gain_cols[:, 2 * DEC_LAYERS + 1 + idx] for idx in range(ENC_LAYERS)])
    final_out = gain_cols[:, 2 * DEC_LAYERS + 1 + ENC_LAYERS]
    return (
        result,
        upstream,
        dec_gain_g,
        dec_qkv_g,
        dec_out_g,
        dec_in_g,
        dec_down_g,
        cross_gain_out,
        cross_q_g,
        cross_kv_g,
        cross_out_g,
        enc_gain_out,
        enc_in_g,
        enc_down_g,
        final_out,
    )


def solution(mesh):
    return jax.shard_map(
        on_device,
        mesh=mesh,
        in_specs=(
            P("dp", "seq", None),
            P("dp", "seq", None, None, None),
            P("dp", "seq"),
            P("dp", "seq", None),
            P("dp", "seq", None),
            P(None, None, ("dp", "seq")),
            P(None, ("dp", "seq"), None),
            P(None, ("dp", "seq"), None),
            P(None, ("dp", "seq"), None),
            P(None, ("dp", "seq"), None),
            P(("dp", "seq")),
            P(("dp", "seq"), None),
            P(("dp", "seq"), None),
            P(("dp", "seq"), None),
            P(None, ("dp", "seq")),
            P(None, ("dp", "seq"), None),
            P(None, ("dp", "seq"), None),
            P(("dp", "seq")),
        ),
        out_specs=(
            P("dp", "seq", None),
            P("dp", "seq", None),
            P(None, None, ("dp", "seq")),
            P(None, ("dp", "seq"), None),
            P(None, ("dp", "seq"), None),
            P(None, ("dp", "seq"), None),
            P(None, None, ("dp", "seq")),
            P(("dp", "seq")),
            P(("dp", "seq"), None),
            P(("dp", "seq"), None),
            P(("dp", "seq"), None),
            P(None, ("dp", "seq")),
            P(None, ("dp", "seq"), None),
            P(None, None, ("dp", "seq")),
            P(("dp", "seq")),
        ),
        check_vma=False,
    )
```

profile of v0, /device:TPU:0, one launch (start us, length us, event | category | flops | bytes accessed | tf_op | source)
XLA Modules:
  0.0 3208.1 jit_solution(11448289618707080892)
XLA Ops:
  12.8 45.1 %all_gather.45 = bf16[2,2,896]{1,0,2:T(2,128)(2,1)S(1)} all-gather(bf16[2,2,28]{1,0,2:T(2,128)(2,1)S(1)} %copy.178), channel_id=1, replica_groups=mesh['dp'=4,'seq'=8] {'dp','seq'}, dimensions={2}, use_global_device_ids=true | all-gather | bytes 7392 | tf_op jit(solution)/shard_map/all_gather | solution.py:306
  58.5 10.5 fusion.133
  69.1 28.5 all-gather.16.cloned.1.call-done
  97.6 19.5 fusion.202
  126.1 40.3 %all-reduce.3 = (bf16[896]{0:T(1024)(128)(2,1)S(1)}, bf16[896]{0:T(1024)(128)(2,1)S(1)}) all-reduce(bf16[896]{0:T(1024)(128)(2,1)S(1)} %dynamic-update-slice, bf16[896]{0:T(1024)(128)(2,1)S(1)} %dynamic-update-slice.1), channel_id=1, replica_groups=mesh['dp'=4,'seq'=8] {'dp','seq'}, use_global_device_ids=true, to_apply=%add | all-reduce | flops 1792 | bytes 7168
  166.4 39.9 %all-gather = bf16[32,28,2]{1,2,0:T(2,128)(2,1)S(1)} all-gather(bf16[1,28,2]{1,2,0:T(2,128)(2,1)S(1)} %bitcast.595), channel_id=1, replica_groups=mesh['dp'=4,'seq'=8] {'dp','seq'}, dimensions={0}, use_global_device_ids=true | all-gather | bytes 3696 | tf_op jit(solution)/shard_map/all_gather | solution.py:298
  216.1 58.4 %all-gather.32.cloned.1.call-done = bf16[32,28,1792]{2,1,0:T(8,128)(2,1)} async-done(((bf16[1,28,1792]{2,1,0:T(8,128)(2,1)}), bf16[32,28,1792]{2,1,0:T(8,128)(2,1)}) %all-gather.32.cloned.1.call-update) | async-done | bytes 3211280 | tf_op jit(solution)/shard_map/all_gather | solution.py:313
  280.0 55.3 %all-gather.20.cloned.1.call-done = bf16[2,896,896]{2,0,1:T(2,128)(2,1)} async-done(((bf16[2,28,896]{2,0,1:T(2,128)(2,1)}), bf16[2,896,896]{2,0,1:T(2,128)(2,1)}) %all-gather.20.cloned.1.call-update) | async-done | bytes 3211280 | tf_op jit(solution)/shard_map/all_gather | solution.py:308
  335.3 9.6 fusion.205
  345.8 88.5 %all-gather.22.cloned.1.call-done = bf16[2,896,3584]{2,0,1:T(2,128)(2,1)} async-done(((bf16[2,28,3584]{2,0,1:T(2,128)(2,1)}), bf16[2,896,3584]{2,0,1:T(2,128)(2,1)}) %all-gather.22.cloned.1.call-update) | async-done | bytes 12845072 | tf_op jit(solution)/shard_map/all_gather | solution.py:299
  434.3 25.6 fusion.201
  459.9 10.7 fusion.74
  473.6 17.7 multiply_convert_fusion.3
  491.4 41.3 %all-gather.24.cloned.1.call-done = bf16[2,3584,896]{2,1,0:T(8,128)(2,1)} async-done(((bf16[2,112,896]{2,1,0:T(8,128)(2,1)}), bf16[2,3584,896]{2,1,0:T(8,128)(2,1)}) %all-gather.24.cloned.1.call-update) | async-done | bytes 12845072 | tf_op jit(solution)/shard_map/all_gather | solution.py:300
  532.7 9.1 multiply_reduce_fusion.6
  541.9 10.8 fusion.75
  552.7 17.6 multiply_convert_fusion.2
  570.3 9.5 multiply_reduce_fusion.5
  584.3 47.9 %all-gather.26.cloned.1.call-done = bf16[2,896,3584]{2,0,1:T(2,128)(2,1)} async-done(((bf16[2,28,3584]{2,0,1:T(2,128)(2,1)}), bf16[2,896,3584]{2,0,1:T(2,128)(2,1)}) %all-gather.26.cloned.1.call-update) | async-done | bytes 12845072 | tf_op jit(solution)/shard_map/all_gather | solution.py:309
  632.1 25.7 fusion.200
  657.8 9.6 all-gather.18.cloned.1.call-done
  700.1 6.0 fusion.40
  706.1 61.3 %all-gather.28.cloned.1.call-done = bf16[2,3584,896]{2,1,0:T(8,128)(2,1)} async-done(((bf16[2,112,896]{2,1,0:T(8,128)(2,1)}), bf16[2,3584,896]{2,1,0:T(8,128)(2,1)}) %all-gather.28.cloned.1.call-update) | async-done | bytes 12845072 | tf_op jit(solution)/shard_map/all_gather | solution.py:310
  767.4 7.0 multiply_reduce_fusion.8
  780.4 32.6 %all-gather.30.cloned.1.call-done = bf16[1,1024,1792]{2,1,0:T(8,128)(2,1)} async-done(((bf16[1,128,1792]{2,1,0:T(8,128)(2,1)}), bf16[1,1024,1792]{2,1,0:T(8,128)(2,1)}) %all-gather.30.cloned.1.call-update) | async-done | bytes 3670032 | tf_op jit(solution)/shard_map/all_gather | solution.py:102
  836.9 7.8 add_convert_fusion.3
  863.2 16.3 copy.251
  892.6 41.2 %reduce-scatter.7.cloned.1.call-done = bf16[128,1792]{1,0:T(8,128)(2,1)} async-done(((bf16[1024,1792]{1,0:T(8,128)(2,1)}), bf16[128,1792]{1,0:T(8,128)(2,1)}) %reduce-scatter.7.cloned.1.call-update) | async-done | bytes 458768
  936.6 5.5 fusion.139
  943.6 7.3 add_convert_fusion.2
  971.9 6.1 fusion.79
  1015.3 16.3 copy.253
  1031.6 5.5 copy.319
  1043.8 11.9 add_convert_fusion.1
  1055.8 10.7 fusion.60
  1068.3 11.5 add_convert_fusion
  1093.2 6.2 fusion.124
  1099.3 6.4 convolution_dynamic-update-slice_fusion.4
  1109.0 6.5 convolution_dynamic-update-slice_fusion.2
  1115.6 8.0 convolution_dynamic-update-slice_fusion.1
  1131.1 6.6 convolution_dynamic-update-slice_fusion
  1137.7 7.7 bitcast_dynamic-update-slice_fusion.4
  1154.8 6.7 bitcast_dynamic-update-slice_fusion.3
  1161.5 6.7 bitcast_dynamic-update-slice_fusion.2
  1168.2 6.7 bitcast_dynamic-update-slice_fusion.1
  1174.9 6.9 bitcast_dynamic-update-slice_fusion
  1202.2 7.8 fusion.110
  1211.0 1970.0 %all-reduce.6.cloned.1.call-done = f32[896,39432]{1,0:T(8,128)} async-done(((f32[896,39432]{1,0:T(8,128)}), f32[896,39432]{1,0:T(8,128)}) %all-reduce.6.cloned.1.call-update) | async-done | bytes 141324304
  (544 shorter events, 277.7 us)
Async XLA Ops:
  7.2 50.7 %copy-start.55 = (bf16[1,128,896]{2,1,0:T(8,128)(2,1)S(1)}, bf16[1,128,896]{2,1,0:T(8,128)(2,1)}, u32[]{:S(2)}) copy-start(bf16[1,128,896]{2,1,0:T(8,128)(2,1)} %param.18) | copy-start | bytes 688132
  7.2 90.4 %all-gather.16.cloned.1.call-start = ((), (), s32[]{:S(2)}) async-start(), calls=%async_computation.2 | async-start | bytes 9934848 | tf_op jit(solution)/shard_map/all_gather | solution.py:307
  7.9 199.7 %all-gather.34.cloned.1.call-start = ((), (), s32[]{:S(2)}) async-start(), calls=%async_computation.11 | async-start | bytes 1892352 | tf_op jit(solution)/shard_map/all_gather | solution.py:312
  8.7 203.8 %all-gather.36.cloned.1.call-start = ((), (), s32[]{:S(2)}) async-start(), calls=%async_computation.12 | async-start | bytes 1892352 | tf_op jit(solution)/shard_map/all_gather | solution.py:314
  9.4 265.1 %all-gather.32.cloned.1.call-start = ((), (), s32[]{:S(2)}) async-start(), calls=%async_computation.10 | async-start | bytes 3784704 | tf_op jit(solution)/shard_map/all_gather | solution.py:313
  10.0 325.3 %all-gather.20.cloned.1.call-start = ((), (), s32[]{:S(2)}) async-start(), calls=%async_computation.4 | async-start | bytes 3311616 | tf_op jit(solution)/shard_map/all_gather | solution.py:308
  10.6 423.7 %all-gather.22.cloned.1.call-start = ((), (), s32[]{:S(2)}) async-start(), calls=%async_computation.5 | async-start | bytes 13246464 | tf_op jit(solution)/shard_map/all_gather | solution.py:299
  11.2 521.5 %all-gather.24.cloned.1.call-start = ((), (), s32[]{:S(2)}) async-start(), calls=%async_computation.6 | async-start | bytes 13246464 | tf_op jit(solution)/shard_map/all_gather | solution.py:300
  11.9 620.2 %all-gather.26.cloned.1.call-start = ((), (), s32[]{:S(2)}) async-start(), calls=%async_computation.7 | async-start | bytes 13246464 | tf_op jit(solution)/shard_map/all_gather | solution.py:309
  12.7 654.7 %all-gather.18.cloned.1.call-start = ((), (), s32[]{:S(2)}) async-start(), calls=%async_computation.3 | async-start | bytes 4128768 | tf_op jit(solution)/shard_map/all_gather | solution.py:102
  58.5 58.5 %copy-start.127 = (f32[128]{0:T(128)}, f32[128]{0:T(128)S(1)}, u32[]{:S(2)}) copy-start(f32[128]{0:T(128)S(1)} %fusion.175) | copy-start | bytes 1540
  69.1 48.0 %copy-start.113 = (f32[896]{0:T(1024)}, f32[896]{0:T(1024)S(1)}, u32[]{:S(2)}) copy-start(f32[896]{0:T(1024)S(1)} %get-tuple-element.104) | copy-start | bytes 10756
  121.7 44.6 %copy-start.135 = (bf16[2,28]{1,0:T(2,128)(2,1)S(1)}, bf16[2,28]{1,0:T(2,128)(2,1)}, u32[]{:S(2)}) copy-start(bf16[2,28]{1,0:T(2,128)(2,1)} %param.32) | copy-start | bytes 340
  122.6 644.8 %all-gather.28.cloned.1.call-start = ((), (), s32[]{:S(2)}) async-start(), calls=%async_computation.8 | async-start | bytes 13246464 | tf_op jit(solution)/shard_map/all_gather | solution.py:310
  122.7 84.5 %collective-permute-start = (bf16[1,2]{1,0:T(2,128)(2,1)S(1)}, bf16[1,2]{1,0:T(2,128)(2,1)S(1)}, u32[]{:S(2)}, u32[]{:S(2)}) collective-permute-start(bf16[1,2]{1,0:T(2,128)(2,1)S(1)} %get-tuple-element.143), channel_id=1, source_target_pairs={{0,1},{1,2},{2,3},{3,4},{4,5},{5,6},{6,7},{8,9},{9,10},{10,11},{11... | collective-permute-start | bytes 20 | tf_op jit(solution)/shard_map/ppermute | solution.py:24
  124.9 688.1 %all-gather.30.cloned.1.call-start = ((), (), s32[]{:S(2)}) async-start(), calls=%async_computation.9 | async-start | bytes 4128768 | tf_op jit(solution)/shard_map/all_gather | solution.py:102
  125.6 334.3 %copy-start.117 = (f32[2,2,128]{2,1,0:T(2,128)}, f32[2,2,128]{2,1,0:T(2,128)S(1)}, u32[]{:S(2)}) copy-start(f32[2,2,128]{2,1,0:T(2,128)S(1)} %add_rsqrt_fusion) | copy-start | bytes 6148
  166.4 413.4 %copy-start.119 = (f32[896]{0:T(1024)}, f32[896]{0:T(1024)S(1)}, u32[]{:S(2)}) copy-start(f32[896]{0:T(1024)S(1)} %convert_element_type.530) | copy-start | bytes 10756
  206.4 253.5 %copy-start.107 = (f32[896]{0:T(1024)}, f32[896]{0:T(1024)S(1)}, u32[]{:S(2)}) copy-start(f32[896]{0:T(1024)S(1)} %get-tuple-element.106) | copy-start | bytes 10756
  206.4 335.4 %copy-start.105 = (f32[896]{0:T(1024)}, f32[896]{0:T(1024)S(1)}, u32[]{:S(2)}) copy-start(f32[896]{0:T(1024)S(1)} %get-tuple-element.105) | copy-start | bytes 10756
  210.1 477.0 %copy-start.14 = (bf16[896,896]{1,0:T(8,128)(2,1)}, bf16[896,896]{1,0:T(8,128)(2,1)S(1)}, u32[]{:S(2)}) copy-start(bf16[896,896]{1,0:T(8,128)(2,1)S(1)} %reshape.1531) | copy-start | bytes 4816900
  541.8 28.5 copy-start.31
  552.7 17.6 copy-start.35
  581.3 107.2 %collective-permute-start.1 = (bf16[1,2,128,896]{3,2,1,0:T(8,128)(2,1)}, bf16[1,2,128,896]{3,2,1,0:T(8,128)(2,1)}, u32[]{:S(2)}, u32[]{:S(2)}) collective-permute-start(bf16[1,2,128,896]{3,2,1,0:T(8,128)(2,1)} %get-tuple-element.141), channel_id=1, source_target_pairs={{0,1},{1,2},{2,3},{3,4},{4,5},{5,6},{6,7},{8,9},{9,10},{10,11},{11... | collective-permute-start | bytes 1376264 | tf_op jit(solution)/shard_map/ppermute | solution.py:24
  687.1 12.3 copy-start.6
  700.1 67.3 %copy-start.44 = (f32[1,128,896]{2,1,0:T(8,128)}, f32[1,128,896]{2,1,0:T(8,128)S(1)}, u32[]{:S(2)}) copy-start(f32[1,128,896]{2,1,0:T(8,128)S(1)} %get-tuple-element.158) | copy-start | bytes 1376260
  706.1 68.2 %copy-start.142 = (f32[128,3584]{1,0:T(8,128)}, f32[128,3584]{1,0:T(8,128)S(1)}, u32[]{:S(2)}) copy-start(f32[128,3584]{1,0:T(8,128)S(1)} %fusion.40) | copy-start | bytes 5505028
  774.4 57.9 %copy-start.50 = (f32[1,128,896]{2,1,0:T(8,128)}, f32[1,128,896]{2,1,0:T(8,128)S(1)}, u32[]{:S(2)}) copy-start(f32[1,128,896]{2,1,0:T(8,128)S(1)} %get-tuple-element.160) | copy-start | bytes 1376260
  780.1 153.7 %reduce-scatter.7.cloned.1.call-start = ((), (), s32[]{:S(2)}) async-start(), calls=%async_computation.13 | async-start | bytes 4128768
  780.4 44.7 %copy-start.75 = (bf16[1,128,896]{1,2,0:T(8,128)(2,1)}, bf16[1,128,896]{1,2,0:T(8,128)(2,1)S(1)}, u32[]{:S(2)}) copy-start(bf16[1,128,896]{1,2,0:T(8,128)(2,1)S(1)} %copy.195) | copy-start | bytes 688132
  833.4 13.6 copy-start.47
  833.4 13.6 copy-start.129
  884.9 202.6 %reduce-scatter.9.cloned.1.call-start = ((), (), s32[]{:S(2)}) async-start(), calls=%async_computation.14 | async-start | bytes 4128768
  892.6 49.5 %copy-start.97 = (bf16[14,64,128]{2,1,0:T(8,128)(2,1)}, bf16[14,64,128]{2,1,0:T(8,128)(2,1)S(1)}, u32[]{:S(2)}) copy-start(bf16[14,64,128]{2,1,0:T(8,128)(2,1)S(1)} %fusion.108) | copy-start | bytes 688132
  892.6 44.0 %copy-start.51 = (f32[1,128,896]{2,1,0:T(8,128)S(1)}, f32[1,128,896]{2,1,0:T(8,128)}, u32[]{:S(2)}) copy-start(f32[1,128,896]{2,1,0:T(8,128)} %copy-done.50) | copy-start | bytes 1376260
  936.6 14.3 slice-start.10
  963.0 15.0 slice-start
  997.1 44.9 %collective-permute-start.2 = (bf16[1,2,128,896]{3,2,1,0:T(8,128)(2,1)}, bf16[1,2,128,896]{3,2,1,0:T(8,128)(2,1)}, u32[]{:S(2)}, u32[]{:S(2)}) collective-permute-start(bf16[1,2,128,896]{3,2,1,0:T(8,128)(2,1)} %fusion.132), channel_id=1, source_target_pairs={{1,0},{2,1},{3,2},{4,3},{5,4},{6,5},{7,6},{9,8},{10,9},{11,10},{12... | collective-permute-start | bytes 1376264 | tf_op jit(solution)/shard_map/ppermute | solution.py:24
  1037.1 2143.8 %all-reduce.6.cloned.1.call-start = ((), (), s32[]{:S(2)}) async-start(), calls=%async_computation.15 | async-start | bytes 283508736
  1043.1 23.4 copy-start.25
  1043.8 12.0 copy-start.32
  1043.8 12.0 copy-start.106
  1043.8 12.0 copy-start.112
  1066.6 13.2 slice-start.6
  1068.3 11.5 slice-start.8
  1068.3 11.5 slice-start.9
  1068.3 11.5 copy-start.63
  1068.3 11.5 copy-start.118
  (132 other events, 627.0 us)
Sparse Core Ops, SparseCore 0:
  11.0 86.5 all-gather.15
  100.4 54.5 all-gather.33
  157.8 54.6 all-gather.35
  215.2 59.2 all-gather.31
  277.3 57.9 all-gather.19
  338.0 96.2 all-gather.21
  437.1 95.4 all-gather.23
  535.5 96.5 all-gather.25
  634.6 32.7 all-gather.17
  670.1 97.2 all-gather.27
  780.2 32.7 all-gather.29
  885.0 48.7 reduce-scatter.6
  1037.2 50.2 reduce-scatter.8
  1200.7 1980.2 all-reduce.5
where the time goes:
time: 3220 us; the launch traced here: 3210 us
  waiting for transfers between devices  2440 us (76%)
  matrix products  277 us (9%)
  local copies, waits for them, and re-layouts  266 us (8%)
  blocking collectives  125 us (4%)
  other arithmetic  72.6 us (2%)
    unnamed x17, waiting for transfers between devices  2020 us
    unnamed x360, local copies, waits for them, and re-layouts  117 us
    all_gather x1, waiting for transfers between devices, on_device(): lax.all_gather(enc_in, ('dp', 'seq'), axis=1, tiled=True)  88.5 us
    dot_general x15, matrix products, back_project(): lax.dot_general(upstream, weight, (((upstream.ndim - 1,), (1,)), ((), ())...  81.6 us
    dot_general x15, matrix products, slab_term(): lax.dot_general(flat_left, flat_right, (((0,), (0,)), ((), ())), preferre...  81.2 us
    dot_general x15, matrix products, project(): return jnp.dot(values, weight, preferred_element_type=jnp.float32)  74.5 us
  transfers between devices with their start and end apart: 17, of which 13 were waited for; matrix products, arithmetic and copies ran while one was open for 10% of the time, Pallas kernels for 0%

commit v1 on v0

--- a/solution.py
+++ b/solution.py
@@ -1,9 +1,308 @@
+import functools
 import jax
 import jax.numpy as jnp
 from jax import lax
+from jax.experimental import pallas as pl
+from jax.experimental.pallas import tpu as pltpu
 from jax.sharding import PartitionSpec as P
 
 D = 896
+FF = 3584
+BF = jnp.bfloat16
+MESH_ID = pl.DeviceIdType.MESH
+ANY = pl.BlockSpec(memory_space=pl.ANY)
+
+
+def grid_sizes():
+    return (lax.axis_size("dp"), lax.axis_size("seq") // 4, 2, 2)
+
+
+def grid_place():
+    seq = lax.axis_index("seq")
+    return (lax.axis_index("dp"), seq // 4, (seq // 2) % 2, seq % 2)
+
+
+def device_at(place):
+    z, y, x, core = place
+    return (z, (y * 2 + x) * 2 + core)
+
+
+def moved(place, sizes, axis, by):
+    size = sizes[axis]
+    there = lax.rem(place[axis] + (by % size), size)
+    return place[:axis] + (there,) + place[axis + 1 :]
+
+
+def greet(place, sizes):
+    barrier = pltpu.get_barrier_semaphore()
+    for axis in range(4):
+        size, here = sizes[axis], place[axis]
+        for by in (1, -1):
+            there = here + by
+
+            @pl.when(inside(there, size))
+            def _():
+                other = place[:axis] + (jnp.clip(there, 0, size - 1),) + place[axis + 1 :]
+                pl.semaphore_signal(barrier, inc=1, device_id=device_at(other), device_id_type=MESH_ID)
+
+    count = 0
+    for axis in range(4):
+        for by in (1, -1):
+            count = count + inside(place[axis] + by, sizes[axis]).astype(jnp.int32)
+    pl.semaphore_wait(barrier, count)
+
+
+class Hop:
+    def __init__(self, copy, sends, receives):
+        self.copy, self.sends, self.receives = copy, sends, receives
+
+    def start(self):
+        pl.when(self.sends)(self.copy[0].start)
+
+    def wait(self):
+        pl.when(self.sends)(self.copy[0].wait_send)
+        pl.when(self.receives)(self.copy[1].wait_recv)
+
+
+def inside(place, size):
+    return jnp.logical_and(place >= 0, place < size)
+
+
+ROUTES = ((2, 0, 1), (1, 0, 2), (0, 2, 1), (1, 0, 2), (2, 0, 1), (0, 1, 2))
+LAGS = (0, 1, 2, 3, 5, 8, 9)
+PIECE = 896
+
+
+def narrow_groups():
+    qkv = 3 * D
+    wide = FF // 2
+    whole = lambda arg, layer: [[(arg, layer, 0, wide)], [(arg, layer, wide, wide)]]
+    return [
+        whole(0, 0),
+        whole(0, 1),
+        [
+            [(7, None, 0, D), (6, None, 0, D), (2, 0, 0, qkv), (3, 0, 0, D), (9, None, 0, 128)],
+            [(7, None, D, D), (8, None, 0, D), (2, 1, 0, qkv), (3, 1, 0, D), (9, None, 0, 128)],
+        ],
+        whole(4, 0),
+        whole(4, 1),
+    ]
+
+
+def half_width(group):
+    return sum(part[3] for part in group[0])
+
+
+def gather_plan():
+    groups = narrow_groups()
+    starts, cursor = [], 0
+    for group in groups:
+        starts.append(cursor)
+        cursor += half_width(group)
+    pieces = []
+    for kind, number in (("n", 0), ("r", 0), ("n", 1), ("r", 1), ("n", 2), ("n", 3), ("r", 2), ("n", 4), ("r", 3)):
+        if kind == "n":
+            width = half_width(groups[number])
+            count = width // PIECE
+            for k in range(count):
+                size = PIECE if k < count - 1 else width - k * PIECE
+                pieces.append((kind, number, k * PIECE, size))
+        else:
+            pieces.append((kind, number, 0, D))
+            pieces.append((kind, number, 1, D))
+    return groups, starts, cursor, pieces
+
+
+def gather_kernel(sizes, *refs):
+    groups, starts, _, pieces = gather_plan()
+    ins, outs = refs[:10], refs[10:19]
+    halves, other, joined, send_sem, recv_sem, load_sem, swap_sem = refs[19:]
+    place = grid_place()
+    z, y, x, core = place
+    sibling = device_at(moved(place, sizes, 3, 1))
+    loads = []
+    for number, group in enumerate(groups):
+        for half in range(2):
+            cursor = starts[number]
+            for arg, layer, first, size in group[half]:
+                source = ins[arg] if layer is None else ins[arg].at[layer]
+                loads.append((source.at[:, pl.ds(first, size)], halves.at[half, :, pl.ds(cursor, size)]))
+                cursor += size
+    for number, (arg, layer) in enumerate(((1, 0), (1, 1), (5, 0), (5, 1))):
+        for part in range(2):
+            loads.append((ins[arg].at[layer, part], outs[5 + number].at[z, y, x, core, part]))
+    started = []
+    for k, (source, target) in enumerate(loads):
+        copy = pltpu.make_async_copy(source, target, load_sem.at[k])
+        copy.start()
+        started.append(copy)
+    greet(place, sizes)
+    for copy in started:
+        copy.wait()
+    swaps = []
+    for number, group in enumerate(groups):
+        columns = pl.ds(starts[number], half_width(group))
+        copy = pltpu.make_async_remote_copy(
+            src_ref=halves.at[1 - core, :, columns],
+            dst_ref=other.at[:, columns],
+            send_sem=swap_sem.at[0, number],
+            recv_sem=swap_sem.at[1, number],
+            device_id=sibling,
+            device_id_type=MESH_ID,
+        )
+        copy.start()
+        swaps.append(copy)
+
+    def view(piece, where):
+        kind, number, first, size = piece
+        iz, iy, ix = where[:3]
+        if kind == "n":
+            start = pl.multiple_of(core * half_width(groups[number]) + first, 128)
+            return outs[number].at[iz, iy, ix, :, pl.ds(start, size)]
+        return outs[5 + number].at[iz, iy, ix, core, first]
+
+    prepared = {}
+
+    def prepare(piece):
+        kind, number, first, size = piece
+        if kind == "n" and number not in prepared:
+            swaps[number].wait()
+            group = groups[number]
+            for begin in range(starts[number], starts[number] + half_width(group), 128):
+                columns = pl.ds(begin, 128)
+                mine = halves[core, :, columns].astype(jnp.float32)
+                theirs = other[:, columns].astype(jnp.float32)
+                both = [jnp.where(core == 0, mine, theirs), jnp.where(core == 0, theirs, mine)]
+                joined[:, columns] = jnp.concatenate(both, 0).astype(BF)
+            width = half_width(group)
+            copy = pltpu.make_async_copy(
+                joined.at[:, pl.ds(starts[number], width)],
+                outs[number].at[z, y, x, :, pl.ds(pl.multiple_of(core * width, 128), width)],
+                load_sem.at[len(loads) + number],
+            )
+            copy.start()
+            copy.wait()
+            prepared[number] = True
+
+    semaphores = [0]
+
+    def transfers(number):
+        piece = pieces[number]
+        steps, done = [], []
+        for axis in ROUTES[number % len(ROUTES)] + (3,):
+            size, here = sizes[axis], place[axis]
+
+            def block(at):
+                where = list(place)
+                for old in done:
+                    where[old] = slice(None)
+                where[axis] = jnp.clip(at, 0, size - 1)
+                return view(piece, where)
+
+            for hop in range(1, size):
+                hops = []
+                for way in (1, -1):
+                    ahead, behind = here + way, here - way
+                    sent, got = here - way * (hop - 1), here - way * hop
+                    if size == 2 and way == -1:
+                        continue
+                    if size == 2:
+                        ahead, behind, got = 1 - here, 1 - here, 1 - here
+                    pair = []
+                    for at, other_end in ((sent, ahead), (got, behind)):
+                        ref = block(at)
+                        target = place[:axis] + (jnp.clip(other_end, 0, size - 1),) + place[axis + 1 :]
+                        pair.append(
+                            pltpu.make_async_remote_copy(
+                                src_ref=ref,
+                                dst_ref=ref,
+                                send_sem=send_sem.at[semaphores[0]],
+                                recv_sem=recv_sem.at[semaphores[0]],
+                                device_id=device_at(target),
+                                device_id_type=MESH_ID,
+                            )
+                        )
+                    semaphores[0] += 1
+                    sends = jnp.logical_and(inside(sent, size), inside(ahead, size))
+                    hops.append(Hop(pair, sends, inside(got, size)))
+                steps.append(hops)
+            done.append(axis)
+        return steps
+
+    running = {}
+    depth = sum(size - 1 for size in sizes)
+    lags = LAGS if depth + 1 == len(LAGS) else list(range(depth + 1))
+    for tick in range(len(pieces) + lags[-1]):
+        for step in reversed(range(depth + 1)):
+            number = tick - lags[step]
+            if number < 0 or number >= len(pieces):
+                continue
+            if step == 0:
+                prepare(pieces[number])
+                running[number] = transfers(number)
+            else:
+                for copy in running[number][step - 1]:
+                    copy.wait()
+            if step < depth:
+                for copy in running[number][step]:
+                    copy.start()
+    for number in range(len(groups)):
+        if number not in prepared:
+            swaps[number].wait()
+
+
+def gather_plainly(enc_in, enc_down, dec_qkv, dec_out, dec_in, dec_down, cca_q, cca_kv, cca_out, gains):
+    get = lambda w: lax.all_gather(w, ("dp", "seq"), axis=w.ndim - 2, tiled=True)
+    kv = get(cca_kv)
+    return dict(
+        enc_in=get(enc_in), enc_down=get(enc_down), dec_in=get(dec_in), dec_down=get(dec_down), dec_qkv=get(dec_qkv),
+        dec_out=get(dec_out), cca_kv=[kv[:, :D], kv[:, D:]], cca_q=get(cca_q), cca_out=get(cca_out), gains=get(gains)[:, :8],
+    )
+
+
+def gather_weights(enc_in, enc_down, dec_qkv, dec_out, dec_in, dec_down, cca_q, cca_kv, cca_out, gains):
+    sizes = grid_sizes()
+    rows = cca_q.shape[0]
+    groups, starts, total, pieces = gather_plan()
+    part = enc_down.shape[1] // 2
+    if rows % 4 or part % 8 or sizes[1:] != (2, 2, 2):
+        return gather_plainly(enc_in, enc_down, dec_qkv, dec_out, dec_in, dec_down, cca_q, cca_kv, cca_out, gains)
+    lead = sizes[:3]
+    shapes = [lead + (2 * rows, 2 * half_width(group)) for group in groups] + [lead + (2, 2, part, D)] * 4
+    per_piece = sum((size - 1) * (1 if size == 2 else 2) for size in sizes)
+    n_loads = sum(len(half) for group in groups for half in group) + 8 + len(groups)
+    split = lambda w: w.reshape(w.shape[0], 2, part, D)
+    outs = pl.pallas_call(
+        functools.partial(gather_kernel, sizes),
+        out_shape=[jax.ShapeDtypeStruct(shape, BF) for shape in shapes],
+        in_specs=[ANY] * 10,
+        out_specs=[ANY] * 9,
+        scratch_shapes=[
+            pltpu.VMEM((2, rows, total), BF),
+            pltpu.VMEM((rows, total), BF),
+            pltpu.VMEM((2 * rows, total), BF),
+            pltpu.SemaphoreType.DMA((per_piece * len(pieces),)),
+            pltpu.SemaphoreType.DMA((per_piece * len(pieces),)),
+            pltpu.SemaphoreType.DMA((n_loads,)),
+            pltpu.SemaphoreType.DMA((2, len(groups))),
+        ],
+        compiler_params=pltpu.CompilerParams(collective_id=0, has_side_effects=True),
+        name="gather_weights",
+    )(enc_in, split(enc_down), dec_qkv, dec_out, dec_in, split(dec_down), cca_q, cca_kv, cca_out, gains)
+    narrow = [out.reshape(D, out.shape[-1]) for out in outs[:5]]
+    tall = [out.reshape(FF, D) for out in outs[5:]]
+    mixed = narrow[2]
+    half = mixed.shape[1] // 2
+    sides = [mixed[:, :half], mixed[:, half:]]
+    qkv = [side[:, 2 * D : 5 * D] for side in sides]
+    out = [side[:, 5 * D : 6 * D] for side in sides]
+    return dict(
+        enc_in=narrow[:2], enc_down=tall[:2], dec_in=narrow[3:], dec_down=tall[2:], dec_qkv=qkv, dec_out=out,
+        cca_kv=[side[:, :D] for side in sides], cca_q=sides[0][:, D : 2 * D], cca_out=sides[1][:, D : 2 * D],
+        gains=sides[0][:, 6 * D : 6 * D + 8],
+    )
+
+
 HEADS = 14
 HEAD = 64
 SPAN = 64
@@ -294,24 +593,17 @@
     enc_final,
 ):
     offset = lax.axis_index("seq") * tokens.shape[1]
-    enc_weights = (
-        lax.all_gather(enc_gain, ("dp", "seq"), axis=1, tiled=True),
-        lax.all_gather(enc_in, ("dp", "seq"), axis=1, tiled=True),
-        lax.all_gather(enc_down, ("dp", "seq"), axis=1, tiled=True),
-        lax.all_gather(enc_final, ("dp", "seq"), axis=0, tiled=True),
-    )
+    rows = cca_q.shape[0]
+    own_gains = jnp.concatenate([dec_gain.reshape(4, rows), cca_gain[None], enc_gain, enc_final[None]], 0).T
+    own_gains = jnp.pad(own_gains, ((0, 0), (0, 120)))
+    full = gather_weights(enc_in, enc_down, dec_qkv, dec_out, dec_in, dec_down, cca_q, cca_kv, cca_out, own_gains)
+    gains = full["gains"].T
+    enc_weights = (gains[5:7], full["enc_in"], full["enc_down"], gains[7])
     encoded, _ = encode(retrieved, enc_weights[0], enc_weights[1], enc_weights[2], enc_weights[3])
     keep_flag = (neigh_doc != span_doc[..., None]).astype(jnp.bfloat16)
     dec_weights = (
-        lax.all_gather(dec_gain, ("dp", "seq"), axis=2, tiled=True),
-        lax.all_gather(dec_qkv, ("dp", "seq"), axis=1, tiled=True),
-        lax.all_gather(dec_out, ("dp", "seq"), axis=1, tiled=True),
-        lax.all_gather(dec_in, ("dp", "seq"), axis=1, tiled=True),
-        lax.all_gather(dec_down, ("dp", "seq"), axis=1, tiled=True),
-        lax.all_gather(cca_gain, ("dp", "seq"), axis=0, tiled=True),
-        lax.all_gather(cca_q, ("dp", "seq"), axis=0, tiled=True),
-        lax.all_gather(cca_kv, ("dp", "seq"), axis=0, tiled=True),
-        lax.all_gather(cca_out, ("dp", "seq"), axis=0, tiled=True),
+        gains[:4].reshape(2, 2, D), full["dec_qkv"], full["dec_out"], full["dec_in"], full["dec_down"],
+        gains[4], full["cca_q"], jnp.concatenate(full["cca_kv"], 1), full["cca_out"],
     )
     norm_gains, qkv_all, out_all, in_all, down_all, cross_gain, cross_q, cross_kv, cross_out = (
         dec_weights
@@ -380,9 +672,9 @@
     def term():
         blocks = [slab_term(left, right) for left, right in pair_list]
         blocks = blocks + [vector[:, None] for vector in gain_list]
-        return jnp.concatenate(blocks, 1)
-
-    owned = lax.psum_scatter(term(), ("dp", "seq"), scatter_dimension=0, tiled=True)
+        return jnp.concatenate(blocks, 1).astype(jnp.bfloat16)
+
+    owned = lax.psum_scatter(term(), ("dp", "seq"), scatter_dimension=0, tiled=True).astype(jnp.float32)
     pieces = []
     cursor = 0
     for left, right in pair_list:

time: 3220 us -> 1920 us (0.60)
  waiting for transfers between devices: 2440 us -> 1090 us
  Pallas kernels: 0 us -> 317 us
  blocking collectives: 125 us -> 0 us
  local copies, waits for them, and re-layouts: 266 us -> 168 us
    unnamed x17 -> x8, waiting for transfers between devices: 2020 us -> 1050 us
    all_gather x9 -> x0, waiting for transfers between devices: 384 us -> none  [the longest x1 88.5 us: on_device(): lax.all_gather(enc_in, ('dp', 'seq'), axis=1, tiled=True)]
    pallas_call x0 -> x1, Pallas kernels: none -> 317 us  [gather_weights(): pl.pallas_call(functools.partial(gather_kernel, sizes), out_shape=[jax.Sh...]
    all_gather x2 -> x0, blocking collectives: 84.9 us -> none  [the longest x1 45.1 us: on_device(): lax.all_gather(dec_gain, ('dp', 'seq'), axis=2, tiled=True)]
    slice x4 -> x2, local copies, waits for them, and re-layouts: 80.4 us -> 3.52 us  [the longest x1 3.39 us: gather_weights(): side[:, :D]]
    unnamed x1 -> x0, blocking collectives: 40.3 us -> none
    unnamed x360 -> x344, local copies, waits for them, and re-layouts: 117 us -> 102 us
  transfers between devices with their start and end apart: 17 -> 8, of which waited for: 13 -> 3; matrix products, arithmetic and copies ran while one was open for 10% -> 10% of each run, Pallas kernels for 0% -> 17%
where the time goes in v1:
time: 1920 us; the launch traced here: 1910 us
  waiting for transfers between devices  1090 us (57%)
  Pallas kernels  317 us (17%)
  matrix products  252 us (13%)
  local copies, waits for them, and re-layouts  168 us (9%)
  other arithmetic  61.9 us (3%)
    unnamed x8, waiting for transfers between devices  1050 us
    pallas_call x1, Pallas kernels, gather_weights(): pl.pallas_call(functools.partial(gather_kernel, sizes), out_shape=[jax.Sh...  317 us
    unnamed x344, local copies, waits for them, and re-layouts  102 us
    dot_general x15, matrix products, back_project(): lax.dot_general(upstream, weight, (((upstream.ndim - 1,), (1,)), ((), ())...  80.6 us
    dot_general x15, matrix products, project(): return jnp.dot(values, weight, preferred_element_type=jnp.float32)  67.7 us
    dot_general x15, matrix products, slab_term(): lax.dot_general(flat_left, flat_right, (((0,), (0,)), ((), ())), preferre...  64.1 us
  transfers between devices with their start and end apart: 8, of which 3 were waited for; matrix products, arithmetic and copies ran while one was open for 10% of the time, Pallas kernels for 17%

profile of v1, /device:TPU:0, one launch (start us, length us, event | category | flops | bytes accessed | tf_op | source)
XLA Modules:
  0.0 1908.2 jit_solution(15705124838801599311)
XLA Ops:
  19.3 317.4 %gather_weights.1 = (bf16[4,2,2,56,3584]{4,3,2,1,0:T(8,128)(2,1)}, bf16[4,2,2,56,3584]{4,3,2,1,0:T(8,128)(2,1)}, bf16[4,2,2,56,11008]{4,3,2,1,0:T(8,128)(2,1)}, ...) custom-call(bf16[2,28,3584]{2,1,0:T(8,128)(2,1)} %copy.137.refs_0_, ...), custom_call_target="tpu_custom_call" | custom-call | tf_op jit(solution)/shard_map/gather_weights/pallas_call | solution.py:275
  343.1 9.8 fusion.84
  353.0 17.6 multiply_convert_fusion.3
  370.6 4.1 multiply_reduce_fusion.6
  374.7 9.5 fusion.85
  384.3 17.8 multiply_convert_fusion.2
  402.1 4.1 multiply_reduce_fusion.5
  414.8 3.6 convolution_convert_fusion.7
  420.7 4.2 fusion.258
  427.8 4.4 copy.142
  448.7 4.2 fusion.249
  452.9 7.6 multiply_reduce_fusion.8
  465.2 37.6 %all-gather.5.cloned.1.call-done = bf16[1,1024,1792]{2,1,0:T(8,128)(2,1)} async-done(((bf16[1,128,1792]{2,1,0:T(8,128)(2,1)}), bf16[1,1024,1792]{2,1,0:T(8,128)(2,1)}) %all-gather.5.cloned.1.call-update) | async-done | bytes 3670032 | tf_op jit(solution)/shard_map/all_gather | solution.py:401
  502.8 4.2 fusion.257
  510.4 4.4 copy.150
  527.4 5.1 add_convert_fusion.3
  539.7 4.7 fusion.86
  552.7 16.3 copy.206
  569.0 5.5 copy.223
  578.5 3.7 fusion.146
  582.2 41.2 %reduce-scatter.7.cloned.1.call-done = bf16[128,1792]{1,0:T(8,128)(2,1)} async-done(((bf16[1024,1792]{1,0:T(8,128)(2,1)}), bf16[128,1792]{1,0:T(8,128)(2,1)}) %reduce-scatter.7.cloned.1.call-update) | async-done | bytes 458768
  626.0 4.1 fusion.186
  631.6 7.3 add_convert_fusion.2
  659.0 6.0 fusion.89
  665.0 4.4 multiply_reduce_fusion
  675.4 3.8 copy.168
  679.1 4.7 fusion.96
  703.3 16.3 copy.208
  719.6 5.5 copy.222
  725.2 4.8 fusion.147
  731.9 13.1 add_convert_fusion.1
  745.0 9.2 fusion.70
  755.2 11.7 add_convert_fusion
  766.9 6.1 fusion.58
  780.8 4.8 fusion.175
  785.6 3.9 fusion.24
  791.6 4.8 fusion.12
  796.4 6.9 fusion.13
  803.4 3.8 fusion.23
  809.0 4.7 fusion.14
  813.7 7.3 bitcast_dynamic-update-slice_fusion
  823.0 3.6 fusion.47
  828.6 5.7 fusion.15
  834.2 5.5 fusion.16
  839.8 5.7 fusion.17
  845.5 6.1 fusion.18
  870.9 7.8 fusion.160
  879.6 1007.2 %all-reduce.4.cloned.1.call-done = bf16[896,39432]{1,0:T(8,128)(2,1)} async-done(((bf16[896,39432]{1,0:T(8,128)(2,1)}), bf16[896,39432]{1,0:T(8,128)(2,1)}) %all-reduce.4.cloned.1.call-update) | async-done | bytes 70662160
  (505 shorter events, 190.6 us)
Async XLA Ops:
  7.2 10.7 copy-start.107
  7.2 413.5 %all-gather.3.cloned.1.call-start = ((), (), s32[]{:S(2)}) async-start(), calls=%async_computation.2 | async-start | bytes 4128768 | tf_op jit(solution)/shard_map/all_gather | solution.py:401
  8.0 406.4 %collective-permute-start = (bf16[1,2]{1,0:T(2,128)(2,1)S(1)}, bf16[1,2]{1,0:T(2,128)(2,1)S(1)}, u32[]{:S(2)}, u32[]{:S(2)}) collective-permute-start(bf16[1,2]{1,0:T(2,128)(2,1)S(1)} %get-tuple-element.140), channel_id=1, source_target_pairs={{0,1},{1,2},{2,3},{3,4},{4,5},{5,6},{6,7},{8,9},{9,10},{10,11},{11... | collective-permute-start | bytes 20 | tf_op jit(solution)/shard_map/ppermute | solution.py:323
  11.5 326.5 %copy-start.131 = (f32[128]{0:T(128)}, f32[128]{0:T(128)S(1)}, u32[]{:S(2)}) copy-start(f32[128]{0:T(128)S(1)} %fusion.228) | copy-start | bytes 1540
  17.9 320.0 %copy-start.62 = (bf16[1,128,896]{2,1,0:T(8,128)(2,1)S(1)}, bf16[1,128,896]{2,1,0:T(8,128)(2,1)}, u32[]{:S(2)}) copy-start(bf16[1,128,896]{2,1,0:T(8,128)(2,1)} %param.18) | copy-start | bytes 688132
  337.9 196.8 %copy-start.104 = (f32[896]{0:T(1024)}, f32[896]{0:T(1024)S(1)}, u32[]{:S(2)}) copy-start(f32[896]{0:T(1024)S(1)} %get-tuple-element.108) | copy-start | bytes 10756
  342.2 160.6 %all-gather.5.cloned.1.call-start = ((), (), s32[]{:S(2)}) async-start(), calls=%async_computation.3 | async-start | bytes 4128768 | tf_op jit(solution)/shard_map/all_gather | solution.py:401
  342.8 10.1 copy-start.127
  342.8 31.9 %copy-start.117 = (f32[896]{0:T(1024)}, f32[896]{0:T(1024)S(1)}, u32[]{:S(2)}) copy-start(f32[896]{0:T(1024)S(1)} %get-tuple-element.106) | copy-start | bytes 10756
  342.8 63.4 %copy-start.111 = (f32[896]{0:T(1024)}, f32[896]{0:T(1024)S(1)}, u32[]{:S(2)}) copy-start(f32[896]{0:T(1024)S(1)} %get-tuple-element.105) | copy-start | bytes 10756
  342.8 27.7 %slice-start.16 = ((s8[6422528]{0:T(1024)(128)(4,1)}), s8[4194304]{0:T(1024)(128)(4,1)S(1)}, s32[]{:S(2)}) async-start(s8[6422528]{0:T(1024)(128)(4,1)} %bitcast.568), calls=%async_computation.23 | async-start | bytes 8388608
  343.1 9.8 copy-start.129
  343.1 27.4 %slice-start.17 = ((s8[6422528]{0:T(1024)(128)(4,1)}), s8[2228224]{0:T(1024)(128)(4,1)S(1)}, s32[]{:S(2)}) async-start(s8[6422528]{0:T(1024)(128)(4,1)} %bitcast.568), calls=%async_computation.24 | async-start | bytes 4456448
  352.9 17.6 copy-start.32
  370.6 31.5 %slice-start.18 = ((s8[6422528]{0:T(1024)(128)(4,1)}), s8[2228224]{0:T(1024)(128)(4,1)S(1)}, s32[]{:S(2)}) async-start(s8[6422528]{0:T(1024)(128)(4,1)} %bitcast.574), calls=%async_computation.25 | async-start | bytes 4456448
  374.7 27.4 %copy-start.72 = (f32[1,2,2,128,896]{4,3,2,1,0:T(8,128)}, f32[1,2,2,128,896]{4,3,2,1,0:T(8,128)S(1)}, u32[]{:S(2)}) copy-start(f32[1,2,2,128,896]{4,3,2,1,0:T(8,128)S(1)} %get-tuple-element.146) | copy-start | bytes 5505028
  374.7 27.3 %slice-start.19 = ((s8[6422528]{0:T(1024)(128)(4,1)}), s8[4194304]{0:T(1024)(128)(4,1)S(1)}, s32[]{:S(2)}) async-start(s8[6422528]{0:T(1024)(128)(4,1)} %bitcast.574), calls=%async_computation.26 | async-start | bytes 8388608
  384.3 17.8 copy-start.33
  407.6 7.2 collective-permute-start.1
  410.8 21.3 %copy-start.64 = (bf16[1,128,896]{1,2,0:T(8,128)(2,1)}, bf16[1,128,896]{1,2,0:T(8,128)(2,1)S(1)}, u32[]{:S(2)}) copy-start(bf16[1,128,896]{1,2,0:T(8,128)(2,1)S(1)} %copy.143) | copy-start | bytes 688132
  419.4 24.4 %copy-start.17 = (bf16[1,2,256,896]{2,3,1,0:T(8,128)(2,1)}, bf16[1,2,256,896]{2,3,1,0:T(8,128)(2,1)S(1)}, u32[]{:S(2)}) copy-start(bf16[1,2,256,896]{2,3,1,0:T(8,128)(2,1)S(1)} %copy.147) | copy-start | bytes 2752516
  460.5 61.4 %copy-start.42 = (f32[1,128,896]{2,1,0:T(8,128)}, f32[1,128,896]{2,1,0:T(8,128)S(1)}, u32[]{:S(2)}) copy-start(f32[1,128,896]{2,1,0:T(8,128)S(1)} %get-tuple-element.157) | copy-start | bytes 1376260
  464.9 158.5 %reduce-scatter.7.cloned.1.call-start = ((), (), s32[]{:S(2)}) async-start(), calls=%async_computation.4 | async-start | bytes 4128768
  465.1 49.6 %copy-start.66 = (bf16[1,128,896]{1,2,0:T(8,128)(2,1)}, bf16[1,128,896]{1,2,0:T(8,128)(2,1)S(1)}, u32[]{:S(2)}) copy-start(bf16[1,128,896]{1,2,0:T(8,128)(2,1)S(1)} %copy.151) | copy-start | bytes 688132
  516.2 11.2 slice-start.12
  524.8 10.0 copy-start.10
  524.9 9.9 copy-start.115
  574.5 201.2 %reduce-scatter.9.cloned.1.call-start = ((), (), s32[]{:S(2)}) async-start(), calls=%async_computation.5 | async-start | bytes 4128768
  582.2 47.9 %copy-start.102 = (bf16[14,64,128]{2,1,0:T(8,128)(2,1)}, bf16[14,64,128]{2,1,0:T(8,128)(2,1)S(1)}, u32[]{:S(2)}) copy-start(bf16[14,64,128]{2,1,0:T(8,128)(2,1)S(1)} %fusion.146) | copy-start | bytes 688132
  582.2 43.8 %copy-start.43 = (f32[1,128,896]{2,1,0:T(8,128)S(1)}, f32[1,128,896]{2,1,0:T(8,128)}, u32[]{:S(2)}) copy-start(f32[1,128,896]{2,1,0:T(8,128)} %copy-done.42) | copy-start | bytes 1376260
  626.0 12.9 slice-start.6
  654.1 10.9 slice-start
  675.4 10.6 slice-start.2
  684.7 45.4 %collective-permute-start.2 = (bf16[1,2,128,896]{3,2,1,0:T(8,128)(2,1)}, bf16[1,2,128,896]{3,2,1,0:T(8,128)(2,1)}, u32[]{:S(2)}, u32[]{:S(2)}) collective-permute-start(bf16[1,2,128,896]{3,2,1,0:T(8,128)(2,1)} %fusion.183), channel_id=1, source_target_pairs={{1,0},{2,1},{3,2},{4,3},{5,4},{6,5},{7,6},{9,8},{10,9},{11,10},{12... | collective-permute-start | bytes 1376264 | tf_op jit(solution)/shard_map/ppermute | solution.py:323
  725.2 1161.6 %all-reduce.4.cloned.1.call-start = ((), (), s32[]{:S(2)}) async-start(), calls=%async_computation.6 | async-start | bytes 141754368
  725.2 29.9 %slice-start.10 = ((s8[7340032]{0:T(1024)(128)(4,1)}), s8[4194304]{0:T(1024)(128)(4,1)S(1)}, s32[]{:S(2)}) async-start(s8[7340032]{0:T(1024)(128)(4,1)} %bitcast.499), calls=%async_computation.17 | async-start | bytes 8388608
  731.1 23.1 %copy-start.22 = (f32[1,1,2,128,896]{4,3,2,1,0:T(8,128)}, f32[1,1,2,128,896]{4,3,2,1,0:T(8,128)S(1)}, u32[]{:S(2)}) copy-start(f32[1,1,2,128,896]{4,3,2,1,0:T(8,128)S(1)} %bitcast_convert_fusion.4) | copy-start | bytes 2752516
  731.8 13.1 copy-start.118
  731.9 13.1 copy-start.126
  731.9 23.2 %slice-start.11 = ((s8[7340032]{0:T(1024)(128)(4,1)}), s8[3145728]{0:T(1024)(128)(4,1)S(1)}, s32[]{:S(2)}) async-start(s8[7340032]{0:T(1024)(128)(4,1)} %bitcast.499), calls=%async_computation.18 | async-start | bytes 6291456
  754.3 12.6 slice-start.14
  755.1 11.8 copy-start.100
  755.1 11.7 copy-start.95
  755.1 11.7 copy-start.130
  755.2 11.7 slice-start.15
  851.5 11.1 copy-start.93
  851.5 13.4 copy-start.92
  851.5 15.6 copy-start.91
  (117 other events, 499.9 us)
Sparse Core Ops, SparseCore 0:
  342.3 33.9 all-gather.2
  465.0 37.7 all-gather.4
  574.6 48.7 reduce-scatter.6
  725.3 50.2 reduce-scatter.8
  869.5 1017.2 all-reduce.3

commit v2 on v1

--- a/solution.py
+++ b/solution.py
@@ -303,6 +303,403 @@
     )
 
 
+ORDERS = ((1, False), (2, False), (1, True), (2, False), (1, False), (2, True))
+CORE, HEAVY, ZED, PAIR, CORE_AGAIN, PER_PIECE = 0, 1, 2, 8, 9, 10
+START = (0, 1, 4, 6, 7, 8, 9, 10, 11)
+SLOTS = dict(part=2, whole=5, half=8, sibling=3, heavy=8, middle=8, last=8, zed=6, final=4)
+
+
+def gradient_pieces():
+    pieces = []
+    both = lambda left, right, out, layer, k: tuple(
+        (left, right, 2 * D * half + D * k, out, layer, 2 * D * half + D * k) for half in range(2)
+    )
+    for layer in reversed(range(2)):
+        base = 8 * layer
+        for k in range(2):
+            pieces.append(both(base + 6, base + 7, 5, layer, k))
+        for k in range(2):
+            pieces.append(both(base + 4, base + 5, 4, layer, k))
+    pieces.append(tuple((8 * layer + 2, 8 * layer + 3, 0, 3, layer, 0) for layer in range(2)))
+    for k in range(3):
+        pieces.append(tuple((8 * layer, 8 * layer + 1, D * k, 2, layer, D * k) for layer in range(2)))
+    pieces.append(((16, 17, 0, 6, None, 0), (20, 21, 0, 8, None, 0)))
+    pieces.append(tuple((18, 19, D * half, 7, None, D * half) for half in range(2)))
+    for layer in reversed(range(2)):
+        base = 22 + 4 * layer
+        for k in range(2):
+            pieces.append(both(base + 2, base + 3, 1, layer, k))
+        for k in range(2):
+            pieces.append(both(base, base + 1, 0, layer, k))
+    return pieces
+
+
+N_OPERANDS = 30
+
+
+class Sums:
+    def __init__(self, place, sizes, sems, buffers, slots, width):
+        self.place, self.sizes, self.width = place, sizes, width
+        self.send_sem, self.recv_sem = sems
+        self.part, self.whole, self.half, self.sibling, self.heavy, self.middle, self.last, self.zed, self.final = buffers
+        self.slots = slots
+
+    def slot(self, name, number):
+        return lax.rem(number, self.slots[name])
+
+    def copy(self, number, which, source, target, device):
+        index = number * PER_PIECE + which
+        return pltpu.make_async_remote_copy(
+            src_ref=source,
+            dst_ref=target,
+            send_sem=self.send_sem.at[index],
+            recv_sem=self.recv_sem.at[index],
+            device_id=device_at(device),
+            device_id_type=MESH_ID,
+        )
+
+    def core_copy(self, number):
+        return self.copy(
+            number,
+            CORE,
+            self.part.at[self.slot("part", number)],
+            self.sibling.at[self.slot("sibling", number)],
+            self.swapped(3),
+        )
+
+    def swapped(self, axis):
+        return self.place[:axis] + (1 - self.place[axis],) + self.place[axis + 1 :]
+
+    def heavy_copy(self, number, axis):
+        whole = self.whole.at[self.slot("whole", number)]
+        there = 1 - self.place[axis]
+        source = whole.at[:, there] if axis == 1 else whole.at[:, :, there]
+        return self.copy(number, HEAVY, source, self.heavy.at[self.slot("heavy", number)], self.swapped(axis))
+
+    def pair_copy(self, number, axis, early):
+        half = self.half.at[self.slot("half", number)]
+        there = 1 - self.place[axis]
+        if early:
+            source, target = half.at[:, there], self.middle.at[self.slot("middle", number)]
+        else:
+            source, target = half.at[self.place[0], there], self.last.at[self.slot("last", number)]
+        return self.copy(number, PAIR, source, target, self.swapped(axis))
+
+    def zed_block(self, number, axis, early, at):
+        half = self.half.at[self.slot("half", number)]
+        at = jnp.clip(at, 0, self.sizes[0] - 1)
+        return half.at[at, pl.ds(self.place[axis], 1)] if early else half.at[at]
+
+    def zed_room(self, number, early, hop, way):
+        room = self.zed.at[self.slot("zed", number), hop - 1, way]
+        return room.at[pl.ds(0, 1)] if early else room
+
+    def zed_hops(self, number, axis, early, hop):
+        z, size = self.place[0], self.sizes[0]
+        found = []
+        for way, by in enumerate((-1, 1)):
+            sent, ahead = z + by * hop, z + by
+            behind, got = z - by, z - by + by * hop
+            room = self.zed_room(number, early, hop, way)
+            device = (jnp.clip(ahead, 0, size - 1),) + self.place[1:]
+            copy = self.copy(number, ZED + 2 * (hop - 1) + way, self.zed_block(number, axis, early, sent), room, device)
+            sends = jnp.logical_and(inside(sent, size), inside(ahead, size))
+            receives = jnp.logical_and(inside(got, size), inside(behind, size))
+            found.append((copy, sends, receives, self.zed_block(number, axis, early, got), room))
+        return found
+
+    def start_zed(self, number, axis, early, hop):
+        for copy, sends, _, _, _ in self.zed_hops(number, axis, early, hop):
+            pl.when(sends)(copy.start)
+
+    def finish_zed(self, number, axis, early, hop):
+        for copy, sends, receives, block, room in self.zed_hops(number, axis, early, hop):
+            pl.when(sends)(copy.wait_send)
+
+            @pl.when(receives)
+            def _():
+                copy.wait_recv()
+                for k in range(1 if early else 2):
+                    block[k] = block[k] + room[k]
+
+    def add_core(self, number):
+        self.core_copy(number).wait()
+        whole, sibling = self.slot("whole", number), self.slot("sibling", number)
+
+        def one(k, _):
+            at = (k // 4, (k // 2) % 2, k % 2)
+            self.whole[(whole, *at)] = self.whole[(whole, *at)] + self.sibling[(sibling, *at)]
+            return 0
+
+        lax.fori_loop(0, 4 * self.sizes[0], one, 0)
+
+    def add_heavy(self, number, axis):
+        self.heavy_copy(number, axis).wait()
+        whole, half, heavy = (self.slot(name, number) for name in ("whole", "half", "heavy"))
+
+        def one(k, _):
+            z, o = k // 2, k % 2
+            at = (z, self.place[1], o) if axis == 1 else (z, o, self.place[2])
+            self.half[half, z, o] = self.whole[(whole, *at)] + self.heavy[heavy, z, o]
+            return 0
+
+        lax.fori_loop(0, 2 * self.sizes[0], one, 0)
+
+    def add_pair(self, number, axis, early):
+        self.pair_copy(number, axis, early).wait()
+        half, here = self.slot("half", number), self.place[axis]
+        if early:
+            for z in range(self.sizes[0]):
+                self.half[half, z, here] = self.half[half, z, here] + self.middle[self.slot("middle", number), z]
+        else:
+            z = self.place[0]
+            self.half[half, z, here] = self.half[half, z, here] + self.last[self.slot("last", number)]
+
+    def split_rows(self, number, axis):
+        half, final = self.slot("half", number), self.slot("final", number)
+        rows = self.half[half, self.place[0], self.place[axis]].astype(jnp.float32)
+        count = rows.shape[0] // 2
+        first, second = rows[:count], rows[count:]
+        self.final[final, 0] = jnp.where(self.place[3] == 0, first, second)
+        self.final[final, 2] = jnp.where(self.place[3] == 0, second, first)
+
+    def final_copy(self, number):
+        final = self.slot("final", number)
+        return self.copy(number, CORE_AGAIN, self.final.at[final, 2], self.final.at[final, 1], self.swapped(3))
+
+    def step(self, step, number, first, early):
+        other = 3 - first
+        sequence = [("pair", 0), ("zed", 3), ("zed", 2), ("zed", 1)] if early else [("zed", 3), ("zed", 2), ("zed", 1), ("pair", 0)]
+        if step == 1:
+            self.heavy_copy(number, first).start()
+            return
+        if step == 2:
+            self.add_heavy(number, first)
+        else:
+            kind, hop = sequence[step - 3]
+            if kind == "pair":
+                self.add_pair(number, other, early)
+            else:
+                self.finish_zed(number, other, early, hop)
+        if step < 6:
+            kind, hop = sequence[step - 2]
+            if kind == "pair":
+                self.pair_copy(number, other, early).start()
+            else:
+                self.start_zed(number, other, early, hop)
+        else:
+            self.split_rows(number, other)
+            self.final_copy(number).start()
+
+
+def reduce_kernel(sizes, tall, *refs):
+    pieces = gradient_pieces()
+    operands, gains = refs[:N_OPERANDS], refs[N_OPERANDS]
+    outs = refs[N_OPERANDS + 1 : N_OPERANDS + 11]
+    scratch = refs[N_OPERANDS + 11 :]
+    left, right, product = scratch[:3]
+    buffers, small = scratch[3:12], scratch[12:21]
+    send_sem, recv_sem, small_send, small_recv, load_sem, out_sem = scratch[21:]
+    place = grid_place()
+    core = place[3]
+    count = len(pieces)
+    sums = Sums(place, sizes, (send_sem, recv_sem), buffers, SLOTS, D)
+    once = Sums(place, sizes, (small_send, small_recv), small, {name: 1 for name in SLOTS}, 128)
+    is_tall = [tall[piece[0][0]] for piece in pieces]
+    first_tall = is_tall.index(True)
+    long_rows, short_rows = left.shape[2], None
+
+    def rows_of(k):
+        return operands[pieces[k][0][0]].shape[0]
+
+    def loads(k, slot):
+        rows = rows_of(k)
+        found = []
+        for half in range(2):
+            l, r, column, _, _, _ = pieces[k][half]
+            mine = jnp.where(core == half, 1, 0)
+            found.append((operands[l], left.at[slot, mine, pl.ds(0, rows)], load_sem.at[slot, half]))
+            found.append((operands[r].at[:, pl.ds(column, D)], right.at[slot, mine, pl.ds(0, rows)], load_sem.at[slot, 2 + half]))
+        return [pltpu.make_async_copy(*args) for args in found]
+
+    def start_loads(number):
+        for k in range(count):
+
+            @pl.when(number == k)
+            def _():
+                for copy in loads(k, k % 2):
+                    copy.start()
+
+    def multiply(number, which, rows):
+        slot = lax.rem(number, 2)
+
+        def block(k, _):
+            columns = pl.ds(pl.multiple_of(k * 128, 128), 128)
+            product[pl.ds(pl.multiple_of(k * 128, 128), 128), :] = lax.dot_general(
+                left[slot, which, pl.ds(0, rows), columns],
+                right[slot, which, pl.ds(0, rows), :],
+                (((0,), (0,)), ((), ())),
+                preferred_element_type=jnp.float32,
+            )
+            return 0
+
+        lax.fori_loop(0, D // 128, block, 0)
+        chunk = sums.whole.shape[4]
+
+        def store(k, _):
+            values = product[pl.ds(pl.multiple_of(k * chunk, 8), chunk), :].astype(BF)
+            at = (k // 4, (k // 2) % 2, k % 2)
+            if which == 0:
+                sums.part[(sums.slot("part", number), *at)] = values
+            else:
+                sums.whole[(sums.slot("whole", number), *at)] = values
+            return 0
+
+        lax.fori_loop(0, D // chunk, store, 0)
+
+    def compute(number):
+        for flag in sorted(set(is_tall)):
+            wanted = jnp.logical_and(number >= first_tall, flag) if flag else number < first_tall
+            k = first_tall if flag else 0
+
+            @pl.when(wanted)
+            def _():
+                for copy in loads(k, lax.rem(number, 2)):
+                    copy.wait()
+                multiply(number, 0, rows_of(k))
+                sums.core_copy(number).start()
+                multiply(number, 1, rows_of(k))
+
+    def out_copies(k):
+        slot = k % SLOTS["final"]
+        found = []
+        for half in range(2):
+            _, _, _, out, layer, column = pieces[k][half]
+            target = outs[out] if layer is None else outs[out].at[layer]
+            source = sums.final.at[slot, jnp.where(core == half, 0, 1)]
+            found.append(pltpu.make_async_copy(source, target.at[:, pl.ds(column, D)], out_sem.at[slot, half]))
+        return found
+
+    greet(place, sizes)
+    small_loads = []
+    for k, target in enumerate((once.part.at[0], once.whole.at[0])):
+        copy = pltpu.make_async_copy(gains, target, out_sem.at[SLOTS["final"], k])
+        copy.start()
+        small_loads.append(copy)
+    start_loads(0)
+
+    def tick(time, _):
+        for step in reversed(range(8)):
+
+            @pl.when(time == START[step])
+            def _():
+                if step == 0:
+                    for copy in small_loads:
+                        copy.wait()
+                    once.core_copy(0).start()
+                elif step == 7:
+                    once.final_copy(0).wait()
+                    copy = pltpu.make_async_copy(once.final.at[0, 0], outs[9], out_sem.at[SLOTS["final"], 0])
+                    copy.start()
+                    copy.wait()
+                else:
+                    if step == 1:
+                        once.add_core(0)
+                    once.step(step, 0, *ORDERS[-1])
+
+        for step in reversed(range(9)):
+            number = time - START[step]
+
+            @pl.when(jnp.logical_and(number >= 0, number < count))
+            def _():
+                if step == 0:
+                    start_loads(number + 1)
+                    compute(number)
+                elif step == 8:
+                    for copy in out_copies_at(number):
+                        copy.wait()
+                elif step == 7:
+                    sums.final_copy(number).wait()
+                    for k in range(count):
+
+                        @pl.when(number == k)
+                        def _():
+                            for copy in out_copies(k):
+                                copy.start()
+
+                else:
+                    if step == 1:
+                        sums.add_core(number)
+                    turn = lax.rem(number, len(ORDERS))
+                    for order in sorted(set(ORDERS)):
+                        here = functools.reduce(jnp.logical_or, [turn == k for k, one in enumerate(ORDERS) if one == order])
+
+                        @pl.when(here)
+                        def _():
+                            sums.step(step, number, *order)
+
+        return 0
+
+    def out_copies_at(number):
+        slot = lax.rem(number, SLOTS["final"])
+        return [
+            pltpu.make_async_copy(sums.final.at[slot, 0], outs[3].at[0, :, pl.ds(0, D)], out_sem.at[slot, half])
+            for half in range(2)
+        ]
+
+    lax.fori_loop(0, count + START[8], tick, 0)
+
+
+def reduce_gradients(operands, gains, layers_rows):
+    sizes = grid_sizes()
+    rows = layers_rows
+    chunk = 2 * rows
+    lead = sizes[:3] + (chunk,)
+    longest = max(x.shape[0] for x in operands)
+    shortest = min(x.shape[0] for x in operands)
+    tall = tuple(x.shape[0] == longest for x in operands)
+    f32 = jnp.float32
+    shapes = [(2, rows, FF), (2, rows, FF), (2, rows, 3 * D), (2, rows, D), (2, rows, FF), (2, rows, FF)]
+    shapes += [(rows, D), (rows, 2 * D), (rows, D), (rows, 128)]
+
+    def rooms(slots, width):
+        z = sizes[0]
+        return [
+            pltpu.VMEM((slots["part"],) + lead + (width,), BF),
+            pltpu.VMEM((slots["whole"],) + lead + (width,), BF),
+            pltpu.VMEM((slots["half"], z, 2, chunk, width), BF),
+            pltpu.VMEM((slots["sibling"],) + lead + (width,), BF),
+            pltpu.VMEM((slots["heavy"], z, 2, chunk, width), BF),
+            pltpu.VMEM((slots["middle"], z, chunk, width), BF),
+            pltpu.VMEM((slots["last"], chunk, width), BF),
+            pltpu.VMEM((slots["zed"], z - 1, 2, 2, chunk, width), BF),
+            pltpu.VMEM((slots["final"], 3, rows, width), f32),
+        ]
+
+    count = len(gradient_pieces())
+    return pl.pallas_call(
+        functools.partial(reduce_kernel, sizes, tall),
+        out_shape=[jax.ShapeDtypeStruct(shape, f32) for shape in shapes],
+        in_specs=[ANY] * (N_OPERANDS + 1),
+        out_specs=[ANY] * 10,
+        scratch_shapes=[
+            pltpu.VMEM((2, 2, longest, D), BF),
+            pltpu.VMEM((2, 2, longest, D), BF),
+            pltpu.VMEM((D, D), f32),
+            *rooms(SLOTS, D),
+            *rooms({name: 1 for name in SLOTS}, 128),
+            pltpu.SemaphoreType.DMA((PER_PIECE * count,)),
+            pltpu.SemaphoreType.DMA((PER_PIECE * count,)),
+            pltpu.SemaphoreType.DMA((PER_PIECE,)),
+            pltpu.SemaphoreType.DMA((PER_PIECE,)),
+            pltpu.SemaphoreType.DMA((2, 4)),
+            pltpu.SemaphoreType.DMA((SLOTS["final"] + 1, 2)),
+        ],
+        compiler_params=pltpu.CompilerParams(collective_id=1, has_side_effects=True, vmem_limit_bytes=62 << 20),
+        name="reduce_gradients",
+    )(*operands, gains.reshape(lead + (128,)))
+
+
 HEADS = 14
 HEAD = 64
 SPAN = 64
@@ -669,53 +1066,50 @@
         gain_list = gain_list + [attn_gain_g[layer_idx], ffn_gain_g[layer_idx]]
     gain_list = gain_list + [cross_gain_g] + list(enc_gain_g) + [final_gain_g]
 
-    def term():
-        blocks = [slab_term(left, right) for left, right in pair_list]
-        blocks = blocks + [vector[:, None] for vector in gain_list]
-        return jnp.concatenate(blocks, 1).astype(jnp.bfloat16)
-
-    owned = lax.psum_scatter(term(), ("dp", "seq"), scatter_dimension=0, tiled=True).astype(jnp.float32)
-    pieces = []
-    cursor = 0
-    for left, right in pair_list:
-        width = right.shape[-1]
-        pieces.append(owned[:, cursor : cursor + width])
-        cursor = cursor + width
-    gain_cols = owned[:, cursor:]
-    dec_qkv_g = jnp.stack([pieces[4 * idx] for idx in range(DEC_LAYERS)])
-    dec_out_g = jnp.stack([pieces[4 * idx + 1] for idx in range(DEC_LAYERS)])
-    dec_in_g = jnp.stack([pieces[4 * idx + 2] for idx in range(DEC_LAYERS)])
-    dec_down_g = jnp.stack([pieces[4 * idx + 3].T for idx in range(DEC_LAYERS)])
-    base = 4 * DEC_LAYERS
-    cross_q_g = pieces[base]
-    cross_kv_g = pieces[base + 1]
-    cross_out_g = pieces[base + 2]
-    base = base + 3
-    enc_in_g = jnp.stack([pieces[base + 2 * idx] for idx in range(ENC_LAYERS)])
-    enc_down_g = jnp.stack([pieces[base + 2 * idx + 1].T for idx in range(ENC_LAYERS)])
-    dec_gain_g = jnp.stack(
-        [jnp.stack([gain_cols[:, 2 * idx], gain_cols[:, 2 * idx + 1]]) for idx in range(DEC_LAYERS)]
-    )
-    cross_gain_out = gain_cols[:, 2 * DEC_LAYERS]
-    enc_gain_out = jnp.stack([gain_cols[:, 2 * DEC_LAYERS + 1 + idx] for idx in range(ENC_LAYERS)])
-    final_out = gain_cols[:, 2 * DEC_LAYERS + 1 + ENC_LAYERS]
+    grads = sum_gradients(pair_list, gain_list, rows)
+    (enc_in_g, enc_down_g, dec_qkv_g, dec_out_g, dec_in_g, dec_down_g, cross_q_g, cross_kv_g, cross_out_g, gain_cols) = grads
+    gain_rows = gain_cols[:, :8].T
     return (
         result,
         upstream,
-        dec_gain_g,
+        gain_rows[:4].reshape(2, 2, rows),
         dec_qkv_g,
         dec_out_g,
         dec_in_g,
-        dec_down_g,
-        cross_gain_out,
+        jnp.swapaxes(dec_down_g, 1, 2),
+        gain_rows[4],
         cross_q_g,
         cross_kv_g,
         cross_out_g,
-        enc_gain_out,
+        gain_rows[5:7],
         enc_in_g,
-        enc_down_g,
-        final_out,
-    )
+        jnp.swapaxes(enc_down_g, 1, 2),
+        gain_rows[7],
+    )
+
+
+def sum_plainly(pair_list, gain_list):
+    blocks = [slab_term(left, right) for left, right in pair_list] + [vector[:, None] for vector in gain_list]
+    owned = lax.psum_scatter(
+        jnp.concatenate(blocks, 1).astype(BF), ("dp", "seq"), scatter_dimension=0, tiled=True
+    ).astype(jnp.float32)
+    pieces, cursor = [], 0
+    for _, right in pair_list:
+        pieces.append(owned[:, cursor : cursor + right.shape[-1]])
+        cursor += right.shape[-1]
+    two = lambda first, second: jnp.stack([pieces[first], pieces[second]])
+    return [
+        two(11, 13), two(12, 14), two(0, 4), two(1, 5), two(2, 6), two(3, 7), pieces[8], pieces[9], pieces[10], owned[:, cursor:]
+    ]
+
+
+def sum_gradients(pair_list, gain_list, rows):
+    sizes = grid_sizes()
+    if rows % 4 or sizes != (4, 2, 2, 2):
+        return sum_plainly(pair_list, gain_list)
+    operands = [x.reshape(-1, x.shape[-1]) for pair in pair_list for x in pair]
+    gains = jnp.pad(jnp.stack(gain_list).astype(BF).T, ((0, 0), (0, 128 - len(gain_list))))
+    return reduce_gradients(operands, gains, rows)
 
 
 def solution(mesh):

time: 1920 us -> 1090 us (0.57)
  waiting for transfers between devices: 1090 us -> 71.7 us
  Pallas kernels: 317 us -> 616 us
  matrix products: 252 us -> 183 us
  local copies, waits for them, and re-layouts: 168 us -> 111 us
    unnamed x8 -> x4, waiting for transfers between devices: 1050 us -> 0.07 us
    pallas_call x0 -> x1, Pallas kernels: none -> 298 us  [reduce_gradients(): pl.pallas_call(functools.partial(reduce_kernel, sizes, tall), out_shape=[...]
    unnamed x344 -> x285, local copies, waits for them, and re-layouts: 102 us -> 32.1 us
    dot_general x15 -> x0, matrix products: 64.1 us -> none  [slab_term(): lax.dot_general(flat_left, flat_right, (((0,), (0,)), ((), ())), preferre...]
    reduce_scatter x0 -> x2, waiting for transfers between devices: none -> 35.4 us  [self_back(): lax.psum_scatter(grad_pairs.astype(jnp.bfloat16), 'seq', scatter_dimensio...]
  transfers between devices with their start and end apart: 8 -> 7, of which waited for: 3 -> 3; matrix products, arithmetic and copies ran while one was open for 10% -> 16% of each run, Pallas kernels for 17% -> 29%
where the time goes in v2:
time: 1090 us; the launch traced here: 1080 us
  Pallas kernels  616 us (57%)
  matrix products  183 us (17%)
  local copies, waits for them, and re-layouts  111 us (10%)
  other arithmetic  74.7 us (7%)
  waiting for transfers between devices  71.7 us (7%)
  between operations  16.4 us (2%)
    pallas_call x1, Pallas kernels, gather_weights(): pl.pallas_call(functools.partial(gather_kernel, sizes), out_shape=[jax.Sh...  318 us
    pallas_call x1, Pallas kernels, reduce_gradients(): pl.pallas_call(functools.partial(reduce_kernel, sizes, tall), out_shape=[...  298 us
    dot_general x15, matrix products, back_project(): lax.dot_general(upstream, weight, (((upstream.ndim - 1,), (1,)), ((), ())...  79.6 us
    dot_general x15, matrix products, project(): return jnp.dot(values, weight, preferred_element_type=jnp.float32)  66 us
    all_gather x2, waiting for transfers between devices, self_forward(): keys_vals = lax.all_gather(joined[..., D:], 'seq', axis=1, tiled=True)  36.2 us
    convert_element_type x2, other arithmetic, feed_forward(): hidden = gelu_exact(hidden_pre).astype(jnp.bfloat16)  35.4 us
    reduce_scatter x2, waiting for transfers between devices, self_back(): lax.psum_scatter(grad_pairs.astype(jnp.bfloat16), 'seq', scatter_dimensio...  35.4 us
    unnamed x285, local copies, waits for them, and re-layouts  32.1 us
  transfers between devices with their start and end apart: 7, of which 3 were waited for; matrix products, arithmetic and copies ran while one was open for 16% of the time, Pallas kernels for 29%

profile of v2, /device:TPU:0, one launch (start us, length us, event | category | flops | bytes accessed | tf_op | source)
XLA Modules:
  0.0 1080.5 jit_solution(12945722200438533253)
XLA Ops:
  19.3 317.8 %gather_weights.1 = (bf16[4,2,2,56,3584]{4,3,2,1,0:T(8,128)(2,1)}, bf16[4,2,2,56,3584]{4,3,2,1,0:T(8,128)(2,1)}, bf16[4,2,2,56,11008]{4,3,2,1,0:T(8,128)(2,1)}, ...) custom-call(bf16[2,28,3584]{2,1,0:T(8,128)(2,1)} %copy.140.refs_0_, ...), custom_call_target="tpu_custom_call" | custom-call | tf_op jit(solution)/shard_map/gather_weights/pallas_call | solution.py:275
  339.1 3.3 fusion.41
  344.5 9.5 fusion.71
  354.0 17.6 %multiply_convert_fusion.3 = (bf16[2,2,128,3584]{3,2,1,0:T(8,128)(2,1)S(1)}, f32[2,2,128,3584]{3,2,1,0:T(8,128)}) fusion(f32[2,2,128,3584]{3,2,1,0:T(8,128)S(1)} %get-tuple-element.152, u8[2,128,3584]{2,1,0:T(8,128)(4,1)S(1)} %get-tuple-element.101, u8[2,128,3584]{2,1,0:T(8,128)(4,1)S(1)} %get-tuple-element.100), kind=kLoop, calls=%fused_computation.37 | loop fusion | flops 128450560 | bytes 20185088 | tf_op jit(solution)/shard_map/convert_element_type | solution.py:771
  371.6 4.1 multiply_reduce_fusion.6
  376.1 9.7 fusion.72
  385.8 17.8 %multiply_convert_fusion.2 = (bf16[2,2,128,3584]{3,2,1,0:T(8,128)(2,1)S(1)}, f32[2,2,128,3584]{3,2,1,0:T(8,128)}) fusion(f32[2,2,128,3584]{3,2,1,0:T(8,128)S(1)} %get-tuple-element.155, u8[2,128,3584]{2,1,0:T(8,128)(4,1)S(1)} %get-tuple-element.99, u8[2,128,3584]{2,1,0:T(8,128)(4,1)S(1)} %get-tuple-element.98), kind=kLoop, calls=%fused_computation.24 | loop fusion | flops 128450560 | bytes 20185088 | tf_op jit(solution)/shard_map/convert_element_type | solution.py:771
  403.7 4.1 multiply_reduce_fusion.5
  409.2 3.1 collective-permute-start.1
  412.5 3.4 fusion.202
  416.5 3.6 convolution_convert_fusion
  422.6 4.2 fusion.204
  426.8 2.9 copy.147
  429.7 4.3 copy.145
  450.9 8.1 multiply_convert_fusion.9
  460.4 3.4 fusion.38
  464.9 36.2 %all-gather.5.cloned.1.call-done = bf16[1,1024,1792]{2,1,0:T(8,128)(2,1)} async-done(((bf16[1,128,1792]{2,1,0:T(8,128)(2,1)}), bf16[1,1024,1792]{2,1,0:T(8,128)(2,1)}) %all-gather.5.cloned.1.call-update) | async-done | bytes 3670032 | tf_op jit(solution)/shard_map/all_gather | solution.py:798
  501.2 4.2 fusion.203
  505.4 2.9 copy.155
  508.3 4.4 copy.153
  522.2 5.5 multiply_convert_fusion.8
  527.7 5.3 add_convert_fusion.3.refs_13_
  536.7 2.7 fusion.141
  540.5 6.0 fusion.73
  546.5 3.9 multiply_reduce_fusion.1
  550.4 3.1 copy.159
  553.4 6.1 multiply_convert_fusion.1
  561.9 3.8 copy.158
  565.7 3.7 pad_maximum_fusion
  575.1 3.7 fusion.130
  579.0 5.3 fusion.144
  584.2 34.1 %reduce-scatter.3.cloned.1.call-done = bf16[1,128,1792]{2,1,0:T(8,128)(2,1)} async-done(((bf16[1,1024,1792]{2,1,0:T(8,128)(2,1)}), bf16[1,128,1792]{2,1,0:T(8,128)(2,1)}) %reduce-scatter.3.cloned.1.call-update) | async-done | bytes 458768 | tf_op jit(solution)/shard_map/reduce_scatter | solution.py:848
  618.4 4.2 fusion.168
  624.1 5.3 add_convert_fusion.2.refs_5_
  642.5 2.9 copy.196
  646.5 2.8 copy.195
  657.8 5.9 fusion.76
  675.0 4.4 fusion.80
  683.7 4.0 reshape.1559
  687.7 3.1 copy.166
  690.8 3.8 copy.165
  694.6 3.6 pad_maximum_fusion.1
  708.2 14.8 %add_convert_fusion.1 = bf16[2,2,128,3584]{3,2,1,0:T(8,128)(2,1)} fusion(f32[2,2,128,3584]{3,2,1,0:T(8,128)} %get-tuple-element.135, f32[2,2,128,3584]{3,2,1,0:T(8,128)} %copy-done.28, bf16[3584,896,1,1]{1,0,3,2:T(8,128)(2,1)} %bitcast.474, bf16[1,2,2,128,896]{4,3,2,1,0:T(8,128)(2,1)} %fusion.180), kind=kOutput, calls=%fused_computation.14 | convolution fusion | flops 3314024448 | bytes 25690112 | tf_op jit(solution)/shard_map/dot_general | solution.py:736
  723.1 9.3 fusion.57
  734.3 9.5 add_convert_fusion
  743.9 8.3 fusion.48
  753.5 4.1 fusion.157
  759.5 297.8 %reduce_gradients.1 = (f32[2,28,3584]{2,1,0:T(8,128)}, f32[2,28,3584]{2,1,0:T(8,128)}, f32[2,28,2688]{2,1,0:T(8,128)}, f32[2,28,896]{2,1,0:T(8,128)}, f32[2,28,3...) custom-call(bf16[128,896]{1,0:T(8,128)(2,1)} %copy-done.81, ...), custom_call_target="tpu_custom_call" | custom-call | tf_op jit(solution)/shard_map/reduce_gradients/pallas_call | solution.py:680
  (443 shorter events, 132.6 us)
Async XLA Ops:
  7.2 10.7 copy-start.88
  7.2 415.4 %all-gather.3.cloned.1.call-start = ((), (), s32[]{:S(2)}) async-start(), calls=%async_computation.2 | async-start | bytes 4128768 | tf_op jit(solution)/shard_map/all_gather | solution.py:798
  8.0 408.1 %collective-permute-start = (bf16[1,2]{1,0:T(2,128)(2,1)S(1)}, bf16[1,2]{1,0:T(2,128)(2,1)S(1)}, u32[]{:S(2)}, u32[]{:S(2)}) collective-permute-start(bf16[1,2]{1,0:T(2,128)(2,1)S(1)} %get-tuple-element.148), channel_id=1, source_target_pairs={{0,1},{1,2},{2,3},{3,4},{4,5},{5,6},{6,7},{8,9},{9,10},{10,11},{11... | collective-permute-start | bytes 20 | tf_op jit(solution)/shard_map/ppermute | solution.py:720
  11.5 326.8 %copy-start.108 = (f32[128]{0:T(128)}, f32[128]{0:T(128)S(1)}, u32[]{:S(2)}) copy-start(f32[128]{0:T(128)S(1)} %fusion.187) | copy-start | bytes 1540
  17.9 320.4 %copy-start.46 = (bf16[1,128,896]{2,1,0:T(8,128)(2,1)S(1)}, bf16[1,128,896]{2,1,0:T(8,128)(2,1)}, u32[]{:S(2)}) copy-start(bf16[1,128,896]{2,1,0:T(8,128)(2,1)} %param.18) | copy-start | bytes 688132
  343.3 157.9 %all-gather.5.cloned.1.call-start = ((), (), s32[]{:S(2)}) async-start(), calls=%async_computation.3 | async-start | bytes 4128768 | tf_op jit(solution)/shard_map/all_gather | solution.py:798
  343.9 31.9 %copy-start.96 = (f32[896]{0:T(1024)}, f32[896]{0:T(1024)S(1)}, u32[]{:S(2)}) copy-start(f32[896]{0:T(1024)S(1)} %get-tuple-element.118) | copy-start | bytes 10756
  343.9 63.9 %copy-start.92 = (f32[896]{0:T(1024)}, f32[896]{0:T(1024)S(1)}, u32[]{:S(2)}) copy-start(f32[896]{0:T(1024)S(1)} %get-tuple-element.117) | copy-start | bytes 10756
  344.2 9.8 copy-start.106
  344.2 27.4 %slice-start.16 = ((s8[6422528]{0:T(1024)(128)(4,1)}), s8[4194304]{0:T(1024)(128)(4,1)S(1)}, s32[]{:S(2)}) async-start(s8[6422528]{0:T(1024)(128)(4,1)} %bitcast.469), calls=%async_computation.22 | async-start | bytes 8388608
  344.5 27.1 %slice-start.17 = ((s8[6422528]{0:T(1024)(128)(4,1)}), s8[2228224]{0:T(1024)(128)(4,1)S(1)}, s32[]{:S(2)}) async-start(s8[6422528]{0:T(1024)(128)(4,1)} %bitcast.469), calls=%async_computation.23 | async-start | bytes 4456448
  354.0 17.6 %copy-start.27 = (f32[2,2,128,3584]{3,2,1,0:T(8,128)}, f32[2,2,128,3584]{3,2,1,0:T(8,128)S(1)}, u32[]{:S(2)}) copy-start(f32[2,2,128,3584]{3,2,1,0:T(8,128)S(1)} %get-tuple-element.152) | copy-start | bytes 22020100
  375.7 10.0 copy-start.102
  375.8 27.9 %copy-start.31 = (f32[1,2,2,128,896]{4,3,2,1,0:T(8,128)}, f32[1,2,2,128,896]{4,3,2,1,0:T(8,128)S(1)}, u32[]{:S(2)}) copy-start(f32[1,2,2,128,896]{4,3,2,1,0:T(8,128)S(1)} %get-tuple-element.154) | copy-start | bytes 5505028
  375.8 10.0 copy-start.100
  375.8 27.8 %slice-start.18 = ((s8[6422528]{0:T(1024)(128)(4,1)}), s8[4194304]{0:T(1024)(128)(4,1)S(1)}, s32[]{:S(2)}) async-start(s8[6422528]{0:T(1024)(128)(4,1)} %bitcast.475), calls=%async_computation.24 | async-start | bytes 8388608
  376.0 9.8 copy-start.49
  376.0 27.6 %slice-start.19 = ((s8[6422528]{0:T(1024)(128)(4,1)}), s8[2228224]{0:T(1024)(128)(4,1)S(1)}, s32[]{:S(2)}) async-start(s8[6422528]{0:T(1024)(128)(4,1)} %bitcast.475), calls=%async_computation.25 | async-start | bytes 4456448
  385.8 17.8 %copy-start.28 = (f32[2,2,128,3584]{3,2,1,0:T(8,128)}, f32[2,2,128,3584]{3,2,1,0:T(8,128)S(1)}, u32[]{:S(2)}) copy-start(f32[2,2,128,3584]{3,2,1,0:T(8,128)S(1)} %get-tuple-element.155) | copy-start | bytes 22020100
  409.2 7.3 collective-permute-start.1
  412.5 21.6 %copy-start.53 = (bf16[1,128,896]{1,2,0:T(8,128)(2,1)}, bf16[1,128,896]{1,2,0:T(8,128)(2,1)S(1)}, u32[]{:S(2)}) copy-start(bf16[1,128,896]{1,2,0:T(8,128)(2,1)S(1)} %copy.146) | copy-start | bytes 688132
  421.3 24.4 %copy-start.18 = (bf16[1,2,256,896]{2,3,1,0:T(8,128)(2,1)}, bf16[1,2,256,896]{2,3,1,0:T(8,128)(2,1)S(1)}, u32[]{:S(2)}) copy-start(bf16[1,2,256,896]{2,3,1,0:T(8,128)(2,1)S(1)} %copy.150) | copy-start | bytes 2752516
  448.6 10.4 copy-start.51
  448.6 10.4 slice-start.10
  460.3 59.6 %copy-start.29 = (f32[1,128,896]{2,1,0:T(8,128)}, f32[1,128,896]{2,1,0:T(8,128)S(1)}, u32[]{:S(2)}) copy-start(f32[1,128,896]{2,1,0:T(8,128)S(1)} %get-tuple-element.166) | copy-start | bytes 1376260
  464.7 153.6 %reduce-scatter.3.cloned.1.call-start = ((), (), s32[]{:S(2)}) async-start(), calls=%async_computation.4 | async-start | bytes 4128768 | tf_op jit(solution)/shard_map/reduce_scatter | solution.py:848
  464.9 47.7 %copy-start.55 = (bf16[1,128,896]{1,2,0:T(8,128)(2,1)}, bf16[1,128,896]{1,2,0:T(8,128)(2,1)S(1)}, u32[]{:S(2)}) copy-start(bf16[1,128,896]{1,2,0:T(8,128)(2,1)S(1)} %copy.154) | copy-start | bytes 688132
  517.9 9.8 slice-start.12
  522.0 13.3 %copy-start.11 = (f32[1,128,896]{2,1,0:T(8,128)}, f32[1,128,896]{2,1,0:T(8,128)S(1)}, u32[]{:S(2)}) copy-start(f32[1,128,896]{2,1,0:T(8,128)S(1)} %get-tuple-element.170) | copy-start | bytes 1376260
  535.3 11.2 %slice-start.2 = ((s8[7340032]{0:T(1024)(128)(4,1)}), s8[3145728]{0:T(1024)(128)(4,1)S(1)}, s32[]{:S(2)}) async-start(s8[7340032]{0:T(1024)(128)(4,1)} %bitcast.370), calls=%async_computation.8 | async-start | bytes 6291456
  569.5 184.1 %reduce-scatter.5.cloned.1.call-start = ((), (), s32[]{:S(2)}) async-start(), calls=%async_computation.5 | async-start | bytes 4128768 | tf_op jit(solution)/shard_map/reduce_scatter | solution.py:848
  579.0 39.4 %copy-start.71 = (bf16[128,896]{1,0:T(8,128)(2,1)}, bf16[128,896]{1,0:T(8,128)(2,1)S(1)}, u32[]{:S(2)}) copy-start(bf16[128,896]{1,0:T(8,128)(2,1)S(1)} %copy.160) | copy-start | bytes 688132
  579.0 39.3 %copy-start.30 = (f32[1,128,896]{2,1,0:T(8,128)S(1)}, f32[1,128,896]{2,1,0:T(8,128)}, u32[]{:S(2)}) copy-start(f32[1,128,896]{2,1,0:T(8,128)} %copy-done.29) | copy-start | bytes 1376260
  618.3 11.2 %slice-start.8 = ((s8[6422528]{0:T(1024)(128)(4,1)}), s8[4194304]{0:T(1024)(128)(4,1)S(1)}, s32[]{:S(2)}) async-start(s8[6422528]{0:T(1024)(128)(4,1)} %bitcast.394), calls=%async_computation.14 | async-start | bytes 8388608
  652.3 11.4 %slice-start = ((s8[7340032]{0:T(1024)(128)(4,1)}), s8[3145728]{0:T(1024)(128)(4,1)S(1)}, s32[]{:S(2)}) async-start(s8[7340032]{0:T(1024)(128)(4,1)} %bitcast.368), calls=%async_computation.6 | async-start | bytes 6291456
  680.8 24.3 %collective-permute-start.2 = (bf16[1,2,128,896]{3,2,1,0:T(8,128)(2,1)}, bf16[1,2,128,896]{3,2,1,0:T(8,128)(2,1)}, u32[]{:S(2)}, u32[]{:S(2)}) collective-permute-start(bf16[1,2,128,896]{3,2,1,0:T(8,128)(2,1)} %fusion.165), channel_id=1, source_target_pairs={{1,0},{2,1},{3,2},{4,3},{5,4},{6,5},{7,6},{9,8},{10,9},{11,10},{12... | collective-permute-start | bytes 1376264 | tf_op jit(solution)/shard_map/ppermute | solution.py:720
  706.2 28.0 %slice-start.4 = ((s8[7340032]{0:T(1024)(128)(4,1)}), s8[4194304]{0:T(1024)(128)(4,1)S(1)}, s32[]{:S(2)}) async-start(s8[7340032]{0:T(1024)(128)(4,1)} %bitcast.387), calls=%async_computation.10 | async-start | bytes 8388608
  706.2 28.0 %slice-start.6 = ((s8[7340032]{0:T(1024)(128)(4,1)}), s8[4194304]{0:T(1024)(128)(4,1)S(1)}, s32[]{:S(2)}) async-start(s8[7340032]{0:T(1024)(128)(4,1)} %bitcast.389), calls=%async_computation.12 | async-start | bytes 8388608
  708.2 14.9 %copy-start.32 = (f32[1,2,2,128,896]{4,3,2,1,0:T(8,128)S(1)}, f32[1,2,2,128,896]{4,3,2,1,0:T(8,128)}, u32[]{:S(2)}) copy-start(f32[1,2,2,128,896]{4,3,2,1,0:T(8,128)} %copy-done.31) | copy-start | bytes 5505028
  708.2 14.9 %copy-start.97 = (f32[896]{0:T(1024)S(1)}, f32[896]{0:T(1024)}, u32[]{:S(2)}) copy-start(f32[896]{0:T(1024)} %copy-done.96) | copy-start | bytes 10756
  708.2 14.9 %copy-start.101 = (f32[2,2,128]{2,1,0:T(2,128)S(1)}, f32[2,2,128]{2,1,0:T(2,128)}, u32[]{:S(2)}) copy-start(f32[2,2,128]{2,1,0:T(2,128)} %copy-done.100) | copy-start | bytes 6148
  708.2 26.0 %slice-start.5 = ((s8[7340032]{0:T(1024)(128)(4,1)}), s8[3145728]{0:T(1024)(128)(4,1)S(1)}, s32[]{:S(2)}) async-start(s8[7340032]{0:T(1024)(128)(4,1)} %bitcast.387), calls=%async_computation.11 | async-start | bytes 6291456
  708.2 26.0 %slice-start.7 = ((s8[7340032]{0:T(1024)(128)(4,1)}), s8[3145728]{0:T(1024)(128)(4,1)S(1)}, s32[]{:S(2)}) async-start(s8[7340032]{0:T(1024)(128)(4,1)} %bitcast.389), calls=%async_computation.13 | async-start | bytes 6291456
  734.3 9.6 copy-start.45
  743.8 9.7 copy-start.47
  743.9 9.7 copy-start.99
  743.9 9.7 copy-start.109
  759.5 299.5 %copy-start.111 = (f32[128]{0:T(128)S(1)}, f32[128]{0:T(128)}, u32[]{:S(2)}) copy-start(f32[128]{0:T(128)} %copy-done.110) | copy-start | bytes 1540
  (93 other events, 346.6 us)
Sparse Core Ops, SparseCore 0:
  343.4 33.2 all-gather.2
  464.8 36.3 all-gather.4
  569.5 48.7 reduce-scatter.2
  703.2 50.2 reduce-scatter.4

commit v3 on v2

--- a/solution.py
+++ b/solution.py
@@ -8,6 +8,16 @@
 
 D = 896
 FF = 3584
+HEADS = 14
+HEAD = 64
+SPAN = 64
+NEIGH = 2
+RET = 128
+ENC_LAYERS = 2
+DEC_LAYERS = 2
+EPSILON = 1e-06
+SCORE_SCALE = 0.125
+MASKED_SCORE = -1000000000.0
 BF = jnp.bfloat16
 MESH_ID = pl.DeviceIdType.MESH
 ANY = pl.BlockSpec(memory_space=pl.ANY)
@@ -700,18 +710,225 @@
     )(*operands, gains.reshape(lead + (128,)))
 
 
-HEADS = 14
-HEAD = 64
-SPAN = 64
-NEIGH = 2
-RET = 128
-ENC_LAYERS = 2
-DEC_LAYERS = 2
-
-
-EPSILON = 1e-06
-SCORE_SCALE = 0.125
-MASKED_SCORE = -1000000000.0
+NN = (((1,), (0,)), ((), ()))
+NT = (((1,), (1,)), ((), ()))
+TN = (((0,), (0,)), ((), ()))
+
+
+def dot(left, right, dims):
+    return lax.dot_general(left, right, dims, preferred_element_type=jnp.float32)
+
+
+def head_sides(values):
+    lane = lax.broadcasted_iota(jnp.int32, values.shape, 1)
+    zero = jnp.zeros_like(values)
+    return [jnp.where(lane < HEAD, values, zero), jnp.where(lane >= HEAD, values, zero)]
+
+
+def attend_kernel(q_ref, k_ref, v_ref, bias_ref, out_ref, total_ref):
+    keys, vals = k_ref[...], v_ref[...]
+    outs = []
+    for side, queries in enumerate(head_sides(q_ref[...])):
+        scores = dot(keys, queries, NT) * SCORE_SCALE + bias_ref[...]
+        peak = jnp.max(scores, 0, keepdims=True)
+        powers = jnp.exp(scores - peak)
+        total = jnp.sum(powers, 0, keepdims=True)
+        total_ref[0, side : side + 1, :] = peak + jnp.log(total)
+        probs = (powers * (1.0 / total)).astype(BF)
+        outs.append(dot(probs, vals, TN))
+    lane = lax.broadcasted_iota(jnp.int32, outs[0].shape, 1)
+    out_ref[...] = jnp.where(lane < HEAD, outs[0], outs[1]).astype(BF)
+
+
+def attend(joined, keys_vals, bias):
+    queries, keys = joined.shape[0], keys_vals.shape[0]
+    pairs = D // 128
+    return pl.pallas_call(
+        attend_kernel,
+        grid=(pairs,),
+        out_shape=[jax.ShapeDtypeStruct((queries, D), BF), jax.ShapeDtypeStruct((pairs, 2, queries), jnp.float32)],
+        in_specs=[
+            pl.BlockSpec((queries, 128), lambda p: (0, p)),
+            pl.BlockSpec((keys, 128), lambda p: (0, p)),
+            pl.BlockSpec((keys, 128), lambda p: (0, pairs + p)),
+            pl.BlockSpec((keys, queries), lambda p: (0, 0)),
+        ],
+        out_specs=[pl.BlockSpec((queries, 128), lambda p: (0, p)), pl.BlockSpec((1, 2, queries), lambda p: (p, 0, 0))],
+        cost_estimate=pl.CostEstimate(
+            flops=4 * queries * keys * D * 2, bytes_accessed=2 * keys * 2 * D, transcendentals=14 * queries * keys
+        ),
+        name="attend",
+    )(joined, keys_vals, keys_vals, bias)
+
+
+def attend_back_kernel(q_ref, k_ref, v_ref, bias_ref, total_ref, grad_ref, gq_ref, gkv_ref):
+    pair = pl.program_id(0)
+    keys, vals = k_ref[...], v_ref[...]
+    q_sides, g_sides = head_sides(q_ref[...]), head_sides(grad_ref[...])
+    grad_q, grad_k, grad_v = [], 0.0, 0.0
+    for side in range(2):
+        scores = dot(keys, q_sides[side], NT) * SCORE_SCALE + bias_ref[...]
+        probs = jnp.exp(scores - total_ref[0, side : side + 1, :])
+        grad_probs = dot(vals, g_sides[side], NT)
+        delta = jnp.sum(probs * grad_probs, 0, keepdims=True)
+        grad_scores = (probs * (grad_probs - delta)).astype(BF)
+        grad_v = grad_v + dot(probs.astype(BF), g_sides[side], NN)
+        grad_k = grad_k + dot(grad_scores, q_sides[side], NN)
+        grad_q.append(dot(grad_scores, keys, TN))
+    lane = lax.broadcasted_iota(jnp.int32, grad_q[0].shape, 1)
+    gq_ref[...] = (jnp.where(lane < HEAD, grad_q[0], grad_q[1]) * SCORE_SCALE).astype(BF)
+    gkv_ref[:, pl.ds(pl.multiple_of(pair * 128, 128), 128)] = (grad_k * SCORE_SCALE).astype(BF)
+    gkv_ref[:, pl.ds(pl.multiple_of(D + pair * 128, 128), 128)] = grad_v.astype(BF)
+
+
+def attend_back(joined, keys_vals, bias, log_total, grad_mixed):
+    queries, keys = joined.shape[0], keys_vals.shape[0]
+    pairs = D // 128
+    return pl.pallas_call(
+        attend_back_kernel,
+        grid=(pairs,),
+        out_shape=[jax.ShapeDtypeStruct((queries, D), BF), jax.ShapeDtypeStruct((keys, 2 * D), BF)],
+        in_specs=[
+            pl.BlockSpec((queries, 128), lambda p: (0, p)),
+            pl.BlockSpec((keys, 128), lambda p: (0, p)),
+            pl.BlockSpec((keys, 128), lambda p: (0, pairs + p)),
+            pl.BlockSpec((keys, queries), lambda p: (0, 0)),
+            pl.BlockSpec((1, 2, queries), lambda p: (p, 0, 0)),
+            pl.BlockSpec((queries, 128), lambda p: (0, p)),
+        ],
+        out_specs=[pl.BlockSpec((queries, 128), lambda p: (0, p)), pl.BlockSpec((keys, 2 * D), lambda p: (0, 0))],
+        cost_estimate=pl.CostEstimate(
+            flops=10 * queries * keys * D * 2, bytes_accessed=4 * keys * 2 * D, transcendentals=14 * queries * keys
+        ),
+        name="attend_back",
+    )(joined, keys_vals, keys_vals, bias, log_total, grad_mixed)
+
+
+def gelu_parts(values):
+    size = jnp.abs(values)
+    bell = jnp.exp(-0.5 * size * size)
+    t = 1.0 / (1.0 + (0.3275911 * 0.7071067811865476) * size)
+    tail = t * (0.127414796 + t * (-0.142248368 + t * (0.7107068705 + t * (-0.7265760135 + t * 0.5307027145)))) * bell
+    share = jnp.where(values >= 0, 1.0 - tail, tail)
+    return values * share, share + values * (0.3989422804014327 * bell)
+
+
+def norm_parts(values):
+    scale = lax.rsqrt(jnp.mean(values * values, -1, keepdims=True) + EPSILON)
+    return values * scale, scale
+
+
+def norm_gradient(values, norm_gain, upstream):
+    unit, scale = norm_parts(values)
+    inner = upstream * norm_gain
+    back = scale * (inner - unit * jnp.mean(inner * unit, -1, keepdims=True))
+    return back, jnp.sum(upstream * unit, 0, keepdims=True)
+
+
+def hidden_block(rows):
+    return 2 * D if rows <= 128 else D
+
+
+def ffn_kernel(stream_ref, gain_ref, in_ref, down_ref, out_ref, inputs_ref, hidden_ref, slope_ref):
+    step = pl.program_id(0)
+
+    @pl.when(step == 0)
+    def _():
+        stream = stream_ref[...].astype(jnp.float32)
+        out_ref[...] = stream
+        inputs_ref[...] = (norm_parts(stream)[0] * gain_ref[...].astype(jnp.float32)).astype(BF)
+
+    value, slope = gelu_parts(dot(inputs_ref[...], in_ref[...], NN))
+    hidden = value.astype(BF)
+    hidden_ref[...] = hidden
+    slope_ref[...] = slope.astype(BF)
+    out_ref[...] += dot(hidden, down_ref[...], NN)
+
+
+def ffn(stream, norm_gain, weight_in, weight_down):
+    rows = stream.shape[0]
+    block = hidden_block(rows)
+    still = lambda j: (0, 0)
+    return pl.pallas_call(
+        ffn_kernel,
+        grid=(FF // block,),
+        out_shape=[
+            jax.ShapeDtypeStruct((rows, D), jnp.float32),
+            jax.ShapeDtypeStruct((rows, D), BF),
+            jax.ShapeDtypeStruct((rows, FF), BF),
+            jax.ShapeDtypeStruct((rows, FF), BF),
+        ],
+        in_specs=[
+            pl.BlockSpec((rows, D), still),
+            pl.BlockSpec((1, D), still),
+            pl.BlockSpec((D, block), lambda j: (0, j)),
+            pl.BlockSpec((block, D), lambda j: (j, 0)),
+        ],
+        out_specs=[
+            pl.BlockSpec((rows, D), still),
+            pl.BlockSpec((rows, D), still),
+            pl.BlockSpec((rows, block), lambda j: (0, j)),
+            pl.BlockSpec((rows, block), lambda j: (0, j)),
+        ],
+        cost_estimate=pl.CostEstimate(
+            flops=4 * rows * D * FF, bytes_accessed=4 * D * FF + 4 * rows * FF + 8 * rows * D, transcendentals=rows * FF
+        ),
+        name="ffn",
+    )(stream, norm_gain, weight_in, weight_down)
+
+
+def ffn_back_kernel(grad_ref, stream_ref, gain_ref, slope_ref, in_ref, down_ref, out_ref, low_ref, pre_ref, gain_out, total):
+    step = pl.program_id(0)
+
+    @pl.when(step == 0)
+    def _():
+        low_ref[...] = grad_ref[...].astype(BF)
+        total[...] = jnp.zeros_like(total)
+
+    pre = (dot(low_ref[...], down_ref[...], NT) * slope_ref[...].astype(jnp.float32)).astype(BF)
+    pre_ref[...] = pre
+    total[...] += dot(pre, in_ref[...], NT)
+
+    @pl.when(step == pl.num_programs(0) - 1)
+    def _():
+        back, gain = norm_gradient(stream_ref[...].astype(jnp.float32), gain_ref[...].astype(jnp.float32), total[...])
+        out_ref[...] = grad_ref[...].astype(jnp.float32) + back
+        gain_out[...] = gain
+
+
+def ffn_back(upstream, stream, norm_gain, slope, weight_in, weight_down):
+    rows = stream.shape[0]
+    block = hidden_block(rows)
+    still = lambda j: (0, 0)
+    return pl.pallas_call(
+        ffn_back_kernel,
+        grid=(FF // block,),
+        out_shape=[
+            jax.ShapeDtypeStruct((rows, D), jnp.float32),
+            jax.ShapeDtypeStruct((rows, D), BF),
+            jax.ShapeDtypeStruct((rows, FF), BF),
+            jax.ShapeDtypeStruct((1, D), jnp.float32),
+        ],
+        in_specs=[
+            pl.BlockSpec((rows, D), still),
+            pl.BlockSpec((rows, D), still),
+            pl.BlockSpec((1, D), still),
+            pl.BlockSpec((rows, block), lambda j: (0, j)),
+            pl.BlockSpec((D, block), lambda j: (0, j)),
+            pl.BlockSpec((block, D), lambda j: (j, 0)),
+        ],
+        out_specs=[
+            pl.BlockSpec((rows, D), still),
+            pl.BlockSpec((rows, D), still),
+            pl.BlockSpec((rows, block), lambda j: (0, j)),
+            pl.BlockSpec((1, D), still),
+        ],
+        scratch_shapes=[pltpu.VMEM((rows, D), jnp.float32)],
+        cost_estimate=pl.CostEstimate(
+            flops=4 * rows * D * FF, bytes_accessed=4 * D * FF + 4 * rows * FF + 16 * rows * D, transcendentals=0
+        ),
+        name="ffn_back",
+    )(upstream, stream, norm_gain, slope, weight_in, weight_down)
 
 
 def shifted(x, axis, by):
@@ -720,253 +937,86 @@
     return lax.ppermute(x, axis, pairs)
 
 
+def slab_term(left, right):
+    return dot(left, right, TN)
+
+
 def normed(values, norm_gain):
-    return values * lax.rsqrt(jnp.mean(values * values, -1, keepdims=True) + EPSILON) * norm_gain
-
-
-def gelu_exact(values):
-    return jax.nn.gelu(values, approximate=False)
-
-
-def project(values, weight):
-    return jnp.dot(values, weight, preferred_element_type=jnp.float32)
-
-
-def back_project(upstream, weight):
-    return lax.dot_general(
-        upstream,
-        weight,
-        (((upstream.ndim - 1,), (1,)), ((), ())),
-        preferred_element_type=jnp.float32,
-    )
-
-
-def slab_term(left, right):
-    flat_left = left.reshape(-1, left.shape[-1])
-    flat_right = right.reshape(-1, right.shape[-1])
-    return lax.dot_general(
-        flat_left, flat_right, (((0,), (0,)), ((), ())), preferred_element_type=jnp.float32
-    )
-
-
-def norm_back(stream, norm_gain, upstream):
-    _, pullback = jax.vjp(normed, stream, norm_gain)
-    return pullback(upstream)
-
-
-def split_heads(values):
-    return values.reshape(values.shape[:-1] + (HEADS, HEAD))
-
-
-def softmax_parts(scores):
-    row_peak = jnp.max(scores, -1, keepdims=True)
-    powers = jnp.exp(scores - row_peak)
-    row_total = jnp.sum(powers, -1, keepdims=True)
-    return (powers / row_total, (row_peak + jnp.log(row_total))[..., 0])
-
-
-def feed_forward(stream, norm_gain, weight_in, weight_down):
-    inputs = normed(stream, norm_gain).astype(jnp.bfloat16)
-    hidden_pre = project(inputs, weight_in)
-    hidden = gelu_exact(hidden_pre).astype(jnp.bfloat16)
-    return (stream + project(hidden, weight_down), (stream, inputs, hidden_pre, hidden))
-
-
-def feed_back(stored, norm_gain, weight_in, weight_down, upstream):
-    stream, inputs, hidden_pre, hidden = stored
-    grad_low = upstream.astype(jnp.bfloat16)
-    grad_hidden = back_project(grad_low, weight_down)
-    _, gelu_pull = jax.vjp(gelu_exact, hidden_pre)
-    grad_pre = gelu_pull(grad_hidden)[0].astype(jnp.bfloat16)
-    stream_grad, gain_grad = norm_back(stream, norm_gain, back_project(grad_pre, weight_in))
-    return (upstream + stream_grad, gain_grad, ((inputs, grad_pre), (grad_low, hidden)))
-
-
-def score_table(queries, keys_all, offset):
-    raw_scores = (
-        jnp.einsum("bqhd,bkhd->bhqk", queries, keys_all, preferred_element_type=jnp.float32)
-        * SCORE_SCALE
-    )
-    key_place = jnp.arange(keys_all.shape[1])
-    query_place = offset + jnp.arange(queries.shape[1])
-    return jnp.where(key_place[None, :] <= query_place[:, None], raw_scores, MASKED_SCORE)
-
-
-def self_forward(stream, norm_gain, weight_qkv, weight_out, offset):
-    inputs = normed(stream, norm_gain).astype(jnp.bfloat16)
-    joined = project(inputs, weight_qkv).astype(jnp.bfloat16)
-    keys_vals = lax.all_gather(joined[..., D:], "seq", axis=1, tiled=True)
-    queries = split_heads(joined[..., :D])
-    scores = score_table(queries, split_heads(keys_vals[..., :D]), offset)
-    attn_probs, log_total = softmax_parts(scores)
-    attn_mixed = jnp.einsum(
-        "bhqk,bkhd->bqhd",
-        attn_probs.astype(jnp.bfloat16),
-        split_heads(keys_vals[..., D:]),
-        preferred_element_type=jnp.float32,
-    )
-    attn_mixed = attn_mixed.astype(jnp.bfloat16).reshape(stream.shape)
-    return (
-        stream + project(attn_mixed, weight_out),
-        (stream, inputs, joined, keys_vals, log_total, attn_mixed),
-    )
-
-
-def self_back(stored, norm_gain, weight_qkv, weight_out, offset, upstream):
-    stream, inputs, joined, keys_vals, log_total, attn_mixed = stored
-    grad_low = upstream.astype(jnp.bfloat16)
-    grad_mixed = split_heads(back_project(grad_low, weight_out).astype(jnp.bfloat16))
-    queries = split_heads(joined[..., :D])
-    keys_all = split_heads(keys_vals[..., :D])
-    vals_all = split_heads(keys_vals[..., D:])
-    scores = score_table(queries, keys_all, offset)
-    attn_probs = jnp.exp(scores - log_total[..., None])
-    grad_probs = jnp.einsum(
-        "bqhd,bkhd->bhqk", grad_mixed, vals_all, preferred_element_type=jnp.float32
-    )
-    row_delta = jnp.sum(attn_probs * grad_probs, -1)
-    grad_scores = (attn_probs * (grad_probs - row_delta[..., None])).astype(jnp.bfloat16)
-    grad_queries = (
-        jnp.einsum("bhqk,bkhd->bqhd", grad_scores, keys_all, preferred_element_type=jnp.float32)
-        * SCORE_SCALE
-    )
-    seqs_here = queries.shape[0]
-    grad_vals = jnp.einsum(
-        "bhqk,bqhd->bkhd",
-        attn_probs.astype(jnp.bfloat16),
-        grad_mixed,
-        preferred_element_type=jnp.float32,
-    )
-    grad_keys = (
-        jnp.einsum("bhqk,bqhd->bkhd", grad_scores, queries, preferred_element_type=jnp.float32)
-        * SCORE_SCALE
-    )
-    length = grad_keys.shape[1]
-    grad_pairs = jnp.concatenate(
-        [grad_keys.reshape(seqs_here, length, D), grad_vals.reshape(seqs_here, length, D)], -1
-    )
-    own_pairs = lax.psum_scatter(
-        grad_pairs.astype(jnp.bfloat16), "seq", scatter_dimension=1, tiled=True
-    ).astype(jnp.float32)
-    grad_joined = jnp.concatenate([grad_queries.reshape(stream.shape), own_pairs], -1).astype(
-        jnp.bfloat16
-    )
-    stream_grad, gain_grad = norm_back(stream, norm_gain, back_project(grad_joined, weight_qkv))
-    return (upstream + stream_grad, gain_grad, ((inputs, grad_joined), (attn_mixed, grad_low)))
-
-
-def cross_scores(queries, keys_vals, prior_flag):
-    raw_scores = (
-        jnp.einsum(
-            "bcqhd,bckhd->bchqk",
-            queries,
-            split_heads(keys_vals[..., :D]),
-            preferred_element_type=jnp.float32,
-        )
-        * SCORE_SCALE
-    )
-    allowed = jnp.repeat(prior_flag, RET, axis=2) > 0.5
-    return jnp.where(allowed[:, :, None, None, :], raw_scores, MASKED_SCORE)
+    return (norm_parts(values)[0] * norm_gain.astype(jnp.float32)).astype(BF)
+
+
+def norm_back(values, norm_gain, upstream):
+    return norm_gradient(values, norm_gain.astype(jnp.float32), upstream)
+
+
+def self_forward(stream, norm_gain, weight_qkv, weight_out, bias):
+    inputs = normed(stream, norm_gain)
+    joined = dot(inputs, weight_qkv, NN).astype(BF)
+    keys_vals = lax.all_gather(joined[:, D:], "seq", axis=0, tiled=True)
+    mixed, log_total = attend(joined, keys_vals, bias)
+    return stream + dot(mixed, weight_out, NN), (stream, inputs, joined, keys_vals, log_total, mixed)
+
+
+def self_back(stored, norm_gain, weight_qkv, weight_out, bias, upstream):
+    stream, inputs, joined, keys_vals, log_total, mixed = stored
+    grad_low = upstream.astype(BF)
+    grad_mixed = dot(grad_low, weight_out, NT).astype(BF)
+    grad_queries, grad_pairs = attend_back(joined, keys_vals, bias, log_total, grad_mixed)
+    own_pairs = lax.psum_scatter(grad_pairs, "seq", scatter_dimension=0, tiled=True)
+    grad_joined = jnp.concatenate([grad_queries, own_pairs], -1)
+    back, gain_grad = norm_back(stream, norm_gain, dot(grad_joined, weight_qkv, NT))
+    return upstream + back, gain_grad, ((inputs, grad_joined), (mixed, grad_low))
+
+
+def causal_bias(queries, keys):
+    offset = lax.axis_index("seq") * queries
+    key_place = lax.broadcasted_iota(jnp.int32, (keys, queries), 0)
+    query_place = offset + lax.broadcasted_iota(jnp.int32, (keys, queries), 1)
+    return jnp.where(key_place <= query_place, 0.0, MASKED_SCORE).astype(jnp.float32)
+
+
+def span_bias(prior_flag, queries):
+    spans = prior_flag.shape[0]
+    keys = spans * NEIGH * RET
+    key_span = lax.broadcasted_iota(jnp.int32, (keys, queries), 0) // (NEIGH * RET)
+    query_span = lax.broadcasted_iota(jnp.int32, (keys, queries), 1) // SPAN
+    allowed = jnp.repeat(prior_flag.reshape(-1), RET)[:, None] > 0.5
+    return jnp.where(key_span == query_span, jnp.where(allowed, 0.0, MASKED_SCORE), 2 * MASKED_SCORE).astype(jnp.float32)
 
 
 def row_gate(prior_flag):
-    return jnp.repeat(jnp.max(prior_flag, -1).astype(jnp.float32), SPAN, axis=1)[..., None]
+    return jnp.repeat(jnp.max(prior_flag, -1).astype(jnp.float32), SPAN)[:, None]
+
+
+def prior_spans(encoded, keep_flag):
+    last_enc, last_flag = shifted((encoded[-1:], keep_flag[-1:]), "seq", 1)
+    return jnp.concatenate([last_enc, encoded[:-1]], 0), jnp.concatenate([last_flag, keep_flag[:-1]], 0)
 
 
 def cross_forward(stream, encoded, keep_flag, norm_gain, weight_q, weight_kv, weight_out):
-    seqs_here = stream.shape[0]
-    spans_here = encoded.shape[1]
-    last_enc, last_flag = shifted((encoded[:, -1], keep_flag[:, -1]), "seq", 1)
-    prior_enc = jnp.concatenate([last_enc[:, None], encoded[:, :-1]], 1)
-    prior_flag = jnp.concatenate([last_flag[:, None], keep_flag[:, :-1]], 1)
-    inputs = normed(stream, norm_gain).astype(jnp.bfloat16)
-    queries = (
-        project(inputs, weight_q)
-        .astype(jnp.bfloat16)
-        .reshape(seqs_here, spans_here, SPAN, HEADS, HEAD)
-    )
-    keys_vals = (
-        project(prior_enc, weight_kv)
-        .astype(jnp.bfloat16)
-        .reshape(seqs_here, spans_here, NEIGH * RET, 2 * D)
-    )
-    scores = cross_scores(queries, keys_vals, prior_flag)
-    attn_probs, log_total = softmax_parts(scores)
-    attn_mixed = jnp.einsum(
-        "bchqk,bckhd->bcqhd",
-        attn_probs.astype(jnp.bfloat16),
-        split_heads(keys_vals[..., D:]),
-        preferred_element_type=jnp.float32,
-    )
-    attn_mixed = attn_mixed.astype(jnp.bfloat16).reshape(stream.shape)
-    branch = row_gate(prior_flag) * project(attn_mixed, weight_out)
-    return (
-        stream + branch,
-        (stream, inputs, prior_enc, prior_flag, queries, keys_vals, log_total, attn_mixed),
-    )
+    prior_enc, prior_flag = prior_spans(encoded, keep_flag)
+    prior_enc = prior_enc.reshape(-1, D)
+    inputs = normed(stream, norm_gain)
+    queries = dot(inputs, weight_q, NN).astype(BF)
+    keys_vals = jnp.concatenate([dot(prior_enc, side, NN).astype(BF) for side in weight_kv], 1)
+    bias = span_bias(prior_flag, stream.shape[0])
+    mixed, log_total = attend(queries, keys_vals, bias)
+    branch = row_gate(prior_flag) * dot(mixed, weight_out, NN)
+    return stream + branch, (stream, inputs, prior_enc, prior_flag, queries, keys_vals, bias, log_total, mixed)
 
 
 def cross_back(stored, norm_gain, weight_q, weight_kv, weight_out, upstream):
-    stream, inputs, prior_enc, prior_flag, queries, keys_vals, log_total, attn_mixed = stored
-    grad_low = (upstream * row_gate(prior_flag)).astype(jnp.bfloat16)
-    grad_mixed = back_project(grad_low, weight_out).astype(jnp.bfloat16).reshape(queries.shape)
-    scores = cross_scores(queries, keys_vals, prior_flag)
-    attn_probs = jnp.exp(scores - log_total[..., None])
-    keys_part = split_heads(keys_vals[..., :D])
-    vals_part = split_heads(keys_vals[..., D:])
-    grad_vals = jnp.einsum(
-        "bchqk,bcqhd->bckhd",
-        attn_probs.astype(jnp.bfloat16),
-        grad_mixed,
-        preferred_element_type=jnp.float32,
-    )
-    grad_probs = jnp.einsum(
-        "bcqhd,bckhd->bchqk", grad_mixed, vals_part, preferred_element_type=jnp.float32
-    )
-    grad_scores = attn_probs * (grad_probs - jnp.sum(attn_probs * grad_probs, -1, keepdims=True))
-    grad_scores = grad_scores.astype(jnp.bfloat16)
-    grad_queries = (
-        jnp.einsum("bchqk,bckhd->bcqhd", grad_scores, keys_part, preferred_element_type=jnp.float32)
-        * SCORE_SCALE
-    )
-    grad_keys = (
-        jnp.einsum("bchqk,bcqhd->bckhd", grad_scores, queries, preferred_element_type=jnp.float32)
-        * SCORE_SCALE
-    )
-    pair_shape = keys_vals.shape[:-1] + (D,)
-    grad_pairs = jnp.concatenate([grad_keys.reshape(pair_shape), grad_vals.reshape(pair_shape)], -1)
-    grad_pairs = grad_pairs.astype(jnp.bfloat16)
-    grad_prior = back_project(grad_pairs, weight_kv).reshape(prior_enc.shape)
-    query_low = grad_queries.reshape(stream.shape).astype(jnp.bfloat16)
-    stream_grad, gain_grad = norm_back(stream, norm_gain, back_project(query_low, weight_q))
-    from_next = shifted(grad_prior[:, 0].astype(jnp.bfloat16), "seq", -1).astype(jnp.float32)
-    encoded_grad = jnp.concatenate([grad_prior[:, 1:], from_next[:, None]], 1)
-    pairs = ((inputs, query_low), (prior_enc, grad_pairs), (attn_mixed, grad_low))
-    return (upstream + stream_grad, gain_grad, pairs, encoded_grad)
-
-
-def encode(retrieved, enc_gain, enc_in, enc_down, enc_final):
-    stream = retrieved.astype(jnp.float32)
-    stored = []
-    for layer_idx in range(ENC_LAYERS):
-        stream, layer_store = feed_forward(
-            stream, enc_gain[layer_idx], enc_in[layer_idx], enc_down[layer_idx]
-        )
-        stored.append(layer_store)
-    return (normed(stream, enc_final).astype(jnp.bfloat16), (stream, stored))
-
-
-def encode_back(retrieved, enc_weights, encoded_grad):
-    enc_gain, enc_in, enc_down, enc_final = enc_weights
-    _, (stream, stored) = encode(retrieved, enc_gain, enc_in, enc_down, enc_final)
-    upstream, final_grad = norm_back(stream, enc_final, encoded_grad)
-    gain_list = [None] * ENC_LAYERS
-    pair_list = [None] * ENC_LAYERS
-    for layer_idx in reversed(range(ENC_LAYERS)):
-        upstream, gain_list[layer_idx], pair_list[layer_idx] = feed_back(
-            stored[layer_idx], enc_gain[layer_idx], enc_in[layer_idx], enc_down[layer_idx], upstream
-        )
-    return (gain_list, pair_list, final_grad)
+    stream, inputs, prior_enc, prior_flag, queries, keys_vals, bias, log_total, mixed = stored
+    grad_low = (upstream * row_gate(prior_flag)).astype(BF)
+    grad_mixed = dot(grad_low, weight_out, NT).astype(BF)
+    grad_queries, grad_pairs = attend_back(queries, keys_vals, bias, log_total, grad_mixed)
+    grad_prior = dot(grad_pairs[:, :D], weight_kv[0], NT) + dot(grad_pairs[:, D:], weight_kv[1], NT)
+    grad_prior = grad_prior.reshape(prior_flag.shape[0], NEIGH * RET, D)
+    from_next = shifted(grad_prior[:1].astype(BF), "seq", -1).astype(jnp.float32)
+    encoded_grad = jnp.concatenate([grad_prior[1:], from_next], 0).reshape(-1, D)
+    back, gain_grad = norm_back(stream, norm_gain, dot(grad_queries, weight_q, NT))
+    pairs = ((inputs, grad_queries), (prior_enc, grad_pairs), (mixed, grad_low))
+    return upstream + back, gain_grad, pairs, encoded_grad
 
 
 def on_device(
@@ -989,89 +1039,80 @@
     enc_down,
     enc_final,
 ):
-    offset = lax.axis_index("seq") * tokens.shape[1]
+    assert tokens.shape[0] == 1
     rows = cca_q.shape[0]
     own_gains = jnp.concatenate([dec_gain.reshape(4, rows), cca_gain[None], enc_gain, enc_final[None]], 0).T
     own_gains = jnp.pad(own_gains, ((0, 0), (0, 120)))
     full = gather_weights(enc_in, enc_down, dec_qkv, dec_out, dec_in, dec_down, cca_q, cca_kv, cca_out, own_gains)
     gains = full["gains"].T
-    enc_weights = (gains[5:7], full["enc_in"], full["enc_down"], gains[7])
-    encoded, _ = encode(retrieved, enc_weights[0], enc_weights[1], enc_weights[2], enc_weights[3])
-    keep_flag = (neigh_doc != span_doc[..., None]).astype(jnp.bfloat16)
-    dec_weights = (
-        gains[:4].reshape(2, 2, D), full["dec_qkv"], full["dec_out"], full["dec_in"], full["dec_down"],
-        gains[4], full["cca_q"], jnp.concatenate(full["cca_kv"], 1), full["cca_out"],
-    )
-    norm_gains, qkv_all, out_all, in_all, down_all, cross_gain, cross_q, cross_kv, cross_out = (
-        dec_weights
-    )
-    stream = tokens.astype(jnp.float32)
-    attn_stores, ffn_stores = ([], [])
-    stream, attn_store = self_forward(stream, norm_gains[0, 0], qkv_all[0], out_all[0], offset)
-    attn_stores.append(attn_store)
-    stream, cross_store = cross_forward(
-        stream, encoded, keep_flag, cross_gain, cross_q, cross_kv, cross_out
-    )
-    stream, ffn_store = feed_forward(stream, norm_gains[0, 1], in_all[0], down_all[0])
-    ffn_stores.append(ffn_store)
-    layer_idx = 1
-    stream, attn_store = self_forward(
-        stream, norm_gains[layer_idx, 0], qkv_all[layer_idx], out_all[layer_idx], offset
-    )
-    attn_stores.append(attn_store)
-    stream, ffn_store = feed_forward(
-        stream, norm_gains[layer_idx, 1], in_all[layer_idx], down_all[layer_idx]
-    )
-    ffn_stores.append(ffn_store)
-    result = stream.astype(jnp.bfloat16)
-    upstream = cotangent.astype(jnp.float32)
-    attn_gain_g = [None] * DEC_LAYERS
-    ffn_gain_g = [None] * DEC_LAYERS
-    attn_pairs = [None] * DEC_LAYERS
-    ffn_pairs = [None] * DEC_LAYERS
-    for layer_idx in reversed(range(1, DEC_LAYERS)):
-        upstream, ffn_gain_g[layer_idx], ffn_pairs[layer_idx] = feed_back(
-            ffn_stores[layer_idx],
-            norm_gains[layer_idx, 1],
-            in_all[layer_idx],
-            down_all[layer_idx],
-            upstream,
+    attn_gain, ffn_gain = (gains[0:1], gains[2:3]), (gains[1:2], gains[3:4])
+    cross_gain, encode_gain, final_gain = gains[4:5], (gains[5:6], gains[6:7]), gains[7:8]
+    cross_weights = (cross_gain, full["cca_q"], full["cca_kv"], full["cca_out"])
+    queries = tokens.shape[1]
+    bias = causal_bias(queries, queries * lax.axis_size("seq"))
+
+    encoder = retrieved.reshape(-1, D)
+    encoder_kept = []
+    for layer in range(ENC_LAYERS):
+        after, inputs, hidden, slope = ffn(encoder, encode_gain[layer], full["enc_in"][layer], full["enc_down"][layer])
+        encoder_kept.append((encoder, inputs, hidden, slope))
+        encoder = after
+    encoded = normed(encoder, final_gain).reshape(span_doc.shape[1], NEIGH * RET, D)
+    keep_flag = (neigh_doc[0] != span_doc[0][:, None]).astype(BF)
+
+    stream = tokens[0].astype(jnp.float32)
+    attn_kept, ffn_kept = [], []
+    for layer in range(DEC_LAYERS):
+        stream, kept = self_forward(stream, attn_gain[layer], full["dec_qkv"][layer], full["dec_out"][layer], bias)
+        attn_kept.append(kept)
+        if layer == 0:
+            stream, cross_kept = cross_forward(stream, encoded, keep_flag, *cross_weights)
+        before = stream
+        stream, inputs, hidden, slope = ffn(before, ffn_gain[layer], full["dec_in"][layer], full["dec_down"][layer])
+        ffn_kept.append((before, inputs, hidden, slope))
+    result = stream.astype(BF)
+
+    upstream = cotangent[0].astype(jnp.float32)
+    attn_gain_g, ffn_gain_g = [None] * DEC_LAYERS, [None] * DEC_LAYERS
+    attn_pairs, ffn_pairs = [None] * DEC_LAYERS, [None] * DEC_LAYERS
+    for layer in reversed(range(DEC_LAYERS)):
+        before, inputs, hidden, slope = ffn_kept[layer]
+        upstream, grad_low, grad_pre, ffn_gain_g[layer] = ffn_back(
+            upstream, before, ffn_gain[layer], slope, full["dec_in"][layer], full["dec_down"][layer]
         )
-        upstream, attn_gain_g[layer_idx], attn_pairs[layer_idx] = self_back(
-            attn_stores[layer_idx],
-            norm_gains[layer_idx, 0],
-            qkv_all[layer_idx],
-            out_all[layer_idx],
-            offset,
-            upstream,
+        ffn_pairs[layer] = ((inputs, grad_pre), (grad_low, hidden))
+        if layer == 0:
+            upstream, cross_gain_g, cross_pairs, encoded_grad = cross_back(cross_kept, *cross_weights, upstream)
+        upstream, attn_gain_g[layer], attn_pairs[layer] = self_back(
+            attn_kept[layer], attn_gain[layer], full["dec_qkv"][layer], full["dec_out"][layer], bias, upstream
         )
-    upstream, ffn_gain_g[0], ffn_pairs[0] = feed_back(
-        ffn_stores[0], norm_gains[0, 1], in_all[0], down_all[0], upstream
-    )
-    upstream, cross_gain_g, cross_pairs, encoded_grad = cross_back(
-        cross_store, cross_gain, cross_q, cross_kv, cross_out, upstream
-    )
-    upstream, attn_gain_g[0], attn_pairs[0] = self_back(
-        attn_stores[0], norm_gains[0, 0], qkv_all[0], out_all[0], offset, upstream
-    )
-    enc_gain_g, enc_pairs, final_gain_g = encode_back(retrieved, enc_weights, encoded_grad)
+
+    enc_upstream, final_gain_g = norm_back(encoder, final_gain, encoded_grad)
+    enc_gain_g, enc_pairs = [None] * ENC_LAYERS, [None] * ENC_LAYERS
+    for layer in reversed(range(ENC_LAYERS)):
+        before, inputs, hidden, slope = encoder_kept[layer]
+        enc_upstream, grad_low, grad_pre, enc_gain_g[layer] = ffn_back(
+            enc_upstream, before, encode_gain[layer], slope, full["enc_in"][layer], full["enc_down"][layer]
+        )
+        enc_pairs[layer] = ((inputs, grad_pre), (grad_low, hidden))
+
     pair_list = []
-    for layer_idx in range(DEC_LAYERS):
-        pair_list = pair_list + list(attn_pairs[layer_idx]) + list(ffn_pairs[layer_idx])
-    pair_list = pair_list + list(cross_pairs)
-    for layer_idx in range(ENC_LAYERS):
-        pair_list = pair_list + list(enc_pairs[layer_idx])
+    for layer in range(DEC_LAYERS):
+        pair_list += list(attn_pairs[layer]) + list(ffn_pairs[layer])
+    pair_list += list(cross_pairs)
+    for layer in range(ENC_LAYERS):
+        pair_list += list(enc_pairs[layer])
     gain_list = []
-    for layer_idx in range(DEC_LAYERS):
-        gain_list = gain_list + [attn_gain_g[layer_idx], ffn_gain_g[layer_idx]]
-    gain_list = gain_list + [cross_gain_g] + list(enc_gain_g) + [final_gain_g]
+    for layer in range(DEC_LAYERS):
+        gain_list += [attn_gain_g[layer], ffn_gain_g[layer]]
+    gain_list = [gain.reshape(D) for gain in gain_list + [cross_gain_g] + enc_gain_g + [final_gain_g]]
 
     grads = sum_gradients(pair_list, gain_list, rows)
     (enc_in_g, enc_down_g, dec_qkv_g, dec_out_g, dec_in_g, dec_down_g, cross_q_g, cross_kv_g, cross_out_g, gain_cols) = grads
     gain_rows = gain_cols[:, :8].T
     return (
-        result,
-        upstream,
+        result[None],
+        upstream[None],
         gain_rows[:4].reshape(2, 2, rows),
         dec_qkv_g,
         dec_out_g,

time: 1090 us -> 999 us (0.917)
  Pallas kernels: 616 us -> 783 us
  matrix products: 183 us -> 48 us
  local copies, waits for them, and re-layouts: 111 us -> 31 us
  other arithmetic: 74.7 us -> 17.3 us
  waiting for transfers between devices: 71.7 us -> 87.8 us
    pallas_call x0 -> x14, Pallas kernels: none -> 166 us  [the longest x4 51.9 us: ffn_back(): pl.pallas_call(ffn_back_kernel, grid=(FF // block,), out_shape=[jax.Shape...]
    dot_general x48 -> x16, matrix products: 183 us -> 48 us  [dot(): lax.dot_general(left, right, dims, preferred_element_type=jnp.float32)]
    convert_element_type x12 -> x10, other arithmetic: 49.1 us -> 4.87 us  [the longest x4 1.6 us: normed(): return (norm_parts(values)[0] * norm_gain.astype(jnp.float32)).astype(BF)]
    concatenate x14 -> x2, local copies, waits for them, and re-layouts: 31.7 us -> 2.86 us  [self_back(): grad_joined = jnp.concatenate([grad_queries, own_pairs], -1)]
    slice x18 -> x7, local copies, waits for them, and re-layouts: 32.1 us -> 3.4 us  [the longest x2 1.68 us: self_forward(): keys_vals = lax.all_gather(joined[:, D:], 'seq', axis=0, tiled=True)]
    reduce_scatter x2, waiting for transfers between devices: 35.4 us -> 50.4 us  [self_back(): lax.psum_scatter(grad_pairs, 'seq', scatter_dimension=0, tiled=True)]
    concatenate x7 -> x3, other arithmetic: 14.8 us -> 1.66 us  [the longest x1 1.44 us: cross_forward(): jnp.concatenate([dot(prior_enc, side, NN).astype(BF) for side in weight_k...]
    unnamed x285 -> x96, local copies, waits for them, and re-layouts: 32.1 us -> 20.7 us
  transfers between devices with their start and end apart: 7 -> 7, of which waited for: 3 -> 4; matrix products, arithmetic and copies ran while one was open for 16% -> 2% of each run, Pallas kernels for 29% -> 7%
where the time goes in v3:
time: 999 us; the launch traced here: 990 us
  Pallas kernels  783 us (78%)
  waiting for transfers between devices  87.8 us (9%)
  matrix products  48 us (5%)
  local copies, waits for them, and re-layouts  31 us (3%)
  other arithmetic  17.3 us (2%)
  between operations  14.7 us (1%)
    pallas_call x1, Pallas kernels, gather_weights(): pl.pallas_call(functools.partial(gather_kernel, sizes), out_shape=[jax.Sh...  317 us
    pallas_call x1, Pallas kernels, reduce_gradients(): pl.pallas_call(functools.partial(reduce_kernel, sizes, tall), out_shape=[...  299 us
    pallas_call x4, Pallas kernels, ffn_back(): pl.pallas_call(ffn_back_kernel, grid=(FF // block,), out_shape=[jax.Shape...  51.9 us
    reduce_scatter x2, waiting for transfers between devices, self_back(): lax.psum_scatter(grad_pairs, 'seq', scatter_dimension=0, tiled=True)  50.4 us
    dot_general x16, matrix products, dot(): lax.dot_general(left, right, dims, preferred_element_type=jnp.float32)  48 us
    pallas_call x4, Pallas kernels, ffn(): pl.pallas_call(ffn_kernel, grid=(FF // block,), out_shape=[jax.ShapeDtype...  47.8 us
    all_gather x2, waiting for transfers between devices, self_forward(): keys_vals = lax.all_gather(joined[:, D:], 'seq', axis=0, tiled=True)  35.9 us
    pallas_call x3, Pallas kernels, attend_back(): pl.pallas_call(attend_back_kernel, grid=(pairs,), out_shape=[jax.ShapeDty...  34.1 us
  transfers between devices with their start and end apart: 7, of which 4 were waited for; matrix products, arithmetic and copies ran while one was open for 2% of the time, Pallas kernels for 7%

profile of v3, /device:TPU:0, one launch (start us, length us, event | category | flops | bytes accessed | tf_op | source)
XLA Modules:
  0.0 989.5 jit_solution(17480951087008407544)
XLA Ops:
  7.3 1.9 copy.70.refs_0_
  9.2 1.7 copy.71.refs_2_
  10.9 1.6 copy.72.refs_3_
  14.0 317.5 %gather_weights.1 = (bf16[4,2,2,56,3584]{4,3,2,1,0:T(8,128)(2,1)}, bf16[4,2,2,56,3584]{4,3,2,1,0:T(8,128)(2,1)}, bf16[4,2,2,56,11008]{4,3,2,1,0:T(8,128)(2,1)}, ...) custom-call(bf16[2,28,3584]{2,1,0:T(8,128)(2,1)} %copy.70.refs_0_, ...), custom_call_target="tpu_custom_call" | custom-call | tf_op jit(solution)/shard_map/gather_weights/pallas_call | solution.py:285
  332.9 3.4 fusion.8.q_ref
  337.8 16.4 %ffn.4 = (f32[512,896]{1,0:T(8,128)}, bf16[512,896]{1,0:T(8,128)(2,1)}, bf16[512,3584]{1,0:T(8,128)(2,1)}, bf16[512,3584]{1,0:T(8,128)(2,1)}) custom-call(bf16[512,896]{1,0:T(8,128)(2,1)} %bitcast.128, bf16[1,896]{1,0:T(2,128)(2,1)} %get-tuple-element.204.gain_ref, bf16[896,3584]{1,0:T(8,128)(2,1)} %bitcast.120, bf16[3584,896]{1,0:T(8,128)(2,1)} %bitcast.122), custom_call_target="tpu_custom_call" | custom-call | flops 6576668672 | bytes 23855104 | tf_op jit(solution)/shard_map/ffn/pallas_call | solution.py:852
  354.3 16.8 %ffn.5 = (f32[512,896]{1,0:T(8,128)}, bf16[512,896]{1,0:T(8,128)(2,1)}, bf16[512,3584]{1,0:T(8,128)(2,1)}, bf16[512,3584]{1,0:T(8,128)(2,1)}) custom-call(f32[512,896]{1,0:T(8,128)} %get-tuple-element.81.stream_ref, bf16[1,896]{1,0:T(2,128)(2,1)} %get-tuple-element.203.gain_ref, bf16[896,3584]{1,0:T(8,128)(2,1)} %bitcast.124, bf16[3584,896]{1,0:T(8,128)(2,1)} %bitcast.126), custom_call_target="tpu_custom_call" | custom-call | flops 6576668672 | bytes 23855104 | tf_op jit(solution)/shard_map/ffn/pallas_call | solution.py:852
  371.1 1.8 multiply_reduce_fusion.1
  373.5 2.3 collective-permute-start.1
  375.9 3.3 collective-permute-start
  381.7 3.0 convolution_convert_fusion
  384.6 2.6 convolution_convert_fusion.1
  388.7 11.8 %attend.3 = (bf16[128,896]{1,0:T(8,128)(2,1)}, f32[7,2,128]{2,1,0:T(2,128)}) custom-call(bf16[128,2688]{1,0:T(8,128)(2,1)} %copy-done.2, bf16[1024,1792]{1,0:T(8,128)(2,1)} %all-gather.3.cloned.1.call-done.k_ref.v_ref, bf16[1024,1792]{1,0:T(8,128)(2,1)} %all-gather.3.cloned.1.call-done.k_ref.v_ref, f32[1024,128]{1,0:T(8,128)} %fusion.66.bias_ref), custom_call_target="tpu_custom_call" | custom-call | flops 939524096 | bytes 3670016 | tf_op jit(solution)/shard_map/attend/pallas_call | solution.py:746
  400.5 2.1 multiply_reduce_fusion.7
  402.7 2.6 fusion.51.q_ref
  405.3 8.7 attend.4
  414.1 2.8 fusion.42.stream_ref
  416.9 7.3 ffn.6
  426.4 3.4 fusion.11.q_ref
  431.9 35.9 %all-gather.5.cloned.1.call-done.k_ref.v_ref = bf16[1024,1792]{1,0:T(8,128)(2,1)} async-done(((bf16[128,1792]{1,0:T(8,128)(2,1)}), bf16[1024,1792]{1,0:T(8,128)(2,1)}) %all-gather.5.cloned.1.call-update) | async-done | bytes 3670032 | tf_op jit(solution)/shard_map/all_gather | solution.py:955
  467.8 11.8 %attend.5 = (bf16[128,896]{1,0:T(8,128)(2,1)}, f32[7,2,128]{2,1,0:T(2,128)}) custom-call(bf16[128,2688]{1,0:T(8,128)(2,1)} %copy-done.3, bf16[1024,1792]{1,0:T(8,128)(2,1)} %all-gather.5.cloned.1.call-done.k_ref.v_ref, bf16[1024,1792]{1,0:T(8,128)(2,1)} %all-gather.5.cloned.1.call-done.k_ref.v_ref, f32[1024,128]{1,0:T(8,128)} %fusion.66.bias_ref), custom_call_target="tpu_custom_call" | custom-call | flops 939524096 | bytes 3670016 | tf_op jit(solution)/shard_map/attend/pallas_call | solution.py:746
  479.6 2.8 fusion.45.stream_ref
  482.3 7.3 ffn.7
  489.6 9.4 ffn_back.4
  500.0 2.8 fusion.57.grad_ref
  502.8 12.5 %attend_back.3 = (bf16[128,896]{1,0:T(8,128)(2,1)}, bf16[1024,1792]{1,0:T(8,128)(2,1)}) custom-call(bf16[128,2688]{1,0:T(8,128)(2,1)} %copy-done.3, bf16[1024,1792]{1,0:T(8,128)(2,1)} %all-gather.5.cloned.1.call-done.k_ref.v_ref, bf16[1024,1792]{1,0:T(8,128)(2,1)} %all-gather.5.cloned.1.call-done.k_ref.v_ref, f32[1024,128]{1,0:T(8,128)} %fusion.66.bias_ref, ...), custom_call_target="tpu_custom_call" | custom-call | flops 2348810240 | bytes 7340032 | tf_op jit(solution)/shard_map/attend_back/pallas_call | solution.py:787
  516.9 47.3 %reduce-scatter.3.cloned.1.call-done = bf16[128,1792]{1,0:T(8,128)(2,1)} async-done(((bf16[1024,1792]{1,0:T(8,128)(2,1)}), bf16[128,1792]{1,0:T(8,128)(2,1)}) %reduce-scatter.3.cloned.1.call-update) | async-done | bytes 458768 | tf_op jit(solution)/shard_map/reduce_scatter | solution.py:965
  564.2 1.8 constant_dynamic-update-slice_fusion.refs_9_
  566.0 4.2 multiply_reduce_fusion.3
  571.1 9.3 ffn_back.5
  581.5 2.8 fusion.54.grad_ref
  584.3 9.2 attend_back.4
  593.5 2.3 multiply_reduce_fusion.2
  596.0 2.8 fusion.48.grad_ref
  598.8 12.4 %attend_back.5 = (bf16[128,896]{1,0:T(8,128)(2,1)}, bf16[1024,1792]{1,0:T(8,128)(2,1)}) custom-call(bf16[128,2688]{1,0:T(8,128)(2,1)} %copy-done.2, bf16[1024,1792]{1,0:T(8,128)(2,1)} %all-gather.3.cloned.1.call-done.k_ref.v_ref, bf16[1024,1792]{1,0:T(8,128)(2,1)} %all-gather.3.cloned.1.call-done.k_ref.v_ref, f32[1024,128]{1,0:T(8,128)} %fusion.66.bias_ref, ...), custom_call_target="tpu_custom_call" | custom-call | flops 2348810240 | bytes 7340032 | tf_op jit(solution)/shard_map/attend_back/pallas_call | solution.py:787
  611.3 3.0 fusion.25
  614.4 2.7 convolution_add_fusion
  621.7 1.6 subtract_multiply_fusion.grad_ref
  623.4 17.1 %ffn_back.6 = (f32[512,896]{1,0:T(8,128)}, bf16[512,896]{1,0:T(8,128)(2,1)}, bf16[512,3584]{1,0:T(8,128)(2,1)}, f32[1,896]{1,0:T(1,128)}) custom-call(f32[512,896]{1,0:T(8,128)} %subtract_multiply_fusion.grad_ref, f32[512,896]{1,0:T(8,128)} %get-tuple-element.81.stream_ref, bf16[1,896]{1,0:T(2,128)(2,1)} %get-tuple-element.203.gain_ref, ...), custom_call_target="tpu_custom_call" | custom-call | flops 6576668672 | bytes 27525120 | tf_op jit(solution)/shard_map/ffn_back/pallas_call | solution.py:903
  640.5 16.2 %ffn_back.7 = (f32[512,896]{1,0:T(8,128)}, bf16[512,896]{1,0:T(8,128)(2,1)}, bf16[512,3584]{1,0:T(8,128)(2,1)}, f32[1,896]{1,0:T(1,128)}) custom-call(f32[512,896]{1,0:T(8,128)} %get-tuple-element.116.grad_ref, bf16[512,896]{1,0:T(8,128)(2,1)} %bitcast.129, bf16[1,896]{1,0:T(2,128)(2,1)} %get-tuple-element.204.gain_ref, ...), custom_call_target="tpu_custom_call" | custom-call | flops 6576668672 | bytes 27525120 | tf_op jit(solution)/shard_map/ffn_back/pallas_call | solution.py:903
  657.4 3.1 reduce-scatter.5.cloned.1.call-done
  661.6 4.8 fusion.73
  667.4 299.2 %reduce_gradients.1 = (f32[2,28,3584]{2,1,0:T(8,128)}, f32[2,28,3584]{2,1,0:T(8,128)}, f32[2,28,2688]{2,1,0:T(8,128)}, f32[2,28,896]{2,1,0:T(8,128)}, f32[2,28,3...) custom-call(bf16[128,896]{1,0:T(8,128)(2,1)} %copy-done.16, ...), custom_call_target="tpu_custom_call" | custom-call | tf_op jit(solution)/shard_map/reduce_gradients/pallas_call | solution.py:690
  968.9 2.5 copy.77
  971.4 1.8 copy.78
  973.1 1.5 copy.79
  974.7 1.5 copy.80
  978.3 1.5 copy.83
  (168 shorter events, 33.0 us)
Async XLA Ops:
  7.2 5.3 copy-start.23
  7.2 6.1 copy-start.35
  7.2 6.1 copy-start.36
  7.2 6.1 copy-start.37
  7.2 6.1 copy-start.34
  7.2 381.5 %all-gather.3.cloned.1.call-start = ((), (), s32[]{:S(2)}) async-start(), calls=%async_computation.2 | async-start | bytes 4128768 | tf_op jit(solution)/shard_map/all_gather | solution.py:955
  12.5 320.2 %copy-start.6 = (bf16[1,128,896]{2,1,0:T(8,128)(2,1)S(1)}, bf16[1,128,896]{2,1,0:T(8,128)(2,1)}, u32[]{:S(2)}) copy-start(bf16[1,128,896]{2,1,0:T(8,128)(2,1)} %param.18) | copy-start | bytes 688132
  332.9 3.4 copy-start.16
  336.3 17.9 %copy-start.2 = (bf16[128,2688]{1,0:T(8,128)(2,1)}, bf16[128,2688]{1,0:T(8,128)(2,1)S(1)}, u32[]{:S(2)}) copy-start(bf16[128,2688]{1,0:T(8,128)(2,1)S(1)} %fusion.8.q_ref) | copy-start | bytes 2064388
  337.2 130.6 %all-gather.5.cloned.1.call-start = ((), (), s32[]{:S(2)}) async-start(), calls=%async_computation.3 | async-start | bytes 4128768 | tf_op jit(solution)/shard_map/all_gather | solution.py:955
  371.1 2.1 copy-start
  373.2 2.6 copy-start.33
  373.2 2.6 copy-start.38
  373.5 8.1 collective-permute-start.1
  375.9 4.2 collective-permute-start
  381.7 3.0 copy-start.5
  402.7 11.4 %copy-start.17 = (bf16[128,896]{1,0:T(8,128)(2,1)}, bf16[128,896]{1,0:T(8,128)(2,1)S(1)}, u32[]{:S(2)}) copy-start(bf16[128,896]{1,0:T(8,128)(2,1)S(1)} %multiply_convert_fusion.3.refs_16_) | copy-start | bytes 688132
  426.4 3.4 copy-start.18
  426.4 4.6 copy-start.27
  429.9 37.9 %copy-start.3 = (bf16[128,2688]{1,0:T(8,128)(2,1)}, bf16[128,2688]{1,0:T(8,128)(2,1)S(1)}, u32[]{:S(2)}) copy-start(bf16[128,2688]{1,0:T(8,128)(2,1)S(1)} %fusion.11.q_ref) | copy-start | bytes 2064388
  430.7 133.4 %reduce-scatter.3.cloned.1.call-start = ((), (), s32[]{:S(2)}) async-start(), calls=%async_computation.4 | async-start | bytes 4128768 | tf_op jit(solution)/shard_map/reduce_scatter | solution.py:965
  431.9 47.7 %copy-start.1 = (f32[128,896]{1,0:T(8,128)S(1)}, f32[128,896]{1,0:T(8,128)}, u32[]{:S(2)}) copy-start(f32[128,896]{1,0:T(8,128)} %get-tuple-element.88) | copy-start | bytes 1376260
  500.0 15.2 %copy-start.20 = (bf16[128,896]{1,0:T(8,128)(2,1)}, bf16[128,896]{1,0:T(8,128)(2,1)S(1)}, u32[]{:S(2)}) copy-start(bf16[128,896]{1,0:T(8,128)(2,1)S(1)} %convert_element_type.102.refs_11_) | copy-start | bytes 688132
  515.3 0.9 copy-start.26
  515.3 145.2 %reduce-scatter.5.cloned.1.call-start = ((), (), s32[]{:S(2)}) async-start(), calls=%async_computation.5 | async-start | bytes 4128768 | tf_op jit(solution)/shard_map/reduce_scatter | solution.py:965
  566.0 4.2 copy-start.9
  581.5 12.0 %copy-start.19 = (bf16[128,896]{1,0:T(8,128)(2,1)}, bf16[128,896]{1,0:T(8,128)(2,1)S(1)}, u32[]{:S(2)}) copy-start(bf16[128,896]{1,0:T(8,128)(2,1)S(1)} %multiply_convert_fusion.1.refs_21_) | copy-start | bytes 688132
  593.5 2.3 copy-start.8
  596.0 15.2 %copy-start.15 = (bf16[128,896]{1,0:T(8,128)(2,1)}, bf16[128,896]{1,0:T(8,128)(2,1)S(1)}, u32[]{:S(2)}) copy-start(bf16[128,896]{1,0:T(8,128)(2,1)S(1)} %get-tuple-element.198.refs_3_) | copy-start | bytes 688132
  611.3 3.1 copy-start.4
  614.4 4.3 copy-start.21
  614.4 5.0 copy-start.30
  614.4 5.0 copy-start.31
  614.4 5.1 copy-start.25
  617.2 3.7 collective-permute-start.2
  640.4 16.9 %copy-start.32 = (f32[1,896]{1,0:T(1,128)S(1)}, f32[1,896]{1,0:T(1,128)}, u32[]{:S(2)}) copy-start(f32[1,896]{1,0:T(1,128)} %get-tuple-element.128) | copy-start | bytes 10756
  640.5 21.1 %copy-start.7 = (bf16[1,128,896]{2,1,0:T(8,128)(2,1)S(1)}, bf16[1,128,896]{2,1,0:T(8,128)(2,1)}, u32[]{:S(2)}) copy-start(bf16[1,128,896]{2,1,0:T(8,128)(2,1)} %param.18) | copy-start | bytes 688132
  661.6 4.8 copy-start.10
  966.7 6.5 copy-start.14
  968.9 5.8 copy-start.13
  973.1 3.7 copy-start.12
  974.7 3.7 copy-start.11
  976.2 3.7 copy-start.22
  978.3 2.5 copy-start.29
  978.3 3.1 copy-start.24
  978.3 3.8 copy-start.28
Sparse Core Ops, SparseCore 0:
  337.3 33.5 all-gather.2
  430.9 36.8 all-gather.4
  515.4 48.7 reduce-scatter.2
  611.4 49.0 reduce-scatter.4

commit v4 on v3

--- a/solution.py
+++ b/solution.py
@@ -1,4 +1,5 @@
 import functools
+import heapq
 import jax
 import jax.numpy as jnp
 from jax import lax
@@ -78,8 +79,41 @@
     return jnp.logical_and(place >= 0, place < size)
 
 
-ROUTES = ((2, 0, 1), (1, 0, 2), (0, 2, 1), (1, 0, 2), (2, 0, 1), (0, 1, 2))
-LAGS = (0, 1, 2, 3, 5, 8, 9)
+ZYX, ZXY, YZX, XZY, YXZ, XYZ = (0, 1, 2), (0, 2, 1), (1, 0, 2), (2, 0, 1), (1, 2, 0), (2, 1, 0)
+ROUTES = (ZXY, ZYX, ZXY, ZYX, ZXY, ZYX, ZYX, ZXY, XZY, ZXY, ZXY, YZX)
+ROUTES += (XZY, YZX, XZY, ZYX, ZXY, YZX, ZYX, YZX, XZY, YXZ, YXZ)
+UNIT_US, HOP_US, CORE_US = 2.2, 2.5, 0.17
+
+
+def schedule(pieces, routes, sizes):
+    chains = []
+    for number, piece in enumerate(pieces):
+        scale, held, chain = piece[3] / PIECE, 1, []
+        for axis in routes[number]:
+            chain += [(axis, held * UNIT_US * scale)] * (sizes[axis] - 1)
+            held *= sizes[axis]
+        chains.append(chain + [(3, held * CORE_US * scale)])
+    free, flying, ready = [0.0] * 4, [0] * 4, [[] for _ in range(4)]
+    for number, chain in enumerate(chains):
+        heapq.heappush(ready[chain[0][0]], (number, number, 0))
+    now, events, order = 0.0, [], []
+    while True:
+        for link in range(4):
+            while ready[link] and flying[link] < 2:
+                _, number, step = heapq.heappop(ready[link])
+                free[link] = max(free[link], now) + chains[number][step][1]
+                flying[link] += 1
+                order.append(("start", number, step, now))
+                heapq.heappush(events, (free[link] + HOP_US, number, step, link))
+        if not events:
+            return order
+        now, number, step, link = heapq.heappop(events)
+        flying[link] -= 1
+        order.append(("wait", number, step, now))
+        if step + 1 < len(chains[number]):
+            heapq.heappush(ready[chains[number][step + 1][0]], (number + step + 1, number, step + 1))
+
+
 PIECE = 896
 
 
@@ -91,11 +125,12 @@
         whole(0, 0),
         whole(0, 1),
         [
-            [(7, None, 0, D), (6, None, 0, D), (2, 0, 0, qkv), (3, 0, 0, D), (9, None, 0, 128)],
-            [(7, None, D, D), (8, None, 0, D), (2, 1, 0, qkv), (3, 1, 0, D), (9, None, 0, 128)],
+            [(7, None, 0, D), (6, None, 0, D), (2, 0, 0, qkv), (3, 0, 0, D)],
+            [(7, None, D, D), (8, None, 0, D), (2, 1, 0, qkv), (3, 1, 0, D)],
         ],
         whole(4, 0),
         whole(4, 1),
+        [[(9, None, 0, 128)], [(9, None, 0, 128)]],
     ]
 
 
@@ -110,23 +145,26 @@
         starts.append(cursor)
         cursor += half_width(group)
     pieces = []
-    for kind, number in (("n", 0), ("r", 0), ("n", 1), ("r", 1), ("n", 2), ("n", 3), ("r", 2), ("n", 4), ("r", 3)):
+    for kind, number in (("n", 5), ("n", 0), ("r", 0), ("n", 1), ("r", 1), ("n", 2), ("n", 3), ("r", 2), ("n", 4), ("r", 3)):
         if kind == "n":
             width = half_width(groups[number])
-            count = width // PIECE
-            for k in range(count):
-                size = PIECE if k < count - 1 else width - k * PIECE
-                pieces.append((kind, number, k * PIECE, size))
+            for first in range(0, width, PIECE):
+                pieces.append((kind, number, first, min(PIECE, width - first)))
         else:
             pieces.append((kind, number, 0, D))
             pieces.append((kind, number, 1, D))
     return groups, starts, cursor, pieces
 
 
+N_GROUPS = 6
+
+
 def gather_kernel(sizes, *refs):
     groups, starts, _, pieces = gather_plan()
-    ins, outs = refs[:10], refs[10:19]
-    halves, other, joined, send_sem, recv_sem, load_sem, swap_sem = refs[19:]
+    ins, neighbours = refs[:10], refs[10]
+    outs, encoder_outs = refs[11 : 15 + N_GROUPS], refs[15 + N_GROUPS : 24 + N_GROUPS]
+    halves, other, joined, own_rows, send_sem, recv_sem, load_sem, swap_sem = refs[24 + N_GROUPS : 32 + N_GROUPS]
+    encoder_rooms = refs[32 + N_GROUPS :]
     place = grid_place()
     z, y, x, core = place
     sibling = device_at(moved(place, sizes, 3, 1))
@@ -140,7 +178,7 @@
                 cursor += size
     for number, (arg, layer) in enumerate(((1, 0), (1, 1), (5, 0), (5, 1))):
         for part in range(2):
-            loads.append((ins[arg].at[layer, part], outs[5 + number].at[z, y, x, core, part]))
+            loads.append((ins[arg].at[layer, part], own_rows.at[2 * number + part]))
     started = []
     for k, (source, target) in enumerate(loads):
         copy = pltpu.make_async_copy(source, target, load_sem.at[k])
@@ -149,6 +187,13 @@
     greet(place, sizes)
     for copy in started:
         copy.wait()
+    placed = []
+    for number in range(4):
+        for part in range(2):
+            k = 2 * number + part
+            target = outs[N_GROUPS + number].at[z, y, x, core, part]
+            placed.append(pltpu.make_async_copy(own_rows.at[k], target, load_sem.at[len(loads) + len(groups) + k]))
+            placed[-1].start()
     swaps = []
     for number, group in enumerate(groups):
         columns = pl.ds(starts[number], half_width(group))
@@ -169,7 +214,7 @@
         if kind == "n":
             start = pl.multiple_of(core * half_width(groups[number]) + first, 128)
             return outs[number].at[iz, iy, ix, :, pl.ds(start, size)]
-        return outs[5 + number].at[iz, iy, ix, core, first]
+        return outs[N_GROUPS + number].at[iz, iy, ix, core, first]
 
     prepared = {}
 
@@ -193,13 +238,17 @@
             copy.start()
             copy.wait()
             prepared[number] = True
+        elif kind == "r" and "r" not in prepared:
+            for copy in placed:
+                copy.wait()
+            prepared["r"] = True
 
     semaphores = [0]
 
     def transfers(number):
         piece = pieces[number]
         steps, done = [], []
-        for axis in ROUTES[number % len(ROUTES)] + (3,):
+        for axis in routes[number] + (3,):
             size, here = sizes[axis], place[axis]
 
             def block(at):
@@ -239,77 +288,194 @@
             done.append(axis)
         return steps
 
-    running = {}
-    depth = sum(size - 1 for size in sizes)
-    lags = LAGS if depth + 1 == len(LAGS) else list(range(depth + 1))
-    for tick in range(len(pieces) + lags[-1]):
-        for step in reversed(range(depth + 1)):
-            number = tick - lags[step]
-            if number < 0 or number >= len(pieces):
-                continue
-            if step == 0:
-                prepare(pieces[number])
-                running[number] = transfers(number)
-            else:
-                for copy in running[number][step - 1]:
+    routes = [ROUTES[number % len(ROUTES)] for number in range(len(pieces))]
+    running = [transfers(number) for number in range(len(pieces))]
+    units = encoder_units(
+        neighbours, outs[N_GROUPS - 1], (outs[0], outs[1]), (outs[N_GROUPS], outs[N_GROUPS + 1]), encoder_outs, encoder_rooms
+    )
+    needs = [{k for k, piece in enumerate(pieces) if piece[:2] in wanted} for wanted in UNIT_NEEDS]
+    due, arrived = 0.0, set()
+    for what, number, step, time in schedule(pieces, routes, sizes):
+        if what == "wait":
+            for copy in running[number][step]:
+                copy.wait()
+            if step + 1 == len(running[number]):
+                arrived.add(number)
+        else:
+            prepare(pieces[number])
+            for copy in running[number][step]:
+                copy.start()
+        if units and time >= due and needs[len(needs) - len(units)] <= arrived:
+            units.pop(0)()
+            due = time + UNIT_TIME
+    for unit in units:
+        unit()
+
+
+HIDDEN_UNITS = 4
+UNIT_TIME = 7.0
+GAINS, FIRST, SECOND = {("n", 5)}, {("n", 0), ("r", 0)}, {("n", 1), ("r", 1)}
+UNIT_NEEDS = [GAINS | FIRST] * (1 + HIDDEN_UNITS) + [SECOND] * (1 + HIDDEN_UNITS) + [set()]
+
+
+def encoder_units(neighbours, gain_columns, weights_in, weights_down, outs, rooms):
+    after, inputs_out, hidden_out, slope_out, encoded_out = outs[0:2], outs[2:4], outs[4:6], outs[6:8], outs[8]
+    stream, inputs, columns, gain_rows, block_in, block_down, hidden, slope, sems = rooms
+    block = FF // HIDDEN_UNITS
+
+    def flat(values, rows):
+        return values.astype(jnp.float32).reshape(rows, values.shape[-1])
+
+    def weights(layer, k):
+        slot = k % 2
+        return [
+            pltpu.make_async_copy(weights_in[layer].at[:, :, :, :, pl.ds(k * block, block)], block_in.at[slot], sems.at[0, slot]),
+            pltpu.make_async_copy(weights_down[layer].at[k], block_down.at[slot], sems.at[1, slot]),
+        ]
+
+    def results(layer, k):
+        slot = k % 2
+        place = pl.ds(k * block, block)
+        return [
+            pltpu.make_async_copy(hidden.at[slot], hidden_out[layer].at[:, place], sems.at[2, slot]),
+            pltpu.make_async_copy(slope.at[slot], slope_out[layer].at[:, place], sems.at[3, slot]),
+        ]
+
+    def stream_copy(layer):
+        return pltpu.make_async_copy(stream, after[layer], sems.at[4, layer])
+
+    def inputs_copy(layer):
+        return pltpu.make_async_copy(inputs, (*inputs_out, encoded_out)[layer], sems.at[5, layer % 2])
+
+    def norm_unit(layer):
+        if layer == 0:
+            first = pltpu.make_async_copy(neighbours, inputs, sems.at[6, 0])
+            second = pltpu.make_async_copy(gain_columns.at[:, :, :, :, pl.ds(0, 128)], columns, sems.at[6, 1])
+            first.start()
+            second.start()
+            first.wait()
+            second.wait()
+            gain_rows[...] = flat(columns[...], D).T
+            stream[...] = inputs[...].astype(jnp.float32)
+        else:
+            for k in (HIDDEN_UNITS - 2, HIDDEN_UNITS - 1):
+                for copy in results(layer - 1, k):
                     copy.wait()
-            if step < depth:
-                for copy in running[number][step]:
-                    copy.start()
-    for number in range(len(groups)):
-        if number not in prepared:
-            swaps[number].wait()
-
-
-def gather_plainly(enc_in, enc_down, dec_qkv, dec_out, dec_in, dec_down, cca_q, cca_kv, cca_out, gains):
+            inputs_copy(layer - 1).wait()
+            stream_copy(layer - 1).start()
+        if layer < ENC_LAYERS:
+            for copy in weights(layer, 0):
+                copy.start()
+        gain = gain_rows[5 + layer : 6 + layer, :]
+        inputs[...] = (norm_parts(stream[...])[0] * gain).astype(BF)
+        inputs_copy(layer).start()
+        if layer == ENC_LAYERS:
+            stream_copy(layer - 1).wait()
+            inputs_copy(layer).wait()
+
+    def hidden_unit(layer, k):
+        slot = k % 2
+        if k + 1 < HIDDEN_UNITS:
+            for copy in weights(layer, k + 1):
+                copy.start()
+        for copy in weights(layer, k):
+            copy.wait()
+        if k >= 2:
+            for copy in results(layer, k - 2):
+                copy.wait()
+        value, rate = gelu_parts(dot(inputs[...], flat(block_in[slot], D).astype(BF), NN))
+        hidden[slot] = value.astype(BF)
+        slope[slot] = rate.astype(BF)
+        for copy in results(layer, k):
+            copy.start()
+        if k == 0 and layer > 0:
+            stream_copy(layer - 1).wait()
+        stream[...] += dot(hidden[slot], flat(block_down[slot], block).astype(BF), NN)
+
+    units = []
+    for layer in range(ENC_LAYERS):
+        units.append(functools.partial(norm_unit, layer))
+        for k in range(HIDDEN_UNITS):
+            units.append(functools.partial(hidden_unit, layer, k))
+    units.append(functools.partial(norm_unit, ENC_LAYERS))
+    return units
+
+
+def gather_plainly(neighbours, enc_in, enc_down, dec_qkv, dec_out, dec_in, dec_down, cca_q, cca_kv, cca_out, gains):
     get = lambda w: lax.all_gather(w, ("dp", "seq"), axis=w.ndim - 2, tiled=True)
     kv = get(cca_kv)
+    enc_in, enc_down, columns = get(enc_in), get(enc_down), get(gains)[:, :8]
+    stream, kept = neighbours, []
+    for layer in range(ENC_LAYERS):
+        gain = columns[:, 5 + layer][None]
+        after, inputs, hidden, slope = ffn(stream, gain, enc_in[layer], enc_down[layer])
+        kept.append((stream, inputs, hidden, slope))
+        stream = after
     return dict(
-        enc_in=get(enc_in), enc_down=get(enc_down), dec_in=get(dec_in), dec_down=get(dec_down), dec_qkv=get(dec_qkv),
-        dec_out=get(dec_out), cca_kv=[kv[:, :D], kv[:, D:]], cca_q=get(cca_q), cca_out=get(cca_out), gains=get(gains)[:, :8],
+        encoder=(stream, kept, normed(stream, columns[:, 7][None])),
+        enc_in=enc_in, enc_down=enc_down, dec_in=get(dec_in), dec_down=get(dec_down), dec_qkv=get(dec_qkv),
+        dec_out=get(dec_out), cca_kv=[kv[:, :D], kv[:, D:]], cca_q=get(cca_q), cca_out=get(cca_out), gains=columns,
     )
 
 
-def gather_weights(enc_in, enc_down, dec_qkv, dec_out, dec_in, dec_down, cca_q, cca_kv, cca_out, gains):
+def gather_weights(neighbours, enc_in, enc_down, dec_qkv, dec_out, dec_in, dec_down, cca_q, cca_kv, cca_out, gains):
     sizes = grid_sizes()
     rows = cca_q.shape[0]
     groups, starts, total, pieces = gather_plan()
     part = enc_down.shape[1] // 2
-    if rows % 4 or part % 8 or sizes[1:] != (2, 2, 2):
-        return gather_plainly(enc_in, enc_down, dec_qkv, dec_out, dec_in, dec_down, cca_q, cca_kv, cca_out, gains)
+    if rows % 4 or part % 8 or sizes != (HIDDEN_UNITS, 2, 2, 2):
+        return gather_plainly(neighbours, enc_in, enc_down, dec_qkv, dec_out, dec_in, dec_down, cca_q, cca_kv, cca_out, gains)
     lead = sizes[:3]
     shapes = [lead + (2 * rows, 2 * half_width(group)) for group in groups] + [lead + (2, 2, part, D)] * 4
+    out_shape = [jax.ShapeDtypeStruct(shape, BF) for shape in shapes]
+    count = neighbours.shape[0]
+    block = FF // HIDDEN_UNITS
+    out_shape += [jax.ShapeDtypeStruct((count, D), jnp.float32)] * 2 + [jax.ShapeDtypeStruct((count, D), BF)] * 2
+    out_shape += [jax.ShapeDtypeStruct((count, FF), BF)] * 4 + [jax.ShapeDtypeStruct((count, D), BF)]
     per_piece = sum((size - 1) * (1 if size == 2 else 2) for size in sizes)
-    n_loads = sum(len(half) for group in groups for half in group) + 8 + len(groups)
+    n_loads = sum(len(half) for group in groups for half in group) + 16 + len(groups)
     split = lambda w: w.reshape(w.shape[0], 2, part, D)
     outs = pl.pallas_call(
         functools.partial(gather_kernel, sizes),
-        out_shape=[jax.ShapeDtypeStruct(shape, BF) for shape in shapes],
-        in_specs=[ANY] * 10,
-        out_specs=[ANY] * 9,
+        out_shape=out_shape,
+        in_specs=[ANY] * 11,
+        out_specs=[ANY] * len(out_shape),
         scratch_shapes=[
             pltpu.VMEM((2, rows, total), BF),
             pltpu.VMEM((rows, total), BF),
             pltpu.VMEM((2 * rows, total), BF),
+            pltpu.VMEM((8, part, D), BF),
             pltpu.SemaphoreType.DMA((per_piece * len(pieces),)),
             pltpu.SemaphoreType.DMA((per_piece * len(pieces),)),
             pltpu.SemaphoreType.DMA((n_loads,)),
             pltpu.SemaphoreType.DMA((2, len(groups))),
+            pltpu.VMEM((count, D), jnp.float32),
+            pltpu.VMEM((count, D), BF),
+            pltpu.VMEM(lead + (2 * rows, 128), BF),
+            pltpu.VMEM((128, D), jnp.float32),
+            pltpu.VMEM((2,) + lead + (2 * rows, block), BF),
+            pltpu.VMEM((2,) + sizes[1:3] + (2, 2, part, D), BF),
+            pltpu.VMEM((2, count, block), BF),
+            pltpu.VMEM((2, count, block), BF),
+            pltpu.SemaphoreType.DMA((7, 2)),
         ],
-        compiler_params=pltpu.CompilerParams(collective_id=0, has_side_effects=True),
+        compiler_params=pltpu.CompilerParams(collective_id=0, has_side_effects=True, vmem_limit_bytes=56 << 20),
         name="gather_weights",
-    )(enc_in, split(enc_down), dec_qkv, dec_out, dec_in, split(dec_down), cca_q, cca_kv, cca_out, gains)
-    narrow = [out.reshape(D, out.shape[-1]) for out in outs[:5]]
-    tall = [out.reshape(FF, D) for out in outs[5:]]
+    )(enc_in, split(enc_down), dec_qkv, dec_out, dec_in, split(dec_down), cca_q, cca_kv, cca_out, gains, neighbours)
+    narrow = [out.reshape(D, out.shape[-1]) for out in outs[:N_GROUPS]]
+    tall = [out.reshape(FF, D) for out in outs[N_GROUPS : N_GROUPS + 4]]
+    first, second, inputs_0, inputs_1, hidden_0, hidden_1, slope_0, slope_1, encoded = outs[N_GROUPS + 4 :]
+    kept = [(neighbours, inputs_0, hidden_0, slope_0), (first, inputs_1, hidden_1, slope_1)]
     mixed = narrow[2]
     half = mixed.shape[1] // 2
     sides = [mixed[:, :half], mixed[:, half:]]
     qkv = [side[:, 2 * D : 5 * D] for side in sides]
     out = [side[:, 5 * D : 6 * D] for side in sides]
     return dict(
-        enc_in=narrow[:2], enc_down=tall[:2], dec_in=narrow[3:], dec_down=tall[2:], dec_qkv=qkv, dec_out=out,
+        encoder=(second, kept, encoded),
+        enc_in=narrow[:2], enc_down=tall[:2], dec_in=narrow[3:5], dec_down=tall[2:], dec_qkv=qkv, dec_out=out,
         cca_kv=[side[:, :D] for side in sides], cca_q=sides[0][:, D : 2 * D], cca_out=sides[1][:, D : 2 * D],
-        gains=sides[0][:, 6 * D : 6 * D + 8],
+        gains=narrow[5][:, :8],
     )
 
 
@@ -1043,7 +1209,10 @@
     rows = cca_q.shape[0]
     own_gains = jnp.concatenate([dec_gain.reshape(4, rows), cca_gain[None], enc_gain, enc_final[None]], 0).T
     own_gains = jnp.pad(own_gains, ((0, 0), (0, 120)))
-    full = gather_weights(enc_in, enc_down, dec_qkv, dec_out, dec_in, dec_down, cca_q, cca_kv, cca_out, own_gains)
+    neighbours = retrieved.reshape(-1, D)
+    full = gather_weights(
+        neighbours, enc_in, enc_down, dec_qkv, dec_out, dec_in, dec_down, cca_q, cca_kv, cca_out, own_gains
+    )
     gains = full["gains"].T
     attn_gain, ffn_gain = (gains[0:1], gains[2:3]), (gains[1:2], gains[3:4])
     cross_gain, encode_gain, final_gain = gains[4:5], (gains[5:6], gains[6:7]), gains[7:8]
@@ -1051,13 +1220,8 @@
     queries = tokens.shape[1]
     bias = causal_bias(queries, queries * lax.axis_size("seq"))
 
-    encoder = retrieved.reshape(-1, D)
-    encoder_kept = []
-    for layer in range(ENC_LAYERS):
-        after, inputs, hidden, slope = ffn(encoder, encode_gain[layer], full["enc_in"][layer], full["enc_down"][layer])
-        encoder_kept.append((encoder, inputs, hidden, slope))
-        encoder = after
-    encoded = normed(encoder, final_gain).reshape(span_doc.shape[1], NEIGH * RET, D)
+    encoder, encoder_kept, encoded = full["encoder"]
+    encoded = encoded.reshape(span_doc.shape[1], NEIGH * RET, D)
     keep_flag = (neigh_doc[0] != span_doc[0][:, None]).astype(BF)
 
     stream = tokens[0].astype(jnp.float32)

time: 999 us -> 935 us (0.936)
  Pallas kernels: 783 us -> 708 us
  waiting for transfers between devices: 87.8 us -> 100 us
    pallas_call x1, Pallas kernels: 317 us -> 274 us  [gather_weights(): pl.pallas_call(functools.partial(gather_kernel, sizes), out_shape=out_sha...]
    pallas_call x4 -> x2, Pallas kernels: 47.8 us -> 14.5 us  [ffn(): pl.pallas_call(ffn_kernel, grid=(FF // block,), out_shape=[jax.ShapeDtype...]
    all_gather x2, waiting for transfers between devices: 35.9 us -> 50.2 us  [self_forward(): keys_vals = lax.all_gather(joined[:, D:], 'seq', axis=0, tiled=True)]
    unnamed x96 -> x98, local copies, waits for them, and re-layouts: 20.7 us -> 23.2 us
  transfers between devices with their start and end apart: 7 -> 7, of which waited for: 4 -> 5; matrix products, arithmetic and copies ran while one was open for 2% -> 2% of each run, Pallas kernels for 7% -> 4%
where the time goes in v4:
time: 935 us; the launch traced here: 925 us
  Pallas kernels  708 us (76%)
  waiting for transfers between devices  100 us (11%)
  matrix products  47.1 us (5%)
  local copies, waits for them, and re-layouts  32.7 us (3%)
  other arithmetic  15.5 us (2%)
  between operations  14.7 us (2%)
    pallas_call x1, Pallas kernels, reduce_gradients(): pl.pallas_call(functools.partial(reduce_kernel, sizes, tall), out_shape=[...  302 us
    pallas_call x1, Pallas kernels, gather_weights(): pl.pallas_call(functools.partial(gather_kernel, sizes), out_shape=out_sha...  274 us
    pallas_call x4, Pallas kernels, ffn_back(): pl.pallas_call(ffn_back_kernel, grid=(FF // block,), out_shape=[jax.Shape...  51.7 us
    all_gather x2, waiting for transfers between devices, self_forward(): keys_vals = lax.all_gather(joined[:, D:], 'seq', axis=0, tiled=True)  50.2 us
    reduce_scatter x2, waiting for transfers between devices, self_back(): lax.psum_scatter(grad_pairs, 'seq', scatter_dimension=0, tiled=True)  49.4 us
    dot_general x16, matrix products, dot(): lax.dot_general(left, right, dims, preferred_element_type=jnp.float32)  47.1 us
    pallas_call x3, Pallas kernels, attend_back(): pl.pallas_call(attend_back_kernel, grid=(pairs,), out_shape=[jax.ShapeDty...  34.1 us
    pallas_call x3, Pallas kernels, attend(): pl.pallas_call(attend_kernel, grid=(pairs,), out_shape=[jax.ShapeDtypeStr...  32.3 us
  transfers between devices with their start and end apart: 7, of which 5 were waited for; matrix products, arithmetic and copies ran while one was open for 2% of the time, Pallas kernels for 4%

profile of v4, /device:TPU:0, one launch (start us, length us, event | category | flops | bytes accessed | tf_op | source)
XLA Modules:
  0.0 924.8 jit_solution(1401151847193262288)
XLA Ops:
  7.3 1.9 copy.70.refs_0_
  9.2 1.7 copy.71.refs_2_
  10.9 1.6 copy.72.refs_3_
  14.0 273.9 %gather_weights.1 = (bf16[4,2,2,56,3584]{4,3,2,1,0:T(8,128)(2,1)}, bf16[4,2,2,56,3584]{4,3,2,1,0:T(8,128)(2,1)}, bf16[4,2,2,56,10752]{4,3,2,1,0:T(8,128)(2,1)}, ...) custom-call(bf16[2,28,3584]{2,1,0:T(8,128)(2,1)} %copy.70.refs_0_, ...), custom_call_target="tpu_custom_call" | custom-call | tf_op jit(solution)/shard_map/gather_weights/pallas_call | solution.py:438
  289.4 3.4 fusion.8.q_ref
  294.4 2.3 collective-permute-start.1
  296.9 1.9 collective-permute-start
  301.9 3.0 convolution_convert_fusion
  304.9 2.6 convolution_convert_fusion.1
  308.9 16.6 %all-gather.3.cloned.1.call-done.k_ref.v_ref = bf16[1024,1792]{1,0:T(8,128)(2,1)} async-done(((bf16[128,1792]{1,0:T(8,128)(2,1)}), bf16[1024,1792]{1,0:T(8,128)(2,1)}) %all-gather.3.cloned.1.call-update) | async-done | bytes 3670032 | tf_op jit(solution)/shard_map/all_gather | solution.py:1121
  325.5 11.8 %attend.3 = (bf16[128,896]{1,0:T(8,128)(2,1)}, f32[7,2,128]{2,1,0:T(2,128)}) custom-call(bf16[128,2688]{1,0:T(8,128)(2,1)} %copy-done.2, bf16[1024,1792]{1,0:T(8,128)(2,1)} %all-gather.3.cloned.1.call-done.k_ref.v_ref, bf16[1024,1792]{1,0:T(8,128)(2,1)} %all-gather.3.cloned.1.call-done.k_ref.v_ref, f32[1024,128]{1,0:T(8,128)} %fusion.66.bias_ref), custom_call_target="tpu_custom_call" | custom-call | flops 939524096 | bytes 3670016 | tf_op jit(solution)/shard_map/attend/pallas_call | solution.py:912
  337.3 2.1 multiply_reduce_fusion.7
  339.5 2.6 fusion.51.q_ref
  342.1 8.7 attend.4
  350.9 2.8 fusion.42.stream_ref
  353.7 7.3 ffn.2
  363.2 3.4 fusion.11.q_ref
  368.6 33.6 %all-gather.5.cloned.1.call-done.k_ref.v_ref = bf16[1024,1792]{1,0:T(8,128)(2,1)} async-done(((bf16[128,1792]{1,0:T(8,128)(2,1)}), bf16[1024,1792]{1,0:T(8,128)(2,1)}) %all-gather.5.cloned.1.call-update) | async-done | bytes 3670032 | tf_op jit(solution)/shard_map/all_gather | solution.py:1121
  402.2 11.8 %attend.5 = (bf16[128,896]{1,0:T(8,128)(2,1)}, f32[7,2,128]{2,1,0:T(2,128)}) custom-call(bf16[128,2688]{1,0:T(8,128)(2,1)} %copy-done.3, bf16[1024,1792]{1,0:T(8,128)(2,1)} %all-gather.5.cloned.1.call-done.k_ref.v_ref, bf16[1024,1792]{1,0:T(8,128)(2,1)} %all-gather.5.cloned.1.call-done.k_ref.v_ref, f32[1024,128]{1,0:T(8,128)} %fusion.66.bias_ref), custom_call_target="tpu_custom_call" | custom-call | flops 939524096 | bytes 3670016 | tf_op jit(solution)/shard_map/attend/pallas_call | solution.py:912
  414.0 2.8 fusion.45.stream_ref
  416.7 7.3 ffn.3
  424.0 9.4 %ffn_back.4 = (f32[128,896]{1,0:T(8,128)}, bf16[128,896]{1,0:T(8,128)(2,1)}, bf16[128,3584]{1,0:T(8,128)(2,1)}, f32[1,896]{1,0:T(1,128)}) custom-call(f32[128,896]{1,0:T(8,128)} %bitcast_convert_fusion.grad_ref, f32[128,896]{1,0:T(8,128)} %fusion.45.stream_ref, bf16[1,896]{1,0:T(2,128)(2,1)} %get-tuple-element.207.gain_ref, ...), custom_call_target="tpu_custom_call" | custom-call | flops 1644167168 | bytes 16515072 | tf_op jit(solution)/shard_map/ffn_back/pallas_call | solution.py:1069
  434.4 2.8 fusion.57.grad_ref
  437.2 12.4 %attend_back.3 = (bf16[128,896]{1,0:T(8,128)(2,1)}, bf16[1024,1792]{1,0:T(8,128)(2,1)}) custom-call(bf16[128,2688]{1,0:T(8,128)(2,1)} %copy-done.3, bf16[1024,1792]{1,0:T(8,128)(2,1)} %all-gather.5.cloned.1.call-done.k_ref.v_ref, bf16[1024,1792]{1,0:T(8,128)(2,1)} %all-gather.5.cloned.1.call-done.k_ref.v_ref, f32[1024,128]{1,0:T(8,128)} %fusion.66.bias_ref, ...), custom_call_target="tpu_custom_call" | custom-call | flops 2348810240 | bytes 7340032 | tf_op jit(solution)/shard_map/attend_back/pallas_call | solution.py:953
  450.6 48.0 %reduce-scatter.3.cloned.1.call-done = bf16[128,1792]{1,0:T(8,128)(2,1)} async-done(((bf16[1024,1792]{1,0:T(8,128)(2,1)}), bf16[128,1792]{1,0:T(8,128)(2,1)}) %reduce-scatter.3.cloned.1.call-update) | async-done | bytes 458768 | tf_op jit(solution)/shard_map/reduce_scatter | solution.py:1131
  499.7 4.2 multiply_reduce_fusion.3
  504.8 9.3 %ffn_back.5 = (f32[128,896]{1,0:T(8,128)}, bf16[128,896]{1,0:T(8,128)(2,1)}, bf16[128,3584]{1,0:T(8,128)(2,1)}, f32[1,896]{1,0:T(1,128)}) custom-call(f32[128,896]{1,0:T(8,128)} %multiply_add_fusion.1.grad_ref, f32[128,896]{1,0:T(8,128)} %fusion.42.stream_ref, bf16[1,896]{1,0:T(2,128)(2,1)} %get-tuple-element.208.gain_ref, ...), custom_call_target="tpu_custom_call" | custom-call | flops 1644167168 | bytes 16515072 | tf_op jit(solution)/shard_map/ffn_back/pallas_call | solution.py:1069
  515.2 2.8 fusion.54.grad_ref
  518.0 9.2 attend_back.4
  527.2 2.3 multiply_reduce_fusion.2
  529.7 2.8 fusion.48.grad_ref
  532.5 12.4 %attend_back.5 = (bf16[128,896]{1,0:T(8,128)(2,1)}, bf16[1024,1792]{1,0:T(8,128)(2,1)}) custom-call(bf16[128,2688]{1,0:T(8,128)(2,1)} %copy-done.2, bf16[1024,1792]{1,0:T(8,128)(2,1)} %all-gather.3.cloned.1.call-done.k_ref.v_ref, bf16[1024,1792]{1,0:T(8,128)(2,1)} %all-gather.3.cloned.1.call-done.k_ref.v_ref, f32[1024,128]{1,0:T(8,128)} %fusion.66.bias_ref, ...), custom_call_target="tpu_custom_call" | custom-call | flops 2348810240 | bytes 7340032 | tf_op jit(solution)/shard_map/attend_back/pallas_call | solution.py:953
  545.0 1.5 copy-done
  547.0 2.6 fusion.25
  549.7 2.9 convolution_add_fusion
  552.7 1.8 collective-permute-start.2
  557.2 1.6 subtract_multiply_fusion.grad_ref
  558.9 16.6 %ffn_back.6 = (f32[512,896]{1,0:T(8,128)}, bf16[512,896]{1,0:T(8,128)(2,1)}, bf16[512,3584]{1,0:T(8,128)(2,1)}, f32[1,896]{1,0:T(1,128)}) custom-call(f32[512,896]{1,0:T(8,128)} %subtract_multiply_fusion.grad_ref, f32[512,896]{1,0:T(8,128)} %get-tuple-element.114.stream_ref, bf16[1,896]{1,0:T(2,128)(2,1)} %get-tuple-element.209.gain_ref, ...), custom_call_target="tpu_custom_call" | custom-call | flops 6576668672 | bytes 27525120 | tf_op jit(solution)/shard_map/ffn_back/pallas_call | solution.py:1069
  575.5 16.5 %ffn_back.7 = (f32[512,896]{1,0:T(8,128)}, bf16[512,896]{1,0:T(8,128)(2,1)}, bf16[512,3584]{1,0:T(8,128)(2,1)}, f32[1,896]{1,0:T(1,128)}) custom-call(f32[512,896]{1,0:T(8,128)} %get-tuple-element.118.grad_ref, bf16[512,896]{1,0:T(8,128)(2,1)} %bitcast.106, bf16[1,896]{1,0:T(2,128)(2,1)} %get-tuple-element.206.gain_ref, ...), custom_call_target="tpu_custom_call" | custom-call | flops 6576668672 | bytes 27525120 | tf_op jit(solution)/shard_map/ffn_back/pallas_call | solution.py:1069
  592.7 1.4 reduce-scatter.5.cloned.1.call-done
  595.2 4.1 fusion.73
  600.4 301.5 %reduce_gradients.1 = (f32[2,28,3584]{2,1,0:T(8,128)}, f32[2,28,3584]{2,1,0:T(8,128)}, f32[2,28,2688]{2,1,0:T(8,128)}, f32[2,28,896]{2,1,0:T(8,128)}, f32[2,28,3...) custom-call(bf16[128,896]{1,0:T(8,128)(2,1)} %copy-done.18, ...), custom_call_target="tpu_custom_call" | custom-call | tf_op jit(solution)/shard_map/reduce_gradients/pallas_call | solution.py:856
  904.2 2.5 copy.77
  906.6 1.8 copy.78
  908.4 1.5 copy.79
  909.9 1.5 copy.80
  912.1 1.5 copy.82
  913.6 1.5 copy.83
  (167 shorter events, 30.8 us)
Async XLA Ops:
  7.2 5.3 copy-start.24
  7.2 6.1 copy-start.36
  7.2 6.1 copy-start.37
  7.2 6.1 copy-start.38
  7.2 6.1 copy-start.35
  7.2 318.3 %all-gather.3.cloned.1.call-start = ((), (), s32[]{:S(2)}) async-start(), calls=%async_computation.2 | async-start | bytes 4128768 | tf_op jit(solution)/shard_map/all_gather | solution.py:1121
  14.0 275.1 %copy-start.6 = (bf16[1,128,896]{2,1,0:T(8,128)(2,1)S(1)}, bf16[1,128,896]{2,1,0:T(8,128)(2,1)}, u32[]{:S(2)}) copy-start(bf16[1,128,896]{2,1,0:T(8,128)(2,1)} %param.18) | copy-start | bytes 688132
  289.4 3.4 copy-start.18
  292.8 7.5 copy-start.2
  292.8 1.6 copy-start.12
  292.8 4.0 copy-start.34
  292.8 4.0 copy-start.39
  293.6 108.6 %all-gather.5.cloned.1.call-start = ((), (), s32[]{:S(2)}) async-start(), calls=%async_computation.3 | async-start | bytes 4128768 | tf_op jit(solution)/shard_map/all_gather | solution.py:1121
  294.4 7.3 collective-permute-start.1
  296.9 3.4 collective-permute-start
  301.9 3.0 copy-start.5
  339.5 11.4 %copy-start.19 = (bf16[128,896]{1,0:T(8,128)(2,1)}, bf16[128,896]{1,0:T(8,128)(2,1)S(1)}, u32[]{:S(2)}) copy-start(bf16[128,896]{1,0:T(8,128)(2,1)S(1)} %multiply_convert_fusion.2.refs_16_) | copy-start | bytes 688132
  363.2 3.4 copy-start.20
  363.2 4.6 copy-start.28
  366.6 35.6 %copy-start.3 = (bf16[128,2688]{1,0:T(8,128)(2,1)}, bf16[128,2688]{1,0:T(8,128)(2,1)S(1)}, u32[]{:S(2)}) copy-start(bf16[128,2688]{1,0:T(8,128)(2,1)S(1)} %fusion.11.q_ref) | copy-start | bytes 2064388
  367.5 131.1 %reduce-scatter.3.cloned.1.call-start = ((), (), s32[]{:S(2)}) async-start(), calls=%async_computation.4 | async-start | bytes 4128768 | tf_op jit(solution)/shard_map/reduce_scatter | solution.py:1131
  368.6 45.4 %copy-start.1 = (f32[128,896]{1,0:T(8,128)S(1)}, f32[128,896]{1,0:T(8,128)}, u32[]{:S(2)}) copy-start(f32[128,896]{1,0:T(8,128)} %get-tuple-element.86) | copy-start | bytes 1376260
  434.4 15.2 %copy-start.22 = (bf16[128,896]{1,0:T(8,128)(2,1)}, bf16[128,896]{1,0:T(8,128)(2,1)S(1)}, u32[]{:S(2)}) copy-start(bf16[128,896]{1,0:T(8,128)(2,1)S(1)} %convert_element_type.97.refs_11_) | copy-start | bytes 688132
  449.7 0.9 copy-start.27
  449.7 144.4 %reduce-scatter.5.cloned.1.call-start = ((), (), s32[]{:S(2)}) async-start(), calls=%async_computation.5 | async-start | bytes 4128768 | tf_op jit(solution)/shard_map/reduce_scatter | solution.py:1131
  499.6 4.2 copy-start.11
  499.6 4.2 copy-start.8
  515.2 12.0 %copy-start.21 = (bf16[128,896]{1,0:T(8,128)(2,1)}, bf16[128,896]{1,0:T(8,128)(2,1)S(1)}, u32[]{:S(2)}) copy-start(bf16[128,896]{1,0:T(8,128)(2,1)S(1)} %multiply_convert_fusion.refs_21_) | copy-start | bytes 688132
  527.2 2.3 copy-start.7
  529.7 15.2 %copy-start.17 = (bf16[128,896]{1,0:T(8,128)(2,1)}, bf16[128,896]{1,0:T(8,128)(2,1)S(1)}, u32[]{:S(2)}) copy-start(bf16[128,896]{1,0:T(8,128)(2,1)S(1)} %get-tuple-element.202.refs_3_) | copy-start | bytes 688132
  544.9 1.5 copy-start
  545.0 2.0 copy-start.4
  549.7 4.8 copy-start.23
  549.7 5.5 copy-start.31
  549.7 5.5 copy-start.32
  549.7 5.6 copy-start.26
  552.7 3.7 collective-permute-start.2
  575.4 17.2 %copy-start.33 = (f32[1,896]{1,0:T(1,128)S(1)}, f32[1,896]{1,0:T(1,128)}, u32[]{:S(2)}) copy-start(f32[1,896]{1,0:T(1,128)} %get-tuple-element.132) | copy-start | bytes 10756
  575.5 18.7 %copy-start.9 = (bf16[128,2688]{1,0:T(8,128)(2,1)S(1)}, bf16[128,2688]{1,0:T(8,128)(2,1)}, u32[]{:S(2)}) copy-start(bf16[128,2688]{1,0:T(8,128)(2,1)} %constant_dynamic-update-slice_fusion.3) | copy-start | bytes 2064388
  595.2 4.2 copy-start.10
  901.9 6.5 copy-start.16
  904.2 5.8 copy-start.15
  908.4 3.7 copy-start.14
  909.9 3.7 copy-start.13
  913.6 2.5 copy-start.30
  913.6 3.1 copy-start.25
  913.6 3.8 copy-start.29
Sparse Core Ops, SparseCore 0:
  293.7 31.7 all-gather.2
  367.6 34.5 all-gather.4
  449.8 48.7 reduce-scatter.2
  545.1 49.0 reduce-scatter.4

commit v5 on v4

--- a/solution.py
+++ b/solution.py
@@ -80,8 +80,8 @@
 
 
 ZYX, ZXY, YZX, XZY, YXZ, XYZ = (0, 1, 2), (0, 2, 1), (1, 0, 2), (2, 0, 1), (1, 2, 0), (2, 1, 0)
-ROUTES = (ZXY, ZYX, ZXY, ZYX, ZXY, ZYX, ZYX, ZXY, XZY, ZXY, ZXY, YZX)
-ROUTES += (XZY, YZX, XZY, ZYX, ZXY, YZX, ZYX, YZX, XZY, YXZ, YXZ)
+ROUTES = (YXZ, ZYX, ZXY, ZYX, ZXY, ZXY, YZX, ZXY, ZYX, ZYX)
+ROUTES += (ZXY, XZY, ZYX, YZX, XZY, XZY, YZX, YXZ, XYZ)
 UNIT_US, HOP_US, CORE_US = 2.2, 2.5, 0.17
 
 
@@ -111,7 +111,7 @@
         flying[link] -= 1
         order.append(("wait", number, step, now))
         if step + 1 < len(chains[number]):
-            heapq.heappush(ready[chains[number][step + 1][0]], (number + step + 1, number, step + 1))
+            heapq.heappush(ready[chains[number][step + 1][0]], (number, number, step + 1))
 
 
 PIECE = 896
@@ -129,7 +129,6 @@
             [(7, None, D, D), (8, None, 0, D), (2, 1, 0, qkv), (3, 1, 0, D)],
         ],
         whole(4, 0),
-        whole(4, 1),
         [[(9, None, 0, 128)], [(9, None, 0, 128)]],
     ]
 
@@ -145,7 +144,7 @@
         starts.append(cursor)
         cursor += half_width(group)
     pieces = []
-    for kind, number in (("n", 5), ("n", 0), ("r", 0), ("n", 1), ("r", 1), ("n", 2), ("n", 3), ("r", 2), ("n", 4), ("r", 3)):
+    for kind, number in (("n", 4), ("n", 0), ("r", 0), ("n", 1), ("r", 1), ("n", 2), ("n", 3), ("r", 2)):
         if kind == "n":
             width = half_width(groups[number])
             for first in range(0, width, PIECE):
@@ -156,15 +155,18 @@
     return groups, starts, cursor, pieces
 
 
-N_GROUPS = 6
+N_GROUPS = 5
+N_TALL = 3
 
 
 def gather_kernel(sizes, *refs):
     groups, starts, _, pieces = gather_plan()
     ins, neighbours = refs[:10], refs[10]
-    outs, encoder_outs = refs[11 : 15 + N_GROUPS], refs[15 + N_GROUPS : 24 + N_GROUPS]
-    halves, other, joined, own_rows, send_sem, recv_sem, load_sem, swap_sem = refs[24 + N_GROUPS : 32 + N_GROUPS]
-    encoder_rooms = refs[32 + N_GROUPS :]
+    n_outs = N_GROUPS + N_TALL
+    outs, encoder_outs, late_out = refs[11 : 11 + n_outs], refs[11 + n_outs : 20 + n_outs], refs[20 + n_outs]
+    halves, other, joined, own_rows, send_sem, recv_sem, load_sem, swap_sem = refs[21 + n_outs : 29 + n_outs]
+    late_in, late_down, late, late_sem = refs[29 + n_outs : 33 + n_outs]
+    encoder_rooms = refs[33 + n_outs :]
     place = grid_place()
     z, y, x, core = place
     sibling = device_at(moved(place, sizes, 3, 1))
@@ -176,10 +178,30 @@
                 source = ins[arg] if layer is None else ins[arg].at[layer]
                 loads.append((source.at[:, pl.ds(first, size)], halves.at[half, :, pl.ds(cursor, size)]))
                 cursor += size
-    for number, (arg, layer) in enumerate(((1, 0), (1, 1), (5, 0), (5, 1))):
+    for number, (arg, layer) in enumerate(((1, 0), (1, 1), (5, 0))):
         for part in range(2):
             loads.append((ins[arg].at[layer, part], own_rows.at[2 * number + part]))
+    late_loads = [
+        pltpu.make_async_copy(ins[4].at[1], late_in, late_sem.at[0]),
+        pltpu.make_async_copy(ins[5].at[1], late_down, late_sem.at[1]),
+    ]
+    late_store = pltpu.make_async_copy(late, late_out, late_sem.at[2])
+
+    def late_unit():
+        for copy in late_loads:
+            copy.wait()
+        down = late_down[...].astype(jnp.float32).reshape(-1, D)
+        fill = jnp.zeros((4 * ROOM - down.shape[0], D), jnp.float32)
+        late[pl.ds(0, 4 * ROOM), :] = jnp.concatenate([down, fill], 0).astype(BF)
+        fill = jnp.zeros((ROOM - late_in.shape[0], D), jnp.float32)
+        for k in range(FF // D):
+            rows = late_in[:, pl.ds(k * D, D)].astype(jnp.float32)
+            late[pl.ds((4 + k) * ROOM, ROOM), :] = jnp.concatenate([rows, fill], 0).astype(BF)
+        late_store.start()
+
     started = []
+    for copy in late_loads:
+        copy.start()
     for k, (source, target) in enumerate(loads):
         copy = pltpu.make_async_copy(source, target, load_sem.at[k])
         copy.start()
@@ -188,7 +210,7 @@
     for copy in started:
         copy.wait()
     placed = []
-    for number in range(4):
+    for number in range(N_TALL):
         for part in range(2):
             k = 2 * number + part
             target = outs[N_GROUPS + number].at[z, y, x, core, part]
@@ -293,7 +315,8 @@
     units = encoder_units(
         neighbours, outs[N_GROUPS - 1], (outs[0], outs[1]), (outs[N_GROUPS], outs[N_GROUPS + 1]), encoder_outs, encoder_rooms
     )
-    needs = [{k for k, piece in enumerate(pieces) if piece[:2] in wanted} for wanted in UNIT_NEEDS]
+    units.insert(0, late_unit)
+    needs = [{k for k, piece in enumerate(pieces) if piece[:2] in wanted} for wanted in [set()] + UNIT_NEEDS]
     due, arrived = 0.0, set()
     for what, number, step, time in schedule(pieces, routes, sizes):
         if what == "wait":
@@ -310,11 +333,15 @@
             due = time + UNIT_TIME
     for unit in units:
         unit()
+    late_store.wait()
+
+
+ROOM = 32
 
 
 HIDDEN_UNITS = 4
 UNIT_TIME = 7.0
-GAINS, FIRST, SECOND = {("n", 5)}, {("n", 0), ("r", 0)}, {("n", 1), ("r", 1)}
+GAINS, FIRST, SECOND = {("n", 4)}, {("n", 0), ("r", 0)}, {("n", 1), ("r", 1)}
 UNIT_NEEDS = [GAINS | FIRST] * (1 + HIDDEN_UNITS) + [SECOND] * (1 + HIDDEN_UNITS) + [set()]
 
 
@@ -426,14 +453,15 @@
     if rows % 4 or part % 8 or sizes != (HIDDEN_UNITS, 2, 2, 2):
         return gather_plainly(neighbours, enc_in, enc_down, dec_qkv, dec_out, dec_in, dec_down, cca_q, cca_kv, cca_out, gains)
     lead = sizes[:3]
-    shapes = [lead + (2 * rows, 2 * half_width(group)) for group in groups] + [lead + (2, 2, part, D)] * 4
+    shapes = [lead + (2 * rows, 2 * half_width(group)) for group in groups] + [lead + (2, 2, part, D)] * N_TALL
     out_shape = [jax.ShapeDtypeStruct(shape, BF) for shape in shapes]
     count = neighbours.shape[0]
     block = FF // HIDDEN_UNITS
     out_shape += [jax.ShapeDtypeStruct((count, D), jnp.float32)] * 2 + [jax.ShapeDtypeStruct((count, D), BF)] * 2
     out_shape += [jax.ShapeDtypeStruct((count, FF), BF)] * 4 + [jax.ShapeDtypeStruct((count, D), BF)]
+    out_shape += [jax.ShapeDtypeStruct((8 * ROOM, D), BF)]
     per_piece = sum((size - 1) * (1 if size == 2 else 2) for size in sizes)
-    n_loads = sum(len(half) for group in groups for half in group) + 16 + len(groups)
+    n_loads = sum(len(half) for group in groups for half in group) + 4 * N_TALL + len(groups)
     split = lambda w: w.reshape(w.shape[0], 2, part, D)
     outs = pl.pallas_call(
         functools.partial(gather_kernel, sizes),
@@ -444,11 +472,15 @@
             pltpu.VMEM((2, rows, total), BF),
             pltpu.VMEM((rows, total), BF),
             pltpu.VMEM((2 * rows, total), BF),
-            pltpu.VMEM((8, part, D), BF),
+            pltpu.VMEM((2 * N_TALL, part, D), BF),
             pltpu.SemaphoreType.DMA((per_piece * len(pieces),)),
             pltpu.SemaphoreType.DMA((per_piece * len(pieces),)),
             pltpu.SemaphoreType.DMA((n_loads,)),
             pltpu.SemaphoreType.DMA((2, len(groups))),
+            pltpu.VMEM((rows, FF), BF),
+            pltpu.VMEM((2, part, D), BF),
+            pltpu.VMEM((8 * ROOM, D), BF),
+            pltpu.SemaphoreType.DMA((3,)),
             pltpu.VMEM((count, D), jnp.float32),
             pltpu.VMEM((count, D), BF),
             pltpu.VMEM(lead + (2 * rows, 128), BF),
@@ -463,8 +495,9 @@
         name="gather_weights",
     )(enc_in, split(enc_down), dec_qkv, dec_out, dec_in, split(dec_down), cca_q, cca_kv, cca_out, gains, neighbours)
     narrow = [out.reshape(D, out.shape[-1]) for out in outs[:N_GROUPS]]
-    tall = [out.reshape(FF, D) for out in outs[N_GROUPS : N_GROUPS + 4]]
-    first, second, inputs_0, inputs_1, hidden_0, hidden_1, slope_0, slope_1, encoded = outs[N_GROUPS + 4 :]
+    tall = [out.reshape(FF, D) for out in outs[N_GROUPS : N_GROUPS + N_TALL]]
+    first, second, inputs_0, inputs_1, hidden_0, hidden_1, slope_0, slope_1, encoded, late = outs[N_GROUPS + N_TALL :]
+    late = lax.all_gather(late, ("dp", "seq"), axis=0, tiled=False)
     kept = [(neighbours, inputs_0, hidden_0, slope_0), (first, inputs_1, hidden_1, slope_1)]
     mixed = narrow[2]
     half = mixed.shape[1] // 2
@@ -473,9 +506,9 @@
     out = [side[:, 5 * D : 6 * D] for side in sides]
     return dict(
         encoder=(second, kept, encoded),
-        enc_in=narrow[:2], enc_down=tall[:2], dec_in=narrow[3:5], dec_down=tall[2:], dec_qkv=qkv, dec_out=out,
+        enc_in=narrow[:2], enc_down=tall[:2], dec_in=[narrow[3], None], dec_down=[tall[2], late], dec_qkv=qkv, dec_out=out,
         cca_kv=[side[:, :D] for side in sides], cca_q=sides[0][:, D : 2 * D], cca_out=sides[1][:, D : 2 * D],
-        gains=narrow[5][:, :8],
+        gains=narrow[4][:, :8],
     )
 
 
@@ -968,6 +1001,242 @@
         ),
         name="attend_back",
     )(joined, keys_vals, keys_vals, bias, log_total, grad_mixed)
+
+
+PAIR_GROUPS = (((0, 1), (2, 1)), ((2, 3), (1, 2)), ((4, 5), (2, 1)), ((6,), (1, 2)))
+BACK_GROUPS = tuple(((pair,), ((2, 1), (1, 2))[pair % 2]) for pair in range(7))
+BACK_LAGS = (2, 5, 7)
+
+
+def greet_plane(place):
+    barrier = pltpu.get_barrier_semaphore()
+    for axis in (1, 2, 3):
+        other = place[:axis] + (1 - place[axis],) + place[axis + 1 :]
+        pl.semaphore_signal(barrier, inc=1, device_id=device_at(other), device_id_type=MESH_ID)
+    pl.semaphore_wait(barrier, 3)
+
+
+def group_columns(pairs):
+    return [pl.ds(side * D + 128 * pairs[0], 128 * len(pairs)) for side in range(2)]
+
+
+def plane_copies(place, axis, sources, targets, send_sem, recv_sem, index):
+    device = place[:axis] + (1 - place[axis],) + place[axis + 1 :]
+    return [
+        pltpu.make_async_remote_copy(
+            src_ref=source,
+            dst_ref=target,
+            send_sem=send_sem.at[index, k],
+            recv_sem=recv_sem.at[index, k],
+            device_id=device_at(device),
+            device_id_type=MESH_ID,
+        )
+        for k, (source, target) in enumerate(zip(sources, targets))
+    ]
+
+
+def start_all(copies):
+    for copy in copies:
+        copy.start()
+
+
+def wait_all(copies):
+    for copy in copies:
+        copy.wait()
+
+
+def attend_gather_kernel(joined_ref, bias_ref, out_ref, total_ref, kept_ref, held, queries, send_sem, recv_sem, load_sem):
+    place = grid_place()
+    _, y, x, core = place
+    loads = [
+        pltpu.make_async_copy(joined_ref.at[:, pl.ds(D, 2 * D)], held.at[y, x, core], load_sem.at[0]),
+        pltpu.make_async_copy(joined_ref.at[:, pl.ds(0, D)], queries, load_sem.at[1]),
+    ]
+    start_all(loads)
+    greet_plane(place)
+    wait_all(loads)
+
+    def step(number, k):
+        pairs, route = PAIR_GROUPS[number]
+        if k == 0:
+            views = [held.at[y, x, core, :, columns] for columns in group_columns(pairs)]
+            axis = route[0]
+        elif k == 1:
+            axis = route[1]
+            views = [(held.at[y, :, core, :, c] if axis == 1 else held.at[:, x, core, :, c]) for c in group_columns(pairs)]
+        else:
+            axis = 3
+            views = [held.at[:, :, core, :, c] for c in group_columns(pairs)]
+        return plane_copies(place, axis, views, views, send_sem, recv_sem, 3 * number + k)
+
+    lane = lax.broadcasted_iota(jnp.int32, (queries.shape[0], 128), 1)
+    rows = bias_ref.shape[0]
+
+    def compute(number):
+        for pair in PAIR_GROUPS[number][0]:
+            keys = held[:, :, :, :, pl.ds(128 * pair, 128)].reshape(rows, 128)
+            vals = held[:, :, :, :, pl.ds(D + 128 * pair, 128)].reshape(rows, 128)
+            outs = []
+            for side, sided in enumerate(head_sides(queries[:, pl.ds(128 * pair, 128)])):
+                scores = dot(keys, sided, NT) * SCORE_SCALE + bias_ref[...]
+                peak = jnp.max(scores, 0, keepdims=True)
+                powers = jnp.exp(scores - peak)
+                total = jnp.sum(powers, 0, keepdims=True)
+                total_ref[pair, side : side + 1, :] = peak + jnp.log(total)
+                outs.append(dot((powers * (1.0 / total)).astype(BF), vals, TN))
+            out_ref[:, pl.ds(128 * pair, 128)] = jnp.where(lane < HEAD, outs[0], outs[1]).astype(BF)
+
+    count = len(PAIR_GROUPS)
+    for number in range(count):
+        start_all(step(number, 0))
+    for number in range(count):
+        wait_all(step(number, 0))
+        start_all(step(number, 1))
+    for number in range(count):
+        wait_all(step(number, 1))
+        start_all(step(number, 2))
+        if number > 0:
+            wait_all(step(number - 1, 2))
+            if number < count - 1:
+                compute(number - 1)
+    wait_all(step(count - 1, 2))
+    keep = pltpu.make_async_copy(held, kept_ref, load_sem.at[0])
+    keep.start()
+    compute(count - 2)
+    compute(count - 1)
+    keep.wait()
+
+
+def whole_block(shape):
+    return pl.BlockSpec(shape, lambda: (0,) * len(shape))
+
+
+def attend_gather(joined, bias):
+    rows = joined.shape[0]
+    _, n_y, n_x, n_core = grid_sizes()
+    lead = (n_y, n_x, n_core)
+    pairs, count = D // 128, len(PAIR_GROUPS)
+    mixed, log_total, kept = pl.pallas_call(
+        attend_gather_kernel,
+        out_shape=[
+            jax.ShapeDtypeStruct((rows, D), BF),
+            jax.ShapeDtypeStruct((pairs, 2, rows), jnp.float32),
+            jax.ShapeDtypeStruct(lead + (rows, 2 * D), BF),
+        ],
+        in_specs=[ANY, whole_block(bias.shape)],
+        out_specs=[whole_block((rows, D)), whole_block((pairs, 2, rows)), ANY],
+        scratch_shapes=[
+            pltpu.VMEM(lead + (rows, 2 * D), BF),
+            pltpu.VMEM((rows, D), BF),
+            pltpu.SemaphoreType.DMA((3 * count, 2)),
+            pltpu.SemaphoreType.DMA((3 * count, 2)),
+            pltpu.SemaphoreType.DMA((2,)),
+        ],
+        compiler_params=pltpu.CompilerParams(collective_id=2, has_side_effects=True, vmem_limit_bytes=32 << 20),
+        name="attend_gather",
+    )(joined, bias)
+    return mixed, log_total, kept.reshape(-1, 2 * D)
+
+
+def attend_scatter_kernel(joined_ref, held_ref, bias_ref, total_ref, grad_ref, gq_ref, own_ref, *scratch):
+    queries, part, from_core, from_first, from_second, send_sem, recv_sem, load_sem = scratch
+    place = grid_place()
+    _, y, x, core = place
+    load = pltpu.make_async_copy(joined_ref.at[:, pl.ds(0, D)], queries, load_sem.at[0])
+    load.start()
+    greet_plane(place)
+    load.wait()
+    rows = bias_ref.shape[0]
+    lane = lax.broadcasted_iota(jnp.int32, (queries.shape[0], 128), 1)
+
+    def compute(number):
+        for pair in BACK_GROUPS[number][0]:
+            columns, beside = pl.ds(128 * pair, 128), pl.ds(D + 128 * pair, 128)
+            keys = held_ref[:, :, :, :, columns].reshape(rows, 128)
+            vals = held_ref[:, :, :, :, beside].reshape(rows, 128)
+            q_sides, g_sides = head_sides(queries[:, columns]), head_sides(grad_ref[:, columns])
+            grad_q, grad_k, grad_v = [], 0.0, 0.0
+            for side in range(2):
+                scores = dot(keys, q_sides[side], NT) * SCORE_SCALE + bias_ref[...]
+                probs = jnp.exp(scores - total_ref[pair, side : side + 1, :])
+                grad_probs = dot(vals, g_sides[side], NT)
+                delta = jnp.sum(probs * grad_probs, 0, keepdims=True)
+                grad_scores = (probs * (grad_probs - delta)).astype(BF)
+                grad_v = grad_v + dot(probs.astype(BF), g_sides[side], NN)
+                grad_k = grad_k + dot(grad_scores, q_sides[side], NN)
+                grad_q.append(dot(grad_scores, keys, TN))
+            gq_ref[:, columns] = (jnp.where(lane < HEAD, grad_q[0], grad_q[1]) * SCORE_SCALE).astype(BF)
+            shape = part.shape[:4] + (128,)
+            part[:, :, :, :, columns] = (grad_k * SCORE_SCALE).astype(BF).reshape(shape)
+            part[:, :, :, :, beside] = grad_v.astype(BF).reshape(shape)
+
+    def step(number, k):
+        pairs, route = BACK_GROUPS[number]
+        columns = group_columns(pairs)
+        if k == 0:
+            axis = 3
+            sources = [part.at[:, :, 1 - core, :, c] for c in columns]
+            targets = [from_core.at[:, :, :, c] for c in columns]
+        elif k == 1:
+            axis = route[1]
+            sources = [(part.at[1 - y, :, core, :, c] if axis == 1 else part.at[:, 1 - x, core, :, c]) for c in columns]
+            targets = [from_first.at[:, :, c] for c in columns]
+        else:
+            axis = route[0]
+            sources = [(part.at[1 - y, x, core, :, c] if axis == 1 else part.at[y, 1 - x, core, :, c]) for c in columns]
+            targets = [from_second.at[:, c] for c in columns]
+        return plane_copies(place, axis, sources, targets, send_sem, recv_sem, 3 * number + k)
+
+    def add(number, k):
+        pairs, route = BACK_GROUPS[number]
+        wait_all(step(number, k))
+        for c in group_columns(pairs):
+            if k == 0:
+                part[:, :, core, :, c] = part[:, :, core, :, c] + from_core[:, :, :, c]
+            elif k == 1 and route[1] == 1:
+                part[y, :, core, :, c] = part[y, :, core, :, c] + from_first[:, :, c]
+            elif k == 1:
+                part[:, x, core, :, c] = part[:, x, core, :, c] + from_first[:, :, c]
+            else:
+                own_ref[:, c] = part[y, x, core, :, c] + from_second[:, c]
+
+    count = len(BACK_GROUPS)
+    for time in range(count + BACK_LAGS[-1]):
+        if time < count:
+            compute(time)
+            start_all(step(time, 0))
+        for k, lag in enumerate(BACK_LAGS):
+            number = time - lag
+            if 0 <= number < count:
+                add(number, k)
+                if k < 2:
+                    start_all(step(number, k + 1))
+
+
+def attend_scatter(joined, keys_vals, bias, log_total, grad_mixed):
+    rows = joined.shape[0]
+    _, n_y, n_x, n_core = grid_sizes()
+    lead = (n_y, n_x, n_core)
+    count = len(BACK_GROUPS)
+    held = keys_vals.reshape(lead + (rows, 2 * D))
+    return pl.pallas_call(
+        attend_scatter_kernel,
+        out_shape=[jax.ShapeDtypeStruct((rows, D), BF), jax.ShapeDtypeStruct((rows, 2 * D), BF)],
+        in_specs=[ANY] + [whole_block(v.shape) for v in (held, bias, log_total, grad_mixed)],
+        out_specs=[whole_block((rows, D)), whole_block((rows, 2 * D))],
+        scratch_shapes=[
+            pltpu.VMEM((rows, D), BF),
+            pltpu.VMEM(lead + (rows, 2 * D), BF),
+            pltpu.VMEM((n_y, n_x, rows, 2 * D), BF),
+            pltpu.VMEM((2, rows, 2 * D), BF),
+            pltpu.VMEM((rows, 2 * D), BF),
+            pltpu.SemaphoreType.DMA((3 * count, 2)),
+            pltpu.SemaphoreType.DMA((3 * count, 2)),
+            pltpu.SemaphoreType.DMA((1,)),
+        ],
+        compiler_params=pltpu.CompilerParams(collective_id=3, has_side_effects=True, vmem_limit_bytes=40 << 20),
+        name="attend_scatter",
+    )(joined, held, bias, log_total, grad_mixed)
 
 
 def gelu_parts(values):
@@ -1097,6 +1366,130 @@
     )(upstream, stream, norm_gain, slope, weight_in, weight_down)
 
 
+def spread_matrix(devices):
+    rows = D // devices
+    source = lax.broadcasted_iota(jnp.int32, (D, devices * ROOM), 0)
+    target = lax.broadcasted_iota(jnp.int32, (D, devices * ROOM), 1)
+    return jnp.where((target // ROOM * rows + target % ROOM == source) & (target % ROOM < rows), 1.0, 0.0).astype(BF)
+
+
+def late_blocks(late, tall):
+    devices = late.shape[0]
+    per_block = D // tall
+    return [
+        pl.BlockSpec((devices, ROOM, D), lambda j: (0, 4 + j, 0)),
+        pl.BlockSpec((per_block, 4 * ROOM, D), lambda j: (j, 0, 0)),
+    ]
+
+
+def late_in_block(ref):
+    return ref[...].reshape(-1, D)
+
+
+def late_down_block(ref):
+    values = ref[...]
+    return values[:, : D // values.shape[0]].reshape(D, D)
+
+
+def late_ffn_kernel(stream_ref, gain_ref, spread_ref, in_ref, down_ref, out_ref, inputs_ref, hidden_ref, slope_ref, spread):
+    step = pl.program_id(0)
+
+    @pl.when(step == 0)
+    def _():
+        stream = stream_ref[...].astype(jnp.float32)
+        out_ref[...] = stream
+        inputs = (norm_parts(stream)[0] * gain_ref[...].astype(jnp.float32)).astype(BF)
+        inputs_ref[...] = inputs
+        spread[...] = dot(inputs, spread_ref[...], NN).astype(BF)
+
+    value, slope = gelu_parts(dot(spread[...], late_in_block(in_ref), NN))
+    hidden = value.astype(BF)
+    hidden_ref[...] = hidden
+    slope_ref[...] = slope.astype(BF)
+    out_ref[...] += dot(hidden, late_down_block(down_ref), NN)
+
+
+def late_ffn(stream, norm_gain, spread, late, tall):
+    rows = stream.shape[0]
+    still = lambda j: (0, 0)
+    return pl.pallas_call(
+        late_ffn_kernel,
+        grid=(FF // D,),
+        out_shape=[
+            jax.ShapeDtypeStruct((rows, D), jnp.float32),
+            jax.ShapeDtypeStruct((rows, D), BF),
+            jax.ShapeDtypeStruct((rows, FF), BF),
+            jax.ShapeDtypeStruct((rows, FF), BF),
+        ],
+        in_specs=[pl.BlockSpec((rows, D), still), pl.BlockSpec((1, D), still), pl.BlockSpec(spread.shape, still)]
+        + late_blocks(late, tall),
+        out_specs=[
+            pl.BlockSpec((rows, D), still),
+            pl.BlockSpec((rows, D), still),
+            pl.BlockSpec((rows, D), lambda j: (0, j)),
+            pl.BlockSpec((rows, D), lambda j: (0, j)),
+        ],
+        scratch_shapes=[pltpu.VMEM((rows, spread.shape[1]), BF)],
+        cost_estimate=pl.CostEstimate(flops=4 * rows * D * FF, bytes_accessed=5 * D * FF, transcendentals=rows * FF),
+        name="late_ffn",
+    )(stream, norm_gain, spread, late, late)
+
+
+def late_back_kernel(grad_ref, stream_ref, gain_ref, spread_ref, slope_ref, in_ref, down_ref, out_ref, low_ref, pre_ref, gain_out, total):
+    step = pl.program_id(0)
+
+    @pl.when(step == 0)
+    def _():
+        low_ref[...] = grad_ref[...].astype(BF)
+        total[...] = jnp.zeros_like(total)
+
+    pre = (dot(low_ref[...], late_down_block(down_ref), NT) * slope_ref[...].astype(jnp.float32)).astype(BF)
+    pre_ref[...] = pre
+    total[...] += dot(pre, late_in_block(in_ref), NT)
+
+    @pl.when(step == pl.num_programs(0) - 1)
+    def _():
+        whole = total[...]
+        high = whole.astype(BF)
+        rest = (whole - high.astype(jnp.float32)).astype(BF)
+        inner = dot(high, spread_ref[...], NT) + dot(rest, spread_ref[...], NT)
+        back, gain = norm_gradient(stream_ref[...].astype(jnp.float32), gain_ref[...].astype(jnp.float32), inner)
+        out_ref[...] = grad_ref[...].astype(jnp.float32) + back
+        gain_out[...] = gain
+
+
+def late_ffn_back(upstream, stream, norm_gain, slope, spread, late, tall):
+    rows = stream.shape[0]
+    still = lambda j: (0, 0)
+    return pl.pallas_call(
+        late_back_kernel,
+        grid=(FF // D,),
+        out_shape=[
+            jax.ShapeDtypeStruct((rows, D), jnp.float32),
+            jax.ShapeDtypeStruct((rows, D), BF),
+            jax.ShapeDtypeStruct((rows, FF), BF),
+            jax.ShapeDtypeStruct((1, D), jnp.float32),
+        ],
+        in_specs=[
+            pl.BlockSpec((rows, D), still),
+            pl.BlockSpec((rows, D), still),
+            pl.BlockSpec((1, D), still),
+            pl.BlockSpec(spread.shape, still),
+            pl.BlockSpec((rows, D), lambda j: (0, j)),
+        ]
+        + late_blocks(late, tall),
+        out_specs=[
+            pl.BlockSpec((rows, D), still),
+            pl.BlockSpec((rows, D), still),
+            pl.BlockSpec((rows, D), lambda j: (0, j)),
+            pl.BlockSpec((1, D), still),
+        ],
+        scratch_shapes=[pltpu.VMEM((rows, spread.shape[1]), jnp.float32)],
+        cost_estimate=pl.CostEstimate(flops=4 * rows * D * FF, bytes_accessed=5 * D * FF, transcendentals=0),
+        name="late_ffn_back",
+    )(upstream, stream, norm_gain, spread, slope, late, late)
+
+
 def shifted(x, axis, by):
     count = lax.axis_size(axis)
     pairs = [(i, i + by) for i in range(count) if 0 <= i + by < count]
@@ -1118,17 +1511,23 @@
 def self_forward(stream, norm_gain, weight_qkv, weight_out, bias):
     inputs = normed(stream, norm_gain)
     joined = dot(inputs, weight_qkv, NN).astype(BF)
-    keys_vals = lax.all_gather(joined[:, D:], "seq", axis=0, tiled=True)
-    mixed, log_total = attend(joined, keys_vals, bias)
+    if grid_sizes() == (4, 2, 2, 2):
+        mixed, log_total, keys_vals = attend_gather(joined, bias)
+    else:
+        keys_vals = lax.all_gather(joined[:, D:], "seq", axis=0, tiled=True)
+        mixed, log_total = attend(joined, keys_vals, bias)
     return stream + dot(mixed, weight_out, NN), (stream, inputs, joined, keys_vals, log_total, mixed)
 
 
-def self_back(stored, norm_gain, weight_qkv, weight_out, bias, upstream):
+def self_back(stored, norm_gain, weight_qkv, weight_out, bias, upstream, covered):
     stream, inputs, joined, keys_vals, log_total, mixed = stored
     grad_low = upstream.astype(BF)
     grad_mixed = dot(grad_low, weight_out, NT).astype(BF)
-    grad_queries, grad_pairs = attend_back(joined, keys_vals, bias, log_total, grad_mixed)
-    own_pairs = lax.psum_scatter(grad_pairs, "seq", scatter_dimension=0, tiled=True)
+    if grid_sizes() == (4, 2, 2, 2) and not covered:
+        grad_queries, own_pairs = attend_scatter(joined, keys_vals, bias, log_total, grad_mixed)
+    else:
+        grad_queries, grad_pairs = attend_back(joined, keys_vals, bias, log_total, grad_mixed)
+        own_pairs = lax.psum_scatter(grad_pairs, "seq", scatter_dimension=0, tiled=True)
     grad_joined = jnp.concatenate([grad_queries, own_pairs], -1)
     back, gain_grad = norm_back(stream, norm_gain, dot(grad_joined, weight_qkv, NT))
     return upstream + back, gain_grad, ((inputs, grad_joined), (mixed, grad_low))
@@ -1232,7 +1631,12 @@
         if layer == 0:
             stream, cross_kept = cross_forward(stream, encoded, keep_flag, *cross_weights)
         before = stream
-        stream, inputs, hidden, slope = ffn(before, ffn_gain[layer], full["dec_in"][layer], full["dec_down"][layer])
+        if full["dec_in"][layer] is None:
+            late, tall = full["dec_down"][layer], dec_down.shape[1]
+            spread = spread_matrix(late.shape[0])
+            stream, inputs, hidden, slope = late_ffn(before, ffn_gain[layer], spread, late, tall)
+        else:
+            stream, inputs, hidden, slope = ffn(before, ffn_gain[layer], full["dec_in"][layer], full["dec_down"][layer])
         ffn_kept.append((before, inputs, hidden, slope))
     result = stream.astype(BF)
 
@@ -1241,14 +1645,16 @@
     attn_pairs, ffn_pairs = [None] * DEC_LAYERS, [None] * DEC_LAYERS
     for layer in reversed(range(DEC_LAYERS)):
         before, inputs, hidden, slope = ffn_kept[layer]
-        upstream, grad_low, grad_pre, ffn_gain_g[layer] = ffn_back(
-            upstream, before, ffn_gain[layer], slope, full["dec_in"][layer], full["dec_down"][layer]
-        )
+        if full["dec_in"][layer] is None:
+            back = late_ffn_back(upstream, before, ffn_gain[layer], slope, spread, late, tall)
+        else:
+            back = ffn_back(upstream, before, ffn_gain[layer], slope, full["dec_in"][layer], full["dec_down"][layer])
+        upstream, grad_low, grad_pre, ffn_gain_g[layer] = back
         ffn_pairs[layer] = ((inputs, grad_pre), (grad_low, hidden))
         if layer == 0:
             upstream, cross_gain_g, cross_pairs, encoded_grad = cross_back(cross_kept, *cross_weights, upstream)
         upstream, attn_gain_g[layer], attn_pairs[layer] = self_back(
-            attn_kept[layer], attn_gain[layer], full["dec_qkv"][layer], full["dec_out"][layer], bias, upstream
+            attn_kept[layer], attn_gain[layer], full["dec_qkv"][layer], full["dec_out"][layer], bias, upstream, layer == 0
         )
 
     enc_upstream, final_gain_g = norm_back(encoder, final_gain, encoded_grad)

time: 935 us -> 839 us (0.90)
  waiting for transfers between devices: 100 us -> 3.07 us
    pallas_call x0 -> x5, Pallas kernels: none -> 99.2 us  [the longest x2 52.7 us: attend_gather(): pl.pallas_call(attend_gather_kernel, out_shape=[jax.ShapeDtypeStruct((row...]
    pallas_call x1, Pallas kernels: 274 us -> 223 us  [gather_weights(): pl.pallas_call(functools.partial(gather_kernel, sizes), out_shape=out_sha...]
    all_gather x2 -> x1, waiting for transfers between devices: 50.2 us -> 0.01 us  [gather_weights(): late = lax.all_gather(late, ('dp', 'seq'), axis=0, tiled=False)]
    reduce_scatter x2 -> x1, waiting for transfers between devices: 49.4 us -> 1.52 us  [self_back(): lax.psum_scatter(grad_pairs, 'seq', scatter_dimension=0, tiled=True)]
    pallas_call x3 -> x1, Pallas kernels: 32.3 us -> 8.88 us  [attend(): pl.pallas_call(attend_kernel, grid=(pairs,), out_shape=[jax.ShapeDtypeStr...]
    pallas_call x3 -> x2, Pallas kernels: 34.1 us -> 21.6 us  [attend_back(): pl.pallas_call(attend_back_kernel, grid=(pairs,), out_shape=[jax.ShapeDty...]
    pallas_call x4 -> x3, Pallas kernels: 51.7 us -> 42.7 us  [ffn_back(): pl.pallas_call(ffn_back_kernel, grid=(FF // block,), out_shape=[jax.Shape...]
    unnamed x98 -> x108, local copies, waits for them, and re-layouts: 23.2 us -> 27.8 us
  transfers between devices with their start and end apart: 7 -> 5, of which waited for: 5 -> 2; matrix products, arithmetic and copies ran while one was open for 2% -> 6% of each run, Pallas kernels for 4% -> 12%
where the time goes in v5:
time: 839 us; the launch traced here: 829 us
  Pallas kernels  703 us (84%)
  matrix products  48.1 us (6%)
  local copies, waits for them, and re-layouts  35.7 us (4%)
  other arithmetic  17.5 us (2%)
  between operations  15.2 us (2%)
    pallas_call x1, Pallas kernels, reduce_gradients(): pl.pallas_call(functools.partial(reduce_kernel, sizes, tall), out_shape=[...  300 us
    pallas_call x1, Pallas kernels, gather_weights(): pl.pallas_call(functools.partial(gather_kernel, sizes), out_shape=out_sha...  223 us
    pallas_call x2, Pallas kernels, attend_gather(): pl.pallas_call(attend_gather_kernel, out_shape=[jax.ShapeDtypeStruct((row...  52.7 us
    dot_general x16, matrix products, dot(): lax.dot_general(left, right, dims, preferred_element_type=jnp.float32)  48.1 us
    pallas_call x3, Pallas kernels, ffn_back(): pl.pallas_call(ffn_back_kernel, grid=(FF // block,), out_shape=[jax.Shape...  42.7 us
    unnamed x108, local copies, waits for them, and re-layouts  27.8 us
    pallas_call x1, Pallas kernels, attend_scatter(): pl.pallas_call(attend_scatter_kernel, out_shape=[jax.ShapeDtypeStruct((ro...  25.5 us
    pallas_call x2, Pallas kernels, attend_back(): pl.pallas_call(attend_back_kernel, grid=(pairs,), out_shape=[jax.ShapeDty...  21.6 us
  transfers between devices with their start and end apart: 5, of which 2 were waited for; matrix products, arithmetic and copies ran while one was open for 6% of the time, Pallas kernels for 12%

profile of v5, /device:TPU:0, one launch (start us, length us, event | category | flops | bytes accessed | tf_op | source)
XLA Modules:
  0.0 828.6 jit_solution(13556462559525943684)
XLA Ops:
  7.3 1.9 copy.70.refs_0_
  9.2 1.7 copy.71.refs_2_
  10.9 1.6 copy.72.refs_3_
  14.0 223.2 %gather_weights.1 = (bf16[4,2,2,56,3584]{4,3,2,1,0:T(8,128)(2,1)}, bf16[4,2,2,56,3584]{4,3,2,1,0:T(8,128)(2,1)}, bf16[4,2,2,56,10752]{4,3,2,1,0:T(8,128)(2,1)}, ...) custom-call(bf16[2,28,3584]{2,1,0:T(8,128)(2,1)} %copy.70.refs_0_, ...), custom_call_target="tpu_custom_call" | custom-call | tf_op jit(solution)/shard_map/gather_weights/pallas_call | solution.py:466
  237.3 2.1 slice_bitcast_fusion.2
  239.4 3.0 collective-permute-start.1
  242.5 1.8 collective-permute-start
  245.5 3.5 fusion.10.joined_ref.q_ref
  249.0 26.6 %attend_gather.2 = (bf16[128,896]{1,0:T(8,128)(2,1)S(1)}, f32[7,2,128]{2,1,0:T(2,128)S(1)}, bf16[2,2,2,128,1792]{4,3,2,1,0:T(8,128)(2,1)S(1)}) custom-call(bf16[128,2688]{1,0:T(8,128)(2,1)S(1)} %fusion.10.joined_ref.q_ref, f32[1024,128]{1,0:T(8,128)S(1)} %fusion.68.bias_ref), custom_call_target="tpu_custom_call" | custom-call | tf_op jit(solution)/shard_map/attend_gather/pallas_call | solution.py:1119
  275.7 3.2 multiply_reduce_fusion.7
  280.5 2.6 fusion.53.q_ref
  283.1 1.8 select_convert_fusion.spread_ref
  287.6 3.0 convolution_convert_fusion
  290.5 2.6 convolution_convert_fusion.1
  294.5 8.9 %attend.1 = (bf16[128,896]{1,0:T(8,128)(2,1)}, f32[7,2,128]{2,1,0:T(2,128)}) custom-call(bf16[128,896]{1,0:T(8,128)(2,1)} %fusion.53.q_ref, bf16[512,1792]{1,0:T(8,128)(2,1)} %pad_maximum_fusion.k_ref.v_ref, bf16[512,1792]{1,0:T(8,128)(2,1)} %pad_maximum_fusion.k_ref.v_ref, f32[512,128]{1,0:T(8,128)} %fusion.78.bias_ref), custom_call_target="tpu_custom_call" | custom-call | flops 469762048 | bytes 1835008 | tf_op jit(solution)/shard_map/attend/pallas_call | solution.py:945
  303.4 2.8 fusion.44.stream_ref
  306.2 7.5 ffn.1
  316.7 3.3 fusion.13.joined_ref
  320.1 26.0 %attend_gather.3 = (bf16[128,896]{1,0:T(8,128)(2,1)S(1)}, f32[7,2,128]{2,1,0:T(2,128)S(1)}, bf16[2,2,2,128,1792]{4,3,2,1,0:T(8,128)(2,1)S(1)}) custom-call(bf16[128,2688]{1,0:T(8,128)(2,1)S(1)} %fusion.13.joined_ref, f32[1024,128]{1,0:T(8,128)S(1)} %fusion.68.bias_ref), custom_call_target="tpu_custom_call" | custom-call | tf_op jit(solution)/shard_map/attend_gather/pallas_call | solution.py:1119
  346.1 1.9 copy-done.2
  348.0 2.7 fusion.47.stream_ref
  350.7 9.7 %late_ffn.1 = (f32[128,896]{1,0:T(8,128)}, bf16[128,896]{1,0:T(8,128)(2,1)}, bf16[128,3584]{1,0:T(8,128)(2,1)}, bf16[128,3584]{1,0:T(8,128)(2,1)}) custom-call(f32[128,896]{1,0:T(8,128)} %fusion.47.stream_ref, bf16[1,896]{1,0:T(2,128)(2,1)} %get-tuple-element.209.gain_ref, bf16[896,1024]{1,0:T(8,128)(2,1)} %select_convert_fusion.spread_ref, ...), custom_call_target="tpu_custom_call" | custom-call | flops 1644167168 | bytes 16056320 | tf_op jit(solution)/shard_map/late_ffn/pallas_call | solution.py:1415
  360.4 11.4 %late_ffn_back.1 = (f32[128,896]{1,0:T(8,128)}, bf16[128,896]{1,0:T(8,128)(2,1)}, bf16[128,3584]{1,0:T(8,128)(2,1)}, f32[1,896]{1,0:T(1,128)}) custom-call(f32[128,896]{1,0:T(8,128)} %bitcast_convert_fusion.grad_ref, f32[128,896]{1,0:T(8,128)} %fusion.47.stream_ref, bf16[1,896]{1,0:T(2,128)(2,1)} %get-tuple-element.209.gain_ref, ...), custom_call_target="tpu_custom_call" | custom-call | flops 1644167168 | bytes 16056320 | tf_op jit(solution)/shard_map/late_ffn_back/pallas_call | solution.py:1464
  372.8 2.1 fusion.59.grad_ref
  375.0 2.0 copy-done.3
  377.0 25.5 %attend_scatter.1 = (bf16[128,896]{1,0:T(8,128)(2,1)S(1)}, bf16[128,1792]{1,0:T(8,128)(2,1)S(1)}) custom-call(bf16[128,2688]{1,0:T(8,128)(2,1)S(1)} %fusion.13.joined_ref, bf16[2,2,2,128,1792]{4,3,2,1,0:T(8,128)(2,1)S(1)} %copy-done.3, f32[1024,128]{1,0:T(8,128)S(1)} %fusion.68.bias_ref, f32[7,2,128]{2,1,0:T(2,128)S(1)} %get-tuple-element.94.total_ref, ...), custom_call_target="tpu_custom_call" | custom-call | tf_op jit(solution)/shard_map/attend_scatter/pallas_call | solution.py:1222
  402.6 4.2 multiply_reduce_fusion.3
  407.7 9.5 %ffn_back.3 = (f32[128,896]{1,0:T(8,128)}, bf16[128,896]{1,0:T(8,128)(2,1)}, bf16[128,3584]{1,0:T(8,128)(2,1)}, f32[1,896]{1,0:T(1,128)}) custom-call(f32[128,896]{1,0:T(8,128)} %multiply_add_fusion.1.grad_ref, f32[128,896]{1,0:T(8,128)} %fusion.44.stream_ref, bf16[1,896]{1,0:T(2,128)(2,1)} %get-tuple-element.210.gain_ref, ...), custom_call_target="tpu_custom_call" | custom-call | flops 1644167168 | bytes 16515072 | tf_op jit(solution)/shard_map/ffn_back/pallas_call | solution.py:1338
  419.1 2.7 fusion.56.grad_ref
  421.8 9.2 %attend_back.2 = (bf16[128,896]{1,0:T(8,128)(2,1)}, bf16[512,1792]{1,0:T(8,128)(2,1)}) custom-call(bf16[128,896]{1,0:T(8,128)(2,1)} %fusion.53.q_ref, bf16[512,1792]{1,0:T(8,128)(2,1)} %pad_maximum_fusion.k_ref.v_ref, bf16[512,1792]{1,0:T(8,128)(2,1)} %pad_maximum_fusion.k_ref.v_ref, f32[512,128]{1,0:T(8,128)} %fusion.78.bias_ref, ...), custom_call_target="tpu_custom_call" | custom-call | flops 1174405120 | bytes 3670016 | tf_op jit(solution)/shard_map/attend_back/pallas_call | solution.py:986
  431.0 2.3 multiply_reduce_fusion.2
  434.2 2.7 fusion.50.grad_ref
  436.9 12.4 %attend_back.3 = (bf16[128,896]{1,0:T(8,128)(2,1)}, bf16[1024,1792]{1,0:T(8,128)(2,1)}) custom-call(bf16[128,2688]{1,0:T(8,128)(2,1)} %copy-done.4, bf16[1024,1792]{1,0:T(8,128)(2,1)} %bitcast.78, bf16[1024,1792]{1,0:T(8,128)(2,1)} %bitcast.79, f32[1024,128]{1,0:T(8,128)} %copy-done.1, f32[7,2,128]{2,1,0:T(2,128)} %copy-done.7, bf16[128,896]{1,0:T(8,128)(2,1)} %fusion.50.grad_ref), custom_call_target="tpu_custom_call" | custom-call | flops 2348810240 | bytes 7340032 | tf_op jit(solution)/shard_map/attend_back/pallas_call | solution.py:986
  451.4 2.6 fusion.27
  454.1 3.0 convolution_add_fusion
  459.3 1.5 collective-permute-done.2
  461.6 1.7 subtract_multiply_fusion.grad_ref
  463.3 16.8 %ffn_back.4 = (f32[512,896]{1,0:T(8,128)}, bf16[512,896]{1,0:T(8,128)(2,1)}, bf16[512,3584]{1,0:T(8,128)(2,1)}, f32[1,896]{1,0:T(1,128)}) custom-call(f32[512,896]{1,0:T(8,128)} %subtract_multiply_fusion.grad_ref, f32[512,896]{1,0:T(8,128)} %get-tuple-element.116.stream_ref, bf16[1,896]{1,0:T(2,128)(2,1)} %get-tuple-element.211.gain_ref, ...), custom_call_target="tpu_custom_call" | custom-call | flops 6576668672 | bytes 27525120 | tf_op jit(solution)/shard_map/ffn_back/pallas_call | solution.py:1338
  480.1 16.5 %ffn_back.5 = (f32[512,896]{1,0:T(8,128)}, bf16[512,896]{1,0:T(8,128)(2,1)}, bf16[512,3584]{1,0:T(8,128)(2,1)}, f32[1,896]{1,0:T(1,128)}) custom-call(f32[512,896]{1,0:T(8,128)} %get-tuple-element.120.grad_ref, bf16[512,896]{1,0:T(8,128)(2,1)} %bitcast.108, bf16[1,896]{1,0:T(2,128)(2,1)} %get-tuple-element.208.gain_ref, ...), custom_call_target="tpu_custom_call" | custom-call | flops 6576668672 | bytes 27525120 | tf_op jit(solution)/shard_map/ffn_back/pallas_call | solution.py:1338
  497.2 1.5 reduce-scatter.2.cloned.1.call-done
  499.8 4.8 fusion.75
  505.7 299.7 %reduce_gradients.1 = (f32[2,28,3584]{2,1,0:T(8,128)}, f32[2,28,3584]{2,1,0:T(8,128)}, f32[2,28,2688]{2,1,0:T(8,128)}, f32[2,28,896]{2,1,0:T(8,128)}, f32[2,28,3...) custom-call(bf16[128,896]{1,0:T(8,128)(2,1)} %copy-done.22, ...), custom_call_target="tpu_custom_call" | custom-call | tf_op jit(solution)/shard_map/reduce_gradients/pallas_call | solution.py:889
  807.6 2.5 copy.77
  810.1 1.8 copy.78
  811.9 1.5 copy.79
  813.4 1.5 copy.80
  815.5 1.5 copy.82
  817.1 1.5 copy.83
  (173 shorter events, 29.7 us)
Async XLA Ops:
  7.2 5.3 copy-start.29
  7.2 6.1 copy-start.41
  7.2 6.1 copy-start.42
  7.2 6.1 copy-start.43
  7.2 6.1 copy-start.40
  7.2 343.5 %all-gather.3.cloned.1.call-start = ((), (), s32[]{:S(2)}) async-start(), calls=%async_computation.2 | async-start | bytes 15138816 | tf_op jit(solution)/shard_map/all_gather | solution.py:500
  237.2 5.2 copy-start.39
  237.2 5.2 copy-start.44
  237.2 7.0 copy-start.33
  237.2 7.2 copy-start.12
  237.3 261.5 %reduce-scatter.2.cloned.1.call-start = ((), (), s32[]{:S(2)}) async-start(), calls=%async_computation.1 | async-start | bytes 4128768 | tf_op jit(solution)/shard_map/reduce_scatter | solution.py:1530
  239.4 47.0 %collective-permute-start.1 = (bf16[1,256,896]{2,1,0:T(8,128)(2,1)}, bf16[1,256,896]{2,1,0:T(8,128)(2,1)}, u32[]{:S(2)}, u32[]{:S(2)}) collective-permute-start(bf16[1,256,896]{2,1,0:T(8,128)(2,1)} %get-tuple-element.206), channel_id=1, source_target_pairs={{0,1},{1,2},{2,3},{3,4},{4,5},{5,6},{6,7},{8,9},{9,10},{10,11},{11... | collective-permute-start | bytes 1376264 | tf_op jit(solution)/shard_map/ppermute | solution.py:1496
  242.5 42.4 %collective-permute-start = (bf16[1,2]{1,0:T(2,128)(2,1)S(1)}, bf16[1,2]{1,0:T(2,128)(2,1)S(1)}, u32[]{:S(2)}, u32[]{:S(2)}) collective-permute-start(bf16[1,2]{1,0:T(2,128)(2,1)S(1)} %get-tuple-element.212), channel_id=1, source_target_pairs={{0,1},{1,2},{2,3},{3,4},{4,5},{5,6},{6,7},{8,9},{9,10},{10,11},{11... | collective-permute-start | bytes 20 | tf_op jit(solution)/shard_map/ppermute | solution.py:1496
  244.8 0.7 copy-start.22
  244.8 130.1 %copy-start.1 = (f32[1024,128]{1,0:T(8,128)}, f32[1024,128]{1,0:T(8,128)S(1)}, u32[]{:S(2)}) copy-start(f32[1024,128]{1,0:T(8,128)S(1)} %fusion.68.bias_ref) | copy-start | bytes 1572868
  248.9 30.0 %copy-start.4 = (bf16[128,2688]{1,0:T(8,128)(2,1)}, bf16[128,2688]{1,0:T(8,128)(2,1)S(1)}, u32[]{:S(2)}) copy-start(bf16[128,2688]{1,0:T(8,128)(2,1)S(1)} %fusion.10.joined_ref.q_ref) | copy-start | bytes 2064388
  248.9 30.6 %copy-start.32 = (bf16[1,128,896]{2,1,0:T(8,128)(2,1)S(1)}, bf16[1,128,896]{2,1,0:T(8,128)(2,1)}, u32[]{:S(2)}) copy-start(bf16[1,128,896]{2,1,0:T(8,128)(2,1)} %param.22) | copy-start | bytes 688132
  275.6 4.8 copy-start
  275.6 4.8 copy-start.6
  275.6 4.8 copy-start.7
  280.5 4.5 copy-start.23
  287.5 3.0 copy-start.11
  316.0 0.7 copy-start.24
  316.7 31.2 %copy-start.9 = (f32[128,896]{1,0:T(8,128)S(1)}, f32[128,896]{1,0:T(8,128)}, u32[]{:S(2)}) copy-start(f32[128,896]{1,0:T(8,128)} %get-tuple-element.87) | copy-start | bytes 1376260
  346.1 1.9 copy-start.2
  348.0 12.4 %copy-start.5 = (bf16[128,896]{1,0:T(8,128)(2,1)}, bf16[128,896]{1,0:T(8,128)(2,1)S(1)}, u32[]{:S(2)}) copy-start(bf16[128,896]{1,0:T(8,128)(2,1)S(1)} %get-tuple-element.88.refs_10_) | copy-start | bytes 688132
  372.8 29.7 %copy-start.26 = (bf16[128,896]{1,0:T(8,128)(2,1)}, bf16[128,896]{1,0:T(8,128)(2,1)S(1)}, u32[]{:S(2)}) copy-start(bf16[128,896]{1,0:T(8,128)(2,1)S(1)} %convert_element_type.103.refs_11_) | copy-start | bytes 688132
  375.0 2.0 copy-start.3
  402.6 4.2 copy-start.16
  402.6 4.2 copy-start.14
  431.0 2.3 copy-start.13
  449.3 1.5 copy-start.8
  449.3 2.0 copy-start.10
  454.0 4.4 copy-start.37
  454.0 4.4 copy-start.36
  454.0 4.4 copy-start.31
  454.0 4.5 copy-start.27
  457.1 3.7 collective-permute-start.2
  480.1 17.1 %copy-start.38 = (f32[1,896]{1,0:T(1,128)S(1)}, f32[1,896]{1,0:T(1,128)}, u32[]{:S(2)}) copy-start(f32[1,896]{1,0:T(1,128)} %get-tuple-element.134) | copy-start | bytes 10756
  499.8 4.9 copy-start.15
  805.4 6.5 copy-start.20
  807.6 5.8 copy-start.19
  811.9 3.7 copy-start.18
  813.4 3.7 copy-start.17
  814.9 3.7 copy-start.28
  817.0 2.5 copy-start.35
  817.0 3.1 copy-start.30
  817.0 3.8 copy-start.34
  (2 other events, 1.4 us)
Sparse Core Ops, SparseCore 0:
  237.4 110.4 all-gather.2
  449.4 49.2 reduce-scatter.1

commit v6 on v5

--- a/solution.py
+++ b/solution.py
@@ -512,10 +512,12 @@
     )
 
 
-ORDERS = ((1, False), (2, False), (1, True), (2, False), (1, False), (2, True))
+YZX_SUM, XZY_SUM, YXZ_SUM, XYZ_SUM = (1, False), (2, False), (1, True), (2, True)
+ORDERS = (YZX_SUM, XZY_SUM, YZX_SUM, XZY_SUM, YXZ_SUM, XZY_SUM, YZX_SUM, XYZ_SUM, YZX_SUM, XZY_SUM, YXZ_SUM)
+ORDERS += (XZY_SUM, YZX_SUM, XYZ_SUM, YZX_SUM, XZY_SUM, YXZ_SUM, XYZ_SUM, YZX_SUM, XYZ_SUM, YXZ_SUM, XYZ_SUM)
 CORE, HEAVY, ZED, PAIR, CORE_AGAIN, PER_PIECE = 0, 1, 2, 8, 9, 10
-START = (0, 1, 4, 6, 7, 8, 9, 10, 11)
-SLOTS = dict(part=2, whole=5, half=8, sibling=3, heavy=8, middle=8, last=8, zed=6, final=4)
+START = (0, 1, 4, 6, 7, 8, 10, 11, 12)
+SLOTS = dict(part=2, whole=5, half=8, sibling=3, heavy=8, middle=8, last=8, zed=7, final=4)
 
 
 def gradient_pieces():
@@ -839,9 +841,8 @@
                 else:
                     if step == 1:
                         sums.add_core(number)
-                    turn = lax.rem(number, len(ORDERS))
                     for order in sorted(set(ORDERS)):
-                        here = functools.reduce(jnp.logical_or, [turn == k for k, one in enumerate(ORDERS) if one == order])
+                        here = functools.reduce(jnp.logical_or, [number == k for k, one in enumerate(ORDERS) if one == order])
 
                         @pl.when(here)
                         def _():

time: 839 us -> 821 us (0.979)
  Pallas kernels: 703 us -> 685 us
    pallas_call x1, Pallas kernels: 300 us -> 281 us  [reduce_gradients(): pl.pallas_call(functools.partial(reduce_kernel, sizes, tall), out_shape=[...]
  transfers between devices with their start and end apart: 5 -> 5, of which waited for: 2 -> 2; matrix products, arithmetic and copies ran while one was open for 6% -> 6% of each run, Pallas kernels for 12% -> 13%
where the time goes in v6:
time: 821 us; the launch traced here: 810 us
  Pallas kernels  685 us (83%)
  matrix products  48.1 us (6%)
  local copies, waits for them, and re-layouts  35.7 us (4%)
  other arithmetic  17.5 us (2%)
  between operations  15.2 us (2%)
    pallas_call x1, Pallas kernels, reduce_gradients(): pl.pallas_call(functools.partial(reduce_kernel, sizes, tall), out_shape=[...  281 us
    pallas_call x1, Pallas kernels, gather_weights(): pl.pallas_call(functools.partial(gather_kernel, sizes), out_shape=out_sha...  223 us
    pallas_call x2, Pallas kernels, attend_gather(): pl.pallas_call(attend_gather_kernel, out_shape=[jax.ShapeDtypeStruct((row...  52.7 us
    dot_general x16, matrix products, dot(): lax.dot_general(left, right, dims, preferred_element_type=jnp.float32)  48.1 us
    pallas_call x3, Pallas kernels, ffn_back(): pl.pallas_call(ffn_back_kernel, grid=(FF // block,), out_shape=[jax.Shape...  42.7 us
    unnamed x108, local copies, waits for them, and re-layouts  27.8 us
    pallas_call x1, Pallas kernels, attend_scatter(): pl.pallas_call(attend_scatter_kernel, out_shape=[jax.ShapeDtypeStruct((ro...  25.5 us
    pallas_call x2, Pallas kernels, attend_back(): pl.pallas_call(attend_back_kernel, grid=(pairs,), out_shape=[jax.ShapeDty...  21.6 us
  transfers between devices with their start and end apart: 5, of which 2 were waited for; matrix products, arithmetic and copies ran while one was open for 6% of the time, Pallas kernels for 13%

profile of v6, /device:TPU:0, one launch (start us, length us, event | category | flops | bytes accessed | tf_op | source)
XLA Modules:
  0.0 810.3 jit_solution(282642829538585398)
XLA Ops:
  7.3 1.9 copy.70.refs_0_
  9.2 1.7 copy.71.refs_2_
  10.9 1.6 copy.72.refs_3_
  14.0 223.2 %gather_weights.1 = (bf16[4,2,2,56,3584]{4,3,2,1,0:T(8,128)(2,1)}, bf16[4,2,2,56,3584]{4,3,2,1,0:T(8,128)(2,1)}, bf16[4,2,2,56,10752]{4,3,2,1,0:T(8,128)(2,1)}, ...) custom-call(bf16[2,28,3584]{2,1,0:T(8,128)(2,1)} %copy.70.refs_0_, ...), custom_call_target="tpu_custom_call" | custom-call | tf_op jit(solution)/shard_map/gather_weights/pallas_call | solution.py:466
  237.3 2.1 slice_bitcast_fusion.2
  239.4 3.0 collective-permute-start.1
  242.5 1.8 collective-permute-start
  245.5 3.5 fusion.10.joined_ref.q_ref
  249.0 26.6 %attend_gather.2 = (bf16[128,896]{1,0:T(8,128)(2,1)S(1)}, f32[7,2,128]{2,1,0:T(2,128)S(1)}, bf16[2,2,2,128,1792]{4,3,2,1,0:T(8,128)(2,1)S(1)}) custom-call(bf16[128,2688]{1,0:T(8,128)(2,1)S(1)} %fusion.10.joined_ref.q_ref, f32[1024,128]{1,0:T(8,128)S(1)} %fusion.68.bias_ref), custom_call_target="tpu_custom_call" | custom-call | tf_op jit(solution)/shard_map/attend_gather/pallas_call | solution.py:1120
  275.7 3.2 multiply_reduce_fusion.7
  280.5 2.6 fusion.53.q_ref
  283.1 1.8 select_convert_fusion.spread_ref
  287.6 3.0 convolution_convert_fusion
  290.5 2.6 convolution_convert_fusion.1
  294.5 8.9 %attend.1 = (bf16[128,896]{1,0:T(8,128)(2,1)}, f32[7,2,128]{2,1,0:T(2,128)}) custom-call(bf16[128,896]{1,0:T(8,128)(2,1)} %fusion.53.q_ref, bf16[512,1792]{1,0:T(8,128)(2,1)} %pad_maximum_fusion.k_ref.v_ref, bf16[512,1792]{1,0:T(8,128)(2,1)} %pad_maximum_fusion.k_ref.v_ref, f32[512,128]{1,0:T(8,128)} %fusion.78.bias_ref), custom_call_target="tpu_custom_call" | custom-call | flops 469762048 | bytes 1835008 | tf_op jit(solution)/shard_map/attend/pallas_call | solution.py:946
  303.4 2.8 fusion.44.stream_ref
  306.2 7.5 ffn.1
  316.7 3.3 fusion.13.joined_ref
  320.1 26.0 %attend_gather.3 = (bf16[128,896]{1,0:T(8,128)(2,1)S(1)}, f32[7,2,128]{2,1,0:T(2,128)S(1)}, bf16[2,2,2,128,1792]{4,3,2,1,0:T(8,128)(2,1)S(1)}) custom-call(bf16[128,2688]{1,0:T(8,128)(2,1)S(1)} %fusion.13.joined_ref, f32[1024,128]{1,0:T(8,128)S(1)} %fusion.68.bias_ref), custom_call_target="tpu_custom_call" | custom-call | tf_op jit(solution)/shard_map/attend_gather/pallas_call | solution.py:1120
  346.1 1.9 copy-done.2
  348.0 2.7 fusion.47.stream_ref
  350.7 9.7 %late_ffn.1 = (f32[128,896]{1,0:T(8,128)}, bf16[128,896]{1,0:T(8,128)(2,1)}, bf16[128,3584]{1,0:T(8,128)(2,1)}, bf16[128,3584]{1,0:T(8,128)(2,1)}) custom-call(f32[128,896]{1,0:T(8,128)} %fusion.47.stream_ref, bf16[1,896]{1,0:T(2,128)(2,1)} %get-tuple-element.209.gain_ref, bf16[896,1024]{1,0:T(8,128)(2,1)} %select_convert_fusion.spread_ref, ...), custom_call_target="tpu_custom_call" | custom-call | flops 1644167168 | bytes 16056320 | tf_op jit(solution)/shard_map/late_ffn/pallas_call | solution.py:1416
  360.4 11.4 %late_ffn_back.1 = (f32[128,896]{1,0:T(8,128)}, bf16[128,896]{1,0:T(8,128)(2,1)}, bf16[128,3584]{1,0:T(8,128)(2,1)}, f32[1,896]{1,0:T(1,128)}) custom-call(f32[128,896]{1,0:T(8,128)} %bitcast_convert_fusion.grad_ref, f32[128,896]{1,0:T(8,128)} %fusion.47.stream_ref, bf16[1,896]{1,0:T(2,128)(2,1)} %get-tuple-element.209.gain_ref, ...), custom_call_target="tpu_custom_call" | custom-call | flops 1644167168 | bytes 16056320 | tf_op jit(solution)/shard_map/late_ffn_back/pallas_call | solution.py:1465
  372.8 2.1 fusion.59.grad_ref
  375.0 2.0 copy-done.3
  377.0 25.5 %attend_scatter.1 = (bf16[128,896]{1,0:T(8,128)(2,1)S(1)}, bf16[128,1792]{1,0:T(8,128)(2,1)S(1)}) custom-call(bf16[128,2688]{1,0:T(8,128)(2,1)S(1)} %fusion.13.joined_ref, bf16[2,2,2,128,1792]{4,3,2,1,0:T(8,128)(2,1)S(1)} %copy-done.3, f32[1024,128]{1,0:T(8,128)S(1)} %fusion.68.bias_ref, f32[7,2,128]{2,1,0:T(2,128)S(1)} %get-tuple-element.94.total_ref, ...), custom_call_target="tpu_custom_call" | custom-call | tf_op jit(solution)/shard_map/attend_scatter/pallas_call | solution.py:1223
  402.6 4.2 multiply_reduce_fusion.3
  407.7 9.5 %ffn_back.3 = (f32[128,896]{1,0:T(8,128)}, bf16[128,896]{1,0:T(8,128)(2,1)}, bf16[128,3584]{1,0:T(8,128)(2,1)}, f32[1,896]{1,0:T(1,128)}) custom-call(f32[128,896]{1,0:T(8,128)} %multiply_add_fusion.1.grad_ref, f32[128,896]{1,0:T(8,128)} %fusion.44.stream_ref, bf16[1,896]{1,0:T(2,128)(2,1)} %get-tuple-element.210.gain_ref, ...), custom_call_target="tpu_custom_call" | custom-call | flops 1644167168 | bytes 16515072 | tf_op jit(solution)/shard_map/ffn_back/pallas_call | solution.py:1339
  419.1 2.7 fusion.56.grad_ref
  421.8 9.2 %attend_back.2 = (bf16[128,896]{1,0:T(8,128)(2,1)}, bf16[512,1792]{1,0:T(8,128)(2,1)}) custom-call(bf16[128,896]{1,0:T(8,128)(2,1)} %fusion.53.q_ref, bf16[512,1792]{1,0:T(8,128)(2,1)} %pad_maximum_fusion.k_ref.v_ref, bf16[512,1792]{1,0:T(8,128)(2,1)} %pad_maximum_fusion.k_ref.v_ref, f32[512,128]{1,0:T(8,128)} %fusion.78.bias_ref, ...), custom_call_target="tpu_custom_call" | custom-call | flops 1174405120 | bytes 3670016 | tf_op jit(solution)/shard_map/attend_back/pallas_call | solution.py:987
  431.0 2.3 multiply_reduce_fusion.2
  434.2 2.7 fusion.50.grad_ref
  436.9 12.4 %attend_back.3 = (bf16[128,896]{1,0:T(8,128)(2,1)}, bf16[1024,1792]{1,0:T(8,128)(2,1)}) custom-call(bf16[128,2688]{1,0:T(8,128)(2,1)} %copy-done.4, bf16[1024,1792]{1,0:T(8,128)(2,1)} %bitcast.78, bf16[1024,1792]{1,0:T(8,128)(2,1)} %bitcast.79, f32[1024,128]{1,0:T(8,128)} %copy-done.1, f32[7,2,128]{2,1,0:T(2,128)} %copy-done.7, bf16[128,896]{1,0:T(8,128)(2,1)} %fusion.50.grad_ref), custom_call_target="tpu_custom_call" | custom-call | flops 2348810240 | bytes 7340032 | tf_op jit(solution)/shard_map/attend_back/pallas_call | solution.py:987
  451.4 2.6 fusion.27
  454.1 3.0 convolution_add_fusion
  459.3 1.5 collective-permute-done.2
  461.6 1.7 subtract_multiply_fusion.grad_ref
  463.3 16.8 %ffn_back.4 = (f32[512,896]{1,0:T(8,128)}, bf16[512,896]{1,0:T(8,128)(2,1)}, bf16[512,3584]{1,0:T(8,128)(2,1)}, f32[1,896]{1,0:T(1,128)}) custom-call(f32[512,896]{1,0:T(8,128)} %subtract_multiply_fusion.grad_ref, f32[512,896]{1,0:T(8,128)} %get-tuple-element.116.stream_ref, bf16[1,896]{1,0:T(2,128)(2,1)} %get-tuple-element.211.gain_ref, ...), custom_call_target="tpu_custom_call" | custom-call | flops 6576668672 | bytes 27525120 | tf_op jit(solution)/shard_map/ffn_back/pallas_call | solution.py:1339
  480.1 16.5 %ffn_back.5 = (f32[512,896]{1,0:T(8,128)}, bf16[512,896]{1,0:T(8,128)(2,1)}, bf16[512,3584]{1,0:T(8,128)(2,1)}, f32[1,896]{1,0:T(1,128)}) custom-call(f32[512,896]{1,0:T(8,128)} %get-tuple-element.120.grad_ref, bf16[512,896]{1,0:T(8,128)(2,1)} %bitcast.108, bf16[1,896]{1,0:T(2,128)(2,1)} %get-tuple-element.208.gain_ref, ...), custom_call_target="tpu_custom_call" | custom-call | flops 6576668672 | bytes 27525120 | tf_op jit(solution)/shard_map/ffn_back/pallas_call | solution.py:1339
  497.2 1.5 reduce-scatter.2.cloned.1.call-done
  499.8 4.8 fusion.75
  505.7 281.4 %reduce_gradients.1 = (f32[2,28,3584]{2,1,0:T(8,128)}, f32[2,28,3584]{2,1,0:T(8,128)}, f32[2,28,2688]{2,1,0:T(8,128)}, f32[2,28,896]{2,1,0:T(8,128)}, f32[2,28,3...) custom-call(bf16[128,896]{1,0:T(8,128)(2,1)} %copy-done.22, ...), custom_call_target="tpu_custom_call" | custom-call | tf_op jit(solution)/shard_map/reduce_gradients/pallas_call | solution.py:890
  789.4 2.5 copy.77
  791.8 1.8 copy.78
  793.6 1.5 copy.79
  795.1 1.5 copy.80
  797.3 1.5 copy.82
  798.8 1.5 copy.83
  (173 shorter events, 29.7 us)
Async XLA Ops:
  7.2 5.3 copy-start.29
  7.2 6.1 copy-start.41
  7.2 6.1 copy-start.42
  7.2 6.1 copy-start.43
  7.2 6.1 copy-start.40
  7.2 343.5 %all-gather.3.cloned.1.call-start = ((), (), s32[]{:S(2)}) async-start(), calls=%async_computation.2 | async-start | bytes 15138816 | tf_op jit(solution)/shard_map/all_gather | solution.py:500
  237.2 5.2 copy-start.39
  237.2 5.2 copy-start.44
  237.2 7.0 copy-start.33
  237.2 7.2 copy-start.12
  237.3 261.5 %reduce-scatter.2.cloned.1.call-start = ((), (), s32[]{:S(2)}) async-start(), calls=%async_computation.1 | async-start | bytes 4128768 | tf_op jit(solution)/shard_map/reduce_scatter | solution.py:1531
  239.4 47.0 %collective-permute-start.1 = (bf16[1,256,896]{2,1,0:T(8,128)(2,1)}, bf16[1,256,896]{2,1,0:T(8,128)(2,1)}, u32[]{:S(2)}, u32[]{:S(2)}) collective-permute-start(bf16[1,256,896]{2,1,0:T(8,128)(2,1)} %get-tuple-element.206), channel_id=1, source_target_pairs={{0,1},{1,2},{2,3},{3,4},{4,5},{5,6},{6,7},{8,9},{9,10},{10,11},{11... | collective-permute-start | bytes 1376264 | tf_op jit(solution)/shard_map/ppermute | solution.py:1497
  242.5 42.4 %collective-permute-start = (bf16[1,2]{1,0:T(2,128)(2,1)S(1)}, bf16[1,2]{1,0:T(2,128)(2,1)S(1)}, u32[]{:S(2)}, u32[]{:S(2)}) collective-permute-start(bf16[1,2]{1,0:T(2,128)(2,1)S(1)} %get-tuple-element.212), channel_id=1, source_target_pairs={{0,1},{1,2},{2,3},{3,4},{4,5},{5,6},{6,7},{8,9},{9,10},{10,11},{11... | collective-permute-start | bytes 20 | tf_op jit(solution)/shard_map/ppermute | solution.py:1497
  244.8 0.7 copy-start.22
  244.8 130.1 %copy-start.1 = (f32[1024,128]{1,0:T(8,128)}, f32[1024,128]{1,0:T(8,128)S(1)}, u32[]{:S(2)}) copy-start(f32[1024,128]{1,0:T(8,128)S(1)} %fusion.68.bias_ref) | copy-start | bytes 1572868
  248.9 30.0 %copy-start.4 = (bf16[128,2688]{1,0:T(8,128)(2,1)}, bf16[128,2688]{1,0:T(8,128)(2,1)S(1)}, u32[]{:S(2)}) copy-start(bf16[128,2688]{1,0:T(8,128)(2,1)S(1)} %fusion.10.joined_ref.q_ref) | copy-start | bytes 2064388
  248.9 30.6 %copy-start.32 = (bf16[1,128,896]{2,1,0:T(8,128)(2,1)S(1)}, bf16[1,128,896]{2,1,0:T(8,128)(2,1)}, u32[]{:S(2)}) copy-start(bf16[1,128,896]{2,1,0:T(8,128)(2,1)} %param.22) | copy-start | bytes 688132
  275.6 4.8 copy-start
  275.6 4.8 copy-start.6
  275.6 4.8 copy-start.7
  280.5 4.5 copy-start.23
  287.5 3.0 copy-start.11
  316.0 0.7 copy-start.24
  316.7 31.2 %copy-start.9 = (f32[128,896]{1,0:T(8,128)S(1)}, f32[128,896]{1,0:T(8,128)}, u32[]{:S(2)}) copy-start(f32[128,896]{1,0:T(8,128)} %get-tuple-element.87) | copy-start | bytes 1376260
  346.1 1.9 copy-start.2
  348.0 12.4 %copy-start.5 = (bf16[128,896]{1,0:T(8,128)(2,1)}, bf16[128,896]{1,0:T(8,128)(2,1)S(1)}, u32[]{:S(2)}) copy-start(bf16[128,896]{1,0:T(8,128)(2,1)S(1)} %get-tuple-element.88.refs_10_) | copy-start | bytes 688132
  372.8 29.7 %copy-start.26 = (bf16[128,896]{1,0:T(8,128)(2,1)}, bf16[128,896]{1,0:T(8,128)(2,1)S(1)}, u32[]{:S(2)}) copy-start(bf16[128,896]{1,0:T(8,128)(2,1)S(1)} %convert_element_type.103.refs_11_) | copy-start | bytes 688132
  375.0 2.0 copy-start.3
  402.6 4.2 copy-start.16
  402.6 4.2 copy-start.14
  431.0 2.3 copy-start.13
  449.3 1.5 copy-start.8
  449.3 2.0 copy-start.10
  454.0 4.4 copy-start.37
  454.0 4.4 copy-start.36
  454.0 4.4 copy-start.31
  454.0 4.5 copy-start.27
  457.1 3.7 collective-permute-start.2
  480.1 17.1 %copy-start.38 = (f32[1,896]{1,0:T(1,128)S(1)}, f32[1,896]{1,0:T(1,128)}, u32[]{:S(2)}) copy-start(f32[1,896]{1,0:T(1,128)} %get-tuple-element.134) | copy-start | bytes 10756
  499.8 4.9 copy-start.15
  787.1 6.5 copy-start.20
  789.4 5.8 copy-start.19
  793.6 3.7 copy-start.18
  795.1 3.7 copy-start.17
  796.6 3.7 copy-start.28
  798.8 2.5 copy-start.35
  798.8 3.1 copy-start.30
  798.8 3.8 copy-start.34
  (2 other events, 1.4 us)
Sparse Core Ops, SparseCore 0:
  237.4 110.4 all-gather.2
  449.4 49.2 reduce-scatter.1

commit v7 on v6

--- a/solution.py
+++ b/solution.py
@@ -910,6 +910,10 @@
     )(*operands, gains.reshape(lead + (128,)))
 
 
+def whole_block(shape):
+    return pl.BlockSpec(shape, lambda *_: (0,) * len(shape))
+
+
 NN = (((1,), (0,)), ((), ()))
 NT = (((1,), (1,)), ((), ()))
 TN = (((0,), (0,)), ((), ()))
@@ -925,19 +929,21 @@
     return [jnp.where(lane < HEAD, values, zero), jnp.where(lane >= HEAD, values, zero)]
 
 
-def attend_kernel(q_ref, k_ref, v_ref, bias_ref, out_ref, total_ref):
-    keys, vals = k_ref[...], v_ref[...]
-    outs = []
-    for side, queries in enumerate(head_sides(q_ref[...])):
-        scores = dot(keys, queries, NT) * SCORE_SCALE + bias_ref[...]
-        peak = jnp.max(scores, 0, keepdims=True)
-        powers = jnp.exp(scores - peak)
-        total = jnp.sum(powers, 0, keepdims=True)
-        total_ref[0, side : side + 1, :] = peak + jnp.log(total)
-        probs = (powers * (1.0 / total)).astype(BF)
-        outs.append(dot(probs, vals, TN))
-    lane = lax.broadcasted_iota(jnp.int32, outs[0].shape, 1)
-    out_ref[...] = jnp.where(lane < HEAD, outs[0], outs[1]).astype(BF)
+def attend_kernel(q_ref, kv_ref, bias_ref, out_ref, total_ref):
+    bias = bias_ref[...]
+    for pair in range(D // 128):
+        columns = pl.ds(128 * pair, 128)
+        keys, vals = kv_ref[:, columns], kv_ref[:, pl.ds(D + 128 * pair, 128)]
+        outs = []
+        for side, queries in enumerate(head_sides(q_ref[:, columns])):
+            scores = dot(keys, queries, NT) * SCORE_SCALE + bias
+            peak = jnp.max(scores, 0, keepdims=True)
+            powers = jnp.exp(scores - peak)
+            total = jnp.sum(powers, 0, keepdims=True)
+            total_ref[pair, side : side + 1, :] = peak + jnp.log(total)
+            outs.append(dot((powers * (1.0 / total)).astype(BF), vals, TN))
+        lane = lax.broadcasted_iota(jnp.int32, outs[0].shape, 1)
+        out_ref[:, columns] = jnp.where(lane < HEAD, outs[0], outs[1]).astype(BF)
 
 
 def attend(joined, keys_vals, bias):
@@ -945,63 +951,52 @@
     pairs = D // 128
     return pl.pallas_call(
         attend_kernel,
-        grid=(pairs,),
         out_shape=[jax.ShapeDtypeStruct((queries, D), BF), jax.ShapeDtypeStruct((pairs, 2, queries), jnp.float32)],
-        in_specs=[
-            pl.BlockSpec((queries, 128), lambda p: (0, p)),
-            pl.BlockSpec((keys, 128), lambda p: (0, p)),
-            pl.BlockSpec((keys, 128), lambda p: (0, pairs + p)),
-            pl.BlockSpec((keys, queries), lambda p: (0, 0)),
-        ],
-        out_specs=[pl.BlockSpec((queries, 128), lambda p: (0, p)), pl.BlockSpec((1, 2, queries), lambda p: (p, 0, 0))],
+        grid=(1,),
+        in_specs=[whole_block((queries, D))] + [whole_block(v.shape) for v in (keys_vals, bias)],
+        out_specs=[whole_block((queries, D)), whole_block((pairs, 2, queries))],
         cost_estimate=pl.CostEstimate(
             flops=4 * queries * keys * D * 2, bytes_accessed=2 * keys * 2 * D, transcendentals=14 * queries * keys
         ),
         name="attend",
-    )(joined, keys_vals, keys_vals, bias)
-
-
-def attend_back_kernel(q_ref, k_ref, v_ref, bias_ref, total_ref, grad_ref, gq_ref, gkv_ref):
-    pair = pl.program_id(0)
-    keys, vals = k_ref[...], v_ref[...]
-    q_sides, g_sides = head_sides(q_ref[...]), head_sides(grad_ref[...])
-    grad_q, grad_k, grad_v = [], 0.0, 0.0
-    for side in range(2):
-        scores = dot(keys, q_sides[side], NT) * SCORE_SCALE + bias_ref[...]
-        probs = jnp.exp(scores - total_ref[0, side : side + 1, :])
-        grad_probs = dot(vals, g_sides[side], NT)
-        delta = jnp.sum(probs * grad_probs, 0, keepdims=True)
-        grad_scores = (probs * (grad_probs - delta)).astype(BF)
-        grad_v = grad_v + dot(probs.astype(BF), g_sides[side], NN)
-        grad_k = grad_k + dot(grad_scores, q_sides[side], NN)
-        grad_q.append(dot(grad_scores, keys, TN))
-    lane = lax.broadcasted_iota(jnp.int32, grad_q[0].shape, 1)
-    gq_ref[...] = (jnp.where(lane < HEAD, grad_q[0], grad_q[1]) * SCORE_SCALE).astype(BF)
-    gkv_ref[:, pl.ds(pl.multiple_of(pair * 128, 128), 128)] = (grad_k * SCORE_SCALE).astype(BF)
-    gkv_ref[:, pl.ds(pl.multiple_of(D + pair * 128, 128), 128)] = grad_v.astype(BF)
+    )(joined, keys_vals, bias)
+
+
+def attend_back_kernel(q_ref, kv_ref, bias_ref, total_ref, grad_ref, gq_ref, gkv_ref):
+    bias = bias_ref[...]
+    for pair in range(D // 128):
+        columns, beside = pl.ds(128 * pair, 128), pl.ds(D + 128 * pair, 128)
+        keys, vals = kv_ref[:, columns], kv_ref[:, beside]
+        q_sides, g_sides = head_sides(q_ref[:, columns]), head_sides(grad_ref[:, columns])
+        grad_q, grad_k, grad_v = [], 0.0, 0.0
+        for side in range(2):
+            scores = dot(keys, q_sides[side], NT) * SCORE_SCALE + bias
+            probs = jnp.exp(scores - total_ref[pair, side : side + 1, :])
+            grad_probs = dot(vals, g_sides[side], NT)
+            delta = jnp.sum(probs * grad_probs, 0, keepdims=True)
+            grad_scores = (probs * (grad_probs - delta)).astype(BF)
+            grad_v = grad_v + dot(probs.astype(BF), g_sides[side], NN)
+            grad_k = grad_k + dot(grad_scores, q_sides[side], NN)
+            grad_q.append(dot(grad_scores, keys, TN))
+        lane = lax.broadcasted_iota(jnp.int32, grad_q[0].shape, 1)
+        gq_ref[:, columns] = (jnp.where(lane < HEAD, grad_q[0], grad_q[1]) * SCORE_SCALE).astype(BF)
+        gkv_ref[:, columns] = (grad_k * SCORE_SCALE).astype(BF)
+        gkv_ref[:, beside] = grad_v.astype(BF)
 
 
 def attend_back(joined, keys_vals, bias, log_total, grad_mixed):
     queries, keys = joined.shape[0], keys_vals.shape[0]
-    pairs = D // 128
     return pl.pallas_call(
         attend_back_kernel,
-        grid=(pairs,),
         out_shape=[jax.ShapeDtypeStruct((queries, D), BF), jax.ShapeDtypeStruct((keys, 2 * D), BF)],
-        in_specs=[
-            pl.BlockSpec((queries, 128), lambda p: (0, p)),
-            pl.BlockSpec((keys, 128), lambda p: (0, p)),
-            pl.BlockSpec((keys, 128), lambda p: (0, pairs + p)),
-            pl.BlockSpec((keys, queries), lambda p: (0, 0)),
-            pl.BlockSpec((1, 2, queries), lambda p: (p, 0, 0)),
-            pl.BlockSpec((queries, 128), lambda p: (0, p)),
-        ],
-        out_specs=[pl.BlockSpec((queries, 128), lambda p: (0, p)), pl.BlockSpec((keys, 2 * D), lambda p: (0, 0))],
+        grid=(1,),
+        in_specs=[whole_block((queries, D))] + [whole_block(v.shape) for v in (keys_vals, bias, log_total, grad_mixed)],
+        out_specs=[whole_block((queries, D)), whole_block((keys, 2 * D))],
         cost_estimate=pl.CostEstimate(
             flops=10 * queries * keys * D * 2, bytes_accessed=4 * keys * 2 * D, transcendentals=14 * queries * keys
         ),
         name="attend_back",
-    )(joined, keys_vals, keys_vals, bias, log_total, grad_mixed)
+    )(joined, keys_vals, bias, log_total, grad_mixed)
 
 
 PAIR_GROUPS = (((0, 1), (2, 1)), ((2, 3), (1, 2)), ((4, 5), (2, 1)), ((6,), (1, 2)))
@@ -1106,10 +1101,6 @@
     compute(count - 2)
     compute(count - 1)
     keep.wait()
-
-
-def whole_block(shape):
-    return pl.BlockSpec(shape, lambda: (0,) * len(shape))
 
 
 def attend_gather(joined, bias):

time: 821 us -> 817 us (level)
    unnamed x108 -> x110, local copies, waits for them, and re-layouts: 27.8 us -> 26.4 us
  transfers between devices with their start and end apart: 5 -> 5, of which waited for: 2 -> 3; matrix products, arithmetic and copies ran while one was open for 6% -> 6% of each run, Pallas kernels for 13% -> 13%
where the time goes in v7:
time: 817 us; the launch traced here: 807 us
  Pallas kernels  683 us (84%)
  matrix products  48.2 us (6%)
  local copies, waits for them, and re-layouts  34.4 us (4%)
  other arithmetic  17.5 us (2%)
  between operations  15.1 us (2%)
    pallas_call x1, Pallas kernels, reduce_gradients(): pl.pallas_call(functools.partial(reduce_kernel, sizes, tall), out_shape=[...  282 us
    pallas_call x1, Pallas kernels, gather_weights(): pl.pallas_call(functools.partial(gather_kernel, sizes), out_shape=out_sha...  223 us
    pallas_call x2, Pallas kernels, attend_gather(): pl.pallas_call(attend_gather_kernel, out_shape=[jax.ShapeDtypeStruct((row...  55.8 us
    dot_general x16, matrix products, dot(): lax.dot_general(left, right, dims, preferred_element_type=jnp.float32)  48.2 us
    pallas_call x3, Pallas kernels, ffn_back(): pl.pallas_call(ffn_back_kernel, grid=(FF // block,), out_shape=[jax.Shape...  42.6 us
    unnamed x110, local copies, waits for them, and re-layouts  26.4 us
    pallas_call x1, Pallas kernels, attend_scatter(): pl.pallas_call(attend_scatter_kernel, out_shape=[jax.ShapeDtypeStruct((ro...  26 us
    pallas_call x2, Pallas kernels, attend_back(): pl.pallas_call(attend_back_kernel, out_shape=[jax.ShapeDtypeStruct((queri...  20.1 us
  transfers between devices with their start and end apart: 5, of which 3 were waited for; matrix products, arithmetic and copies ran while one was open for 6% of the time, Pallas kernels for 13%

profile of v7, /device:TPU:0, one launch (start us, length us, event | category | flops | bytes accessed | tf_op | source)
XLA Modules:
  0.0 807.1 jit_solution(1536391332423914659)
XLA Ops:
  7.3 1.9 copy.70.refs_0_
  9.2 1.7 copy.71.refs_2_
  10.9 1.6 copy.72.refs_3_
  14.0 223.3 %gather_weights.1 = (bf16[4,2,2,56,3584]{4,3,2,1,0:T(8,128)(2,1)}, bf16[4,2,2,56,3584]{4,3,2,1,0:T(8,128)(2,1)}, bf16[4,2,2,56,10752]{4,3,2,1,0:T(8,128)(2,1)}, ...) custom-call(bf16[2,28,3584]{2,1,0:T(8,128)(2,1)} %copy.70.refs_0_, ...), custom_call_target="tpu_custom_call" | custom-call | tf_op jit(solution)/shard_map/gather_weights/pallas_call | solution.py:466
  237.4 2.1 slice_bitcast_fusion.2
  239.5 3.0 collective-permute-start.1
  242.6 1.8 collective-permute-start
  245.6 3.5 fusion.10.joined_ref.q_ref
  249.1 26.5 %attend_gather.2 = (bf16[128,896]{1,0:T(8,128)(2,1)S(1)}, f32[7,2,128]{2,1,0:T(2,128)S(1)}, bf16[2,2,2,128,1792]{4,3,2,1,0:T(8,128)(2,1)S(1)}) custom-call(bf16[128,2688]{1,0:T(8,128)(2,1)S(1)} %fusion.10.joined_ref.q_ref, f32[1024,128]{1,0:T(8,128)S(1)} %fusion.68.bias_ref), custom_call_target="tpu_custom_call" | custom-call | tf_op jit(solution)/shard_map/attend_gather/pallas_call | solution.py:1111
  275.7 3.2 multiply_reduce_fusion.7
  280.5 2.6 fusion.53.q_ref
  283.1 1.8 select_convert_fusion.spread_ref
  287.6 3.0 convolution_convert_fusion
  290.5 2.6 convolution_convert_fusion.1
  294.5 4.8 attend.1
  299.3 2.8 fusion.44.stream_ref
  302.1 7.8 ffn.1
  312.2 3.4 fusion.13.joined_ref
  315.6 29.3 %attend_gather.3 = (bf16[128,896]{1,0:T(8,128)(2,1)S(1)}, f32[7,2,128]{2,1,0:T(2,128)S(1)}, bf16[2,2,2,128,1792]{4,3,2,1,0:T(8,128)(2,1)S(1)}) custom-call(bf16[128,2688]{1,0:T(8,128)(2,1)S(1)} %fusion.13.joined_ref, f32[1024,128]{1,0:T(8,128)S(1)} %fusion.68.bias_ref), custom_call_target="tpu_custom_call" | custom-call | tf_op jit(solution)/shard_map/attend_gather/pallas_call | solution.py:1111
  344.9 1.9 copy-done.1
  346.8 2.9 fusion.47.stream_ref
  350.1 9.7 %late_ffn.1 = (f32[128,896]{1,0:T(8,128)}, bf16[128,896]{1,0:T(8,128)(2,1)}, bf16[128,3584]{1,0:T(8,128)(2,1)}, bf16[128,3584]{1,0:T(8,128)(2,1)}) custom-call(f32[128,896]{1,0:T(8,128)} %fusion.47.stream_ref, bf16[1,896]{1,0:T(2,128)(2,1)} %get-tuple-element.209.gain_ref, bf16[896,1024]{1,0:T(8,128)(2,1)} %select_convert_fusion.spread_ref, ...), custom_call_target="tpu_custom_call" | custom-call | flops 1644167168 | bytes 16056320 | tf_op jit(solution)/shard_map/late_ffn/pallas_call | solution.py:1407
  359.8 11.5 %late_ffn_back.1 = (f32[128,896]{1,0:T(8,128)}, bf16[128,896]{1,0:T(8,128)(2,1)}, bf16[128,3584]{1,0:T(8,128)(2,1)}, f32[1,896]{1,0:T(1,128)}) custom-call(f32[128,896]{1,0:T(8,128)} %bitcast_convert_fusion.grad_ref, f32[128,896]{1,0:T(8,128)} %fusion.47.stream_ref, bf16[1,896]{1,0:T(2,128)(2,1)} %get-tuple-element.209.gain_ref, ...), custom_call_target="tpu_custom_call" | custom-call | flops 1644167168 | bytes 16056320 | tf_op jit(solution)/shard_map/late_ffn_back/pallas_call | solution.py:1456
  372.3 2.1 fusion.59.grad_ref
  374.4 2.0 copy-done.2
  376.4 26.0 %attend_scatter.1 = (bf16[128,896]{1,0:T(8,128)(2,1)S(1)}, bf16[128,1792]{1,0:T(8,128)(2,1)S(1)}) custom-call(bf16[128,2688]{1,0:T(8,128)(2,1)S(1)} %fusion.13.joined_ref, bf16[2,2,2,128,1792]{4,3,2,1,0:T(8,128)(2,1)S(1)} %copy-done.2, f32[1024,128]{1,0:T(8,128)S(1)} %fusion.68.bias_ref, f32[7,2,128]{2,1,0:T(2,128)S(1)} %get-tuple-element.94.total_ref, ...), custom_call_target="tpu_custom_call" | custom-call | tf_op jit(solution)/shard_map/attend_scatter/pallas_call | solution.py:1214
  402.5 4.2 multiply_reduce_fusion.3
  407.6 9.6 %ffn_back.3 = (f32[128,896]{1,0:T(8,128)}, bf16[128,896]{1,0:T(8,128)(2,1)}, bf16[128,3584]{1,0:T(8,128)(2,1)}, f32[1,896]{1,0:T(1,128)}) custom-call(f32[128,896]{1,0:T(8,128)} %multiply_add_fusion.1.grad_ref, f32[128,896]{1,0:T(8,128)} %fusion.44.stream_ref, bf16[1,896]{1,0:T(2,128)(2,1)} %get-tuple-element.210.gain_ref, ...), custom_call_target="tpu_custom_call" | custom-call | flops 1644167168 | bytes 16515072 | tf_op jit(solution)/shard_map/ffn_back/pallas_call | solution.py:1330
  419.0 2.7 fusion.56.grad_ref
  421.7 8.0 attend_back.2
  429.7 2.3 multiply_reduce_fusion.2
  432.3 2.8 fusion.50.grad_ref
  435.0 12.1 %attend_back.3 = (bf16[128,896]{1,0:T(8,128)(2,1)}, bf16[1024,1792]{1,0:T(8,128)(2,1)}) custom-call(bf16[128,2688]{1,0:T(8,128)(2,1)} %copy-done.4, bf16[1024,1792]{1,0:T(8,128)(2,1)} %bitcast.78, f32[1024,128]{1,0:T(8,128)} %copy-done, f32[7,2,128]{2,1,0:T(2,128)} %copy-done.7, bf16[128,896]{1,0:T(8,128)(2,1)} %fusion.50.grad_ref), custom_call_target="tpu_custom_call" | custom-call | flops 2348810240 | bytes 7340032 | tf_op jit(solution)/shard_map/attend_back/pallas_call | solution.py:989
  447.1 1.5 copy-done.8
  449.2 2.6 fusion.27
  451.9 2.7 convolution_add_fusion
  456.9 1.6 collective-permute-done.2
  459.3 1.7 subtract_multiply_fusion.grad_ref
  461.0 16.7 %ffn_back.4 = (f32[512,896]{1,0:T(8,128)}, bf16[512,896]{1,0:T(8,128)(2,1)}, bf16[512,3584]{1,0:T(8,128)(2,1)}, f32[1,896]{1,0:T(1,128)}) custom-call(f32[512,896]{1,0:T(8,128)} %subtract_multiply_fusion.grad_ref, f32[512,896]{1,0:T(8,128)} %get-tuple-element.116.stream_ref, bf16[1,896]{1,0:T(2,128)(2,1)} %get-tuple-element.211.gain_ref, ...), custom_call_target="tpu_custom_call" | custom-call | flops 6576668672 | bytes 27525120 | tf_op jit(solution)/shard_map/ffn_back/pallas_call | solution.py:1330
  477.7 16.3 %ffn_back.5 = (f32[512,896]{1,0:T(8,128)}, bf16[512,896]{1,0:T(8,128)(2,1)}, bf16[512,3584]{1,0:T(8,128)(2,1)}, f32[1,896]{1,0:T(1,128)}) custom-call(f32[512,896]{1,0:T(8,128)} %get-tuple-element.120.grad_ref, bf16[512,896]{1,0:T(8,128)(2,1)} %bitcast.107, bf16[1,896]{1,0:T(2,128)(2,1)} %get-tuple-element.208.gain_ref, ...), custom_call_target="tpu_custom_call" | custom-call | flops 6576668672 | bytes 27525120 | tf_op jit(solution)/shard_map/ffn_back/pallas_call | solution.py:1330
  496.4 4.8 fusion.75
  502.2 281.8 %reduce_gradients.1 = (f32[2,28,3584]{2,1,0:T(8,128)}, f32[2,28,3584]{2,1,0:T(8,128)}, f32[2,28,2688]{2,1,0:T(8,128)}, f32[2,28,896]{2,1,0:T(8,128)}, f32[2,28,3...) custom-call(bf16[128,896]{1,0:T(8,128)(2,1)} %copy-done.23, ...), custom_call_target="tpu_custom_call" | custom-call | tf_op jit(solution)/shard_map/reduce_gradients/pallas_call | solution.py:890
  786.2 2.5 copy.77
  788.7 1.8 copy.78
  790.5 1.5 copy.79
  792.0 1.5 copy.80
  794.2 1.5 copy.82
  795.7 1.5 copy.83
  (175 shorter events, 28.0 us)
Async XLA Ops:
  7.2 5.3 copy-start.30
  7.2 6.1 copy-start.42
  7.2 6.1 copy-start.43
  7.2 6.1 copy-start.44
  7.2 6.1 copy-start.41
  7.2 342.9 %all-gather.3.cloned.1.call-start = ((), (), s32[]{:S(2)}) async-start(), calls=%async_computation.2 | async-start | bytes 15138816 | tf_op jit(solution)/shard_map/all_gather | solution.py:500
  237.3 5.2 copy-start.40
  237.3 5.2 copy-start.45
  237.3 7.1 copy-start.34
  237.3 7.3 copy-start.12
  237.4 258.0 %reduce-scatter.2.cloned.1.call-start = ((), (), s32[]{:S(2)}) async-start(), calls=%async_computation.1 | async-start | bytes 4128768 | tf_op jit(solution)/shard_map/reduce_scatter | solution.py:1522
  239.5 47.0 %collective-permute-start.1 = (bf16[1,256,896]{2,1,0:T(8,128)(2,1)S(1)}, bf16[1,256,896]{2,1,0:T(8,128)(2,1)}, u32[]{:S(2)}, u32[]{:S(2)}) collective-permute-start(bf16[1,256,896]{2,1,0:T(8,128)(2,1)S(1)} %get-tuple-element.206), channel_id=1, source_target_pairs={{0,1},{1,2},{2,3},{3,4},{4,5},{5,6},{6,7},{8,9},{9,10},{10,11},{11... | collective-permute-start | bytes 1376264 | tf_op jit(solution)/shard_map/ppermute | solution.py:1488
  242.6 42.4 %collective-permute-start = (bf16[1,2]{1,0:T(2,128)(2,1)S(1)}, bf16[1,2]{1,0:T(2,128)(2,1)S(1)}, u32[]{:S(2)}, u32[]{:S(2)}) collective-permute-start(bf16[1,2]{1,0:T(2,128)(2,1)S(1)} %get-tuple-element.212), channel_id=1, source_target_pairs={{0,1},{1,2},{2,3},{3,4},{4,5},{5,6},{6,7},{8,9},{9,10},{10,11},{11... | collective-permute-start | bytes 20 | tf_op jit(solution)/shard_map/ppermute | solution.py:1488
  244.9 129.4 %copy-start = (f32[1024,128]{1,0:T(8,128)}, f32[1024,128]{1,0:T(8,128)S(1)}, u32[]{:S(2)}) copy-start(f32[1024,128]{1,0:T(8,128)S(1)} %fusion.68.bias_ref) | copy-start | bytes 1572868
  249.1 29.8 %copy-start.4 = (bf16[128,2688]{1,0:T(8,128)(2,1)}, bf16[128,2688]{1,0:T(8,128)(2,1)S(1)}, u32[]{:S(2)}) copy-start(bf16[128,2688]{1,0:T(8,128)(2,1)S(1)} %fusion.10.joined_ref.q_ref) | copy-start | bytes 2064388
  249.1 30.4 %copy-start.33 = (bf16[1,128,896]{2,1,0:T(8,128)(2,1)S(1)}, bf16[1,128,896]{2,1,0:T(8,128)(2,1)}, u32[]{:S(2)}) copy-start(bf16[1,128,896]{2,1,0:T(8,128)(2,1)} %param.22) | copy-start | bytes 688132
  275.6 4.8 copy-start.5
  275.6 4.8 copy-start.6
  275.6 4.8 copy-start.7
  280.5 4.5 copy-start.24
  280.5 6.0 copy-start.13
  287.6 3.0 copy-start.11
  312.2 3.4 copy-start.25
  312.2 34.6 %copy-start.9 = (f32[128,896]{1,0:T(8,128)S(1)}, f32[128,896]{1,0:T(8,128)}, u32[]{:S(2)}) copy-start(f32[128,896]{1,0:T(8,128)} %get-tuple-element.87) | copy-start | bytes 1376260
  344.9 1.9 copy-start.1
  346.8 13.0 %copy-start.3 = (bf16[128,896]{1,0:T(8,128)(2,1)}, bf16[128,896]{1,0:T(8,128)(2,1)S(1)}, u32[]{:S(2)}) copy-start(bf16[128,896]{1,0:T(8,128)(2,1)S(1)} %get-tuple-element.88.refs_10_) | copy-start | bytes 688132
  372.3 30.2 %copy-start.27 = (bf16[128,896]{1,0:T(8,128)(2,1)}, bf16[128,896]{1,0:T(8,128)(2,1)S(1)}, u32[]{:S(2)}) copy-start(bf16[128,896]{1,0:T(8,128)(2,1)S(1)} %convert_element_type.103.refs_11_) | copy-start | bytes 688132
  374.4 2.0 copy-start.2
  402.5 4.2 copy-start.17
  402.5 4.2 copy-start.15
  429.7 2.3 copy-start.14
  432.2 14.9 %copy-start.22 = (bf16[128,896]{1,0:T(8,128)(2,1)}, bf16[128,896]{1,0:T(8,128)(2,1)S(1)}, u32[]{:S(2)}) copy-start(bf16[128,896]{1,0:T(8,128)(2,1)S(1)} %get-tuple-element.204.refs_3_) | copy-start | bytes 688132
  447.1 2.0 copy-start.10
  451.8 4.2 copy-start.38
  451.8 4.2 copy-start.37
  451.8 4.2 copy-start.32
  451.8 4.2 copy-start.28
  454.7 3.8 collective-permute-start.2
  477.7 17.0 %copy-start.39 = (f32[1,896]{1,0:T(1,128)S(1)}, f32[1,896]{1,0:T(1,128)}, u32[]{:S(2)}) copy-start(f32[1,896]{1,0:T(1,128)} %get-tuple-element.134) | copy-start | bytes 10756
  496.4 4.8 copy-start.16
  784.0 6.5 copy-start.21
  786.2 5.8 copy-start.20
  790.5 3.7 copy-start.19
  792.0 3.7 copy-start.18
  793.5 3.7 copy-start.29
  795.7 2.5 copy-start.36
  795.7 3.1 copy-start.31
  795.7 3.8 copy-start.35
  (3 other events, 2.9 us)
Sparse Core Ops, SparseCore 0:
  237.5 112.5 all-gather.2
  447.2 48.0 reduce-scatter.1

commit v8 on v7

--- a/solution.py
+++ b/solution.py
@@ -999,8 +999,8 @@
     )(joined, keys_vals, bias, log_total, grad_mixed)
 
 
-PAIR_GROUPS = (((0, 1), (2, 1)), ((2, 3), (1, 2)), ((4, 5), (2, 1)), ((6,), (1, 2)))
-BACK_GROUPS = tuple(((pair,), ((2, 1), (1, 2))[pair % 2]) for pair in range(7))
+PAIR_GROUPS = tuple(((pair,), ((2, 1), (1, 2))[pair % 2]) for pair in range(7))
+BACK_GROUPS = PAIR_GROUPS
 BACK_LAGS = (2, 5, 7)
 
 
@@ -1088,18 +1088,15 @@
     for number in range(count):
         wait_all(step(number, 0))
         start_all(step(number, 1))
-    for number in range(count):
-        wait_all(step(number, 1))
-        start_all(step(number, 2))
-        if number > 0:
-            wait_all(step(number - 1, 2))
-            if number < count - 1:
-                compute(number - 1)
-    wait_all(step(count - 1, 2))
+    for time in range(count + 2):
+        if time < count:
+            wait_all(step(time, 1))
+            start_all(step(time, 2))
+        if time >= 2:
+            wait_all(step(time - 2, 2))
+            compute(time - 2)
     keep = pltpu.make_async_copy(held, kept_ref, load_sem.at[0])
     keep.start()
-    compute(count - 2)
-    compute(count - 1)
     keep.wait()
 
 

time: 817 us -> 820 us (level)
  transfers between devices with their start and end apart: 5 -> 5, of which waited for: 3 -> 3; matrix products, arithmetic and copies ran while one was open for 6% -> 6% of each run, Pallas kernels for 13% -> 12%
where the time goes in v8:
time: 820 us; the launch traced here: 809 us
  Pallas kernels  681 us (83%)
  matrix products  48.2 us (6%)
  local copies, waits for them, and re-layouts  34.4 us (4%)
  other arithmetic  17.5 us (2%)
  between operations  15.4 us (2%)
    pallas_call x1, Pallas kernels, reduce_gradients(): pl.pallas_call(functools.partial(reduce_kernel, sizes, tall), out_shape=[...  282 us
    pallas_call x1, Pallas kernels, gather_weights(): pl.pallas_call(functools.partial(gather_kernel, sizes), out_shape=out_sha...  223 us
    pallas_call x2, Pallas kernels, attend_gather(): pl.pallas_call(attend_gather_kernel, out_shape=[jax.ShapeDtypeStruct((row...  55 us
    dot_general x16, matrix products, dot(): lax.dot_general(left, right, dims, preferred_element_type=jnp.float32)  48.2 us
    pallas_call x3, Pallas kernels, ffn_back(): pl.pallas_call(ffn_back_kernel, grid=(FF // block,), out_shape=[jax.Shape...  42.4 us
    unnamed x110, local copies, waits for them, and re-layouts  26.4 us
    pallas_call x1, Pallas kernels, attend_scatter(): pl.pallas_call(attend_scatter_kernel, out_shape=[jax.ShapeDtypeStruct((ro...  26.1 us
    pallas_call x2, Pallas kernels, attend_back(): pl.pallas_call(attend_back_kernel, out_shape=[jax.ShapeDtypeStruct((queri...  19.9 us
  transfers between devices with their start and end apart: 5, of which 3 were waited for; matrix products, arithmetic and copies ran while one was open for 6% of the time, Pallas kernels for 12%

profile of v8, /device:TPU:0, one launch (start us, length us, event | category | flops | bytes accessed | tf_op | source)
XLA Modules:
  0.0 809.3 jit_solution(12072662957711926799)
XLA Ops:
  7.3 1.9 copy.70.refs_0_
  9.2 1.7 copy.71.refs_2_
  10.9 1.6 copy.72.refs_3_
  14.0 222.9 %gather_weights.1 = (bf16[4,2,2,56,3584]{4,3,2,1,0:T(8,128)(2,1)}, bf16[4,2,2,56,3584]{4,3,2,1,0:T(8,128)(2,1)}, bf16[4,2,2,56,10752]{4,3,2,1,0:T(8,128)(2,1)}, ...) custom-call(bf16[2,28,3584]{2,1,0:T(8,128)(2,1)} %copy.70.refs_0_, ...), custom_call_target="tpu_custom_call" | custom-call | tf_op jit(solution)/shard_map/gather_weights/pallas_call | solution.py:466
  237.1 2.1 slice_bitcast_fusion.2
  239.2 3.0 collective-permute-start.1
  242.3 1.9 collective-permute-start
  245.4 3.5 fusion.10.joined_ref.q_ref
  248.9 25.0 %attend_gather.2 = (bf16[128,896]{1,0:T(8,128)(2,1)S(1)}, f32[7,2,128]{2,1,0:T(2,128)S(1)}, bf16[2,2,2,128,1792]{4,3,2,1,0:T(8,128)(2,1)S(1)}) custom-call(bf16[128,2688]{1,0:T(8,128)(2,1)S(1)} %fusion.10.joined_ref.q_ref, f32[1024,128]{1,0:T(8,128)S(1)} %fusion.68.bias_ref), custom_call_target="tpu_custom_call" | custom-call | tf_op jit(solution)/shard_map/attend_gather/pallas_call | solution.py:1108
  274.0 3.2 multiply_reduce_fusion.7
  278.8 2.7 fusion.53.q_ref
  281.4 1.8 select_convert_fusion.spread_ref
  285.9 3.0 convolution_convert_fusion
  288.9 2.6 convolution_convert_fusion.1
  292.8 4.5 attend.1
  297.4 2.8 fusion.44.stream_ref
  300.1 7.4 ffn.1
  309.8 3.4 fusion.13.joined_ref
  313.2 30.1 %attend_gather.3 = (bf16[128,896]{1,0:T(8,128)(2,1)S(1)}, f32[7,2,128]{2,1,0:T(2,128)S(1)}, bf16[2,2,2,128,1792]{4,3,2,1,0:T(8,128)(2,1)S(1)}) custom-call(bf16[128,2688]{1,0:T(8,128)(2,1)S(1)} %fusion.13.joined_ref, f32[1024,128]{1,0:T(8,128)S(1)} %fusion.68.bias_ref), custom_call_target="tpu_custom_call" | custom-call | tf_op jit(solution)/shard_map/attend_gather/pallas_call | solution.py:1108
  343.3 1.9 copy-done.1
  345.2 2.9 fusion.47.stream_ref
  348.1 3.9 all-gather.3.cloned.1.call-done
  352.0 9.7 %late_ffn.1 = (f32[128,896]{1,0:T(8,128)}, bf16[128,896]{1,0:T(8,128)(2,1)}, bf16[128,3584]{1,0:T(8,128)(2,1)}, bf16[128,3584]{1,0:T(8,128)(2,1)}) custom-call(f32[128,896]{1,0:T(8,128)} %fusion.47.stream_ref, bf16[1,896]{1,0:T(2,128)(2,1)} %get-tuple-element.209.gain_ref, bf16[896,1024]{1,0:T(8,128)(2,1)} %select_convert_fusion.spread_ref, ...), custom_call_target="tpu_custom_call" | custom-call | flops 1644167168 | bytes 16056320 | tf_op jit(solution)/shard_map/late_ffn/pallas_call | solution.py:1404
  361.7 11.5 %late_ffn_back.1 = (f32[128,896]{1,0:T(8,128)}, bf16[128,896]{1,0:T(8,128)(2,1)}, bf16[128,3584]{1,0:T(8,128)(2,1)}, f32[1,896]{1,0:T(1,128)}) custom-call(f32[128,896]{1,0:T(8,128)} %bitcast_convert_fusion.grad_ref, f32[128,896]{1,0:T(8,128)} %fusion.47.stream_ref, bf16[1,896]{1,0:T(2,128)(2,1)} %get-tuple-element.209.gain_ref, ...), custom_call_target="tpu_custom_call" | custom-call | flops 1644167168 | bytes 16056320 | tf_op jit(solution)/shard_map/late_ffn_back/pallas_call | solution.py:1453
  374.2 2.1 fusion.59.grad_ref
  376.3 2.0 copy-done.2
  378.3 26.1 %attend_scatter.1 = (bf16[128,896]{1,0:T(8,128)(2,1)S(1)}, bf16[128,1792]{1,0:T(8,128)(2,1)S(1)}) custom-call(bf16[128,2688]{1,0:T(8,128)(2,1)S(1)} %fusion.13.joined_ref, bf16[2,2,2,128,1792]{4,3,2,1,0:T(8,128)(2,1)S(1)} %copy-done.2, f32[1024,128]{1,0:T(8,128)S(1)} %fusion.68.bias_ref, f32[7,2,128]{2,1,0:T(2,128)S(1)} %get-tuple-element.94.total_ref, ...), custom_call_target="tpu_custom_call" | custom-call | tf_op jit(solution)/shard_map/attend_scatter/pallas_call | solution.py:1211
  404.6 4.2 multiply_reduce_fusion.3
  409.7 9.5 %ffn_back.3 = (f32[128,896]{1,0:T(8,128)}, bf16[128,896]{1,0:T(8,128)(2,1)}, bf16[128,3584]{1,0:T(8,128)(2,1)}, f32[1,896]{1,0:T(1,128)}) custom-call(f32[128,896]{1,0:T(8,128)} %multiply_add_fusion.1.grad_ref, f32[128,896]{1,0:T(8,128)} %fusion.44.stream_ref, bf16[1,896]{1,0:T(2,128)(2,1)} %get-tuple-element.210.gain_ref, ...), custom_call_target="tpu_custom_call" | custom-call | flops 1644167168 | bytes 16515072 | tf_op jit(solution)/shard_map/ffn_back/pallas_call | solution.py:1327
  421.1 2.7 fusion.56.grad_ref
  423.8 8.0 attend_back.2
  431.8 2.3 multiply_reduce_fusion.2
  434.3 2.8 fusion.50.grad_ref
  437.1 11.9 %attend_back.3 = (bf16[128,896]{1,0:T(8,128)(2,1)}, bf16[1024,1792]{1,0:T(8,128)(2,1)}) custom-call(bf16[128,2688]{1,0:T(8,128)(2,1)} %copy-done.4, bf16[1024,1792]{1,0:T(8,128)(2,1)} %bitcast.78, f32[1024,128]{1,0:T(8,128)} %copy-done, f32[7,2,128]{2,1,0:T(2,128)} %copy-done.7, bf16[128,896]{1,0:T(8,128)(2,1)} %fusion.50.grad_ref), custom_call_target="tpu_custom_call" | custom-call | flops 2348810240 | bytes 7340032 | tf_op jit(solution)/shard_map/attend_back/pallas_call | solution.py:989
  451.0 2.6 fusion.27
  453.7 2.7 convolution_add_fusion
  458.7 1.8 collective-permute-done.2
  461.4 1.7 subtract_multiply_fusion.grad_ref
  463.0 16.6 %ffn_back.4 = (f32[512,896]{1,0:T(8,128)}, bf16[512,896]{1,0:T(8,128)(2,1)}, bf16[512,3584]{1,0:T(8,128)(2,1)}, f32[1,896]{1,0:T(1,128)}) custom-call(f32[512,896]{1,0:T(8,128)} %subtract_multiply_fusion.grad_ref, f32[512,896]{1,0:T(8,128)} %get-tuple-element.116.stream_ref, bf16[1,896]{1,0:T(2,128)(2,1)} %get-tuple-element.211.gain_ref, ...), custom_call_target="tpu_custom_call" | custom-call | flops 6576668672 | bytes 27525120 | tf_op jit(solution)/shard_map/ffn_back/pallas_call | solution.py:1327
  479.7 16.2 %ffn_back.5 = (f32[512,896]{1,0:T(8,128)}, bf16[512,896]{1,0:T(8,128)(2,1)}, bf16[512,3584]{1,0:T(8,128)(2,1)}, f32[1,896]{1,0:T(1,128)}) custom-call(f32[512,896]{1,0:T(8,128)} %get-tuple-element.120.grad_ref, bf16[512,896]{1,0:T(8,128)(2,1)} %bitcast.107, bf16[1,896]{1,0:T(2,128)(2,1)} %get-tuple-element.208.gain_ref, ...), custom_call_target="tpu_custom_call" | custom-call | flops 6576668672 | bytes 27525120 | tf_op jit(solution)/shard_map/ffn_back/pallas_call | solution.py:1327
  498.2 4.8 fusion.75
  504.0 281.9 %reduce_gradients.1 = (f32[2,28,3584]{2,1,0:T(8,128)}, f32[2,28,3584]{2,1,0:T(8,128)}, f32[2,28,2688]{2,1,0:T(8,128)}, f32[2,28,896]{2,1,0:T(8,128)}, f32[2,28,3...) custom-call(bf16[128,896]{1,0:T(8,128)(2,1)} %copy-done.23, ...), custom_call_target="tpu_custom_call" | custom-call | tf_op jit(solution)/shard_map/reduce_gradients/pallas_call | solution.py:890
  788.2 2.5 copy.77
  790.6 1.8 copy.78
  792.4 1.5 copy.79
  793.9 1.5 copy.80
  796.1 1.5 copy.82
  797.6 1.5 copy.83
  (175 shorter events, 28.9 us)
Async XLA Ops:
  7.2 5.3 copy-start.30
  7.2 6.1 copy-start.42
  7.2 6.1 copy-start.43
  7.2 6.1 copy-start.44
  7.2 6.1 copy-start.41
  7.2 344.8 %all-gather.3.cloned.1.call-start = ((), (), s32[]{:S(2)}) async-start(), calls=%async_computation.2 | async-start | bytes 15138816 | tf_op jit(solution)/shard_map/all_gather | solution.py:500
  237.0 5.2 copy-start.40
  237.0 5.2 copy-start.45
  237.0 7.2 copy-start.34
  237.0 7.4 copy-start.12
  237.0 260.1 %reduce-scatter.2.cloned.1.call-start = ((), (), s32[]{:S(2)}) async-start(), calls=%async_computation.1 | async-start | bytes 4128768 | tf_op jit(solution)/shard_map/reduce_scatter | solution.py:1519
  239.2 45.6 %collective-permute-start.1 = (bf16[1,256,896]{2,1,0:T(8,128)(2,1)S(1)}, bf16[1,256,896]{2,1,0:T(8,128)(2,1)}, u32[]{:S(2)}, u32[]{:S(2)}) collective-permute-start(bf16[1,256,896]{2,1,0:T(8,128)(2,1)S(1)} %get-tuple-element.206), channel_id=1, source_target_pairs={{0,1},{1,2},{2,3},{3,4},{4,5},{5,6},{6,7},{8,9},{9,10},{10,11},{11... | collective-permute-start | bytes 1376264 | tf_op jit(solution)/shard_map/ppermute | solution.py:1485
  242.3 41.0 %collective-permute-start = (bf16[1,2]{1,0:T(2,128)(2,1)S(1)}, bf16[1,2]{1,0:T(2,128)(2,1)S(1)}, u32[]{:S(2)}, u32[]{:S(2)}) collective-permute-start(bf16[1,2]{1,0:T(2,128)(2,1)S(1)} %get-tuple-element.212), channel_id=1, source_target_pairs={{0,1},{1,2},{2,3},{3,4},{4,5},{5,6},{6,7},{8,9},{9,10},{10,11},{11... | collective-permute-start | bytes 20 | tf_op jit(solution)/shard_map/ppermute | solution.py:1485
  244.8 131.5 %copy-start = (f32[1024,128]{1,0:T(8,128)}, f32[1024,128]{1,0:T(8,128)S(1)}, u32[]{:S(2)}) copy-start(f32[1024,128]{1,0:T(8,128)S(1)} %fusion.68.bias_ref) | copy-start | bytes 1572868
  248.9 28.3 %copy-start.4 = (bf16[128,2688]{1,0:T(8,128)(2,1)}, bf16[128,2688]{1,0:T(8,128)(2,1)S(1)}, u32[]{:S(2)}) copy-start(bf16[128,2688]{1,0:T(8,128)(2,1)S(1)} %fusion.10.joined_ref.q_ref) | copy-start | bytes 2064388
  248.9 28.9 %copy-start.33 = (bf16[1,128,896]{2,1,0:T(8,128)(2,1)S(1)}, bf16[1,128,896]{2,1,0:T(8,128)(2,1)}, u32[]{:S(2)}) copy-start(bf16[1,128,896]{2,1,0:T(8,128)(2,1)} %param.22) | copy-start | bytes 688132
  273.9 4.8 copy-start.5
  273.9 4.8 copy-start.6
  273.9 4.8 copy-start.7
  278.8 4.5 copy-start.24
  278.8 6.0 copy-start.13
  285.9 3.0 copy-start.11
  309.8 3.4 copy-start.25
  309.8 35.3 %copy-start.9 = (f32[128,896]{1,0:T(8,128)S(1)}, f32[128,896]{1,0:T(8,128)}, u32[]{:S(2)}) copy-start(f32[128,896]{1,0:T(8,128)} %get-tuple-element.87) | copy-start | bytes 1376260
  343.3 1.9 copy-start.1
  345.1 16.5 %copy-start.3 = (bf16[128,896]{1,0:T(8,128)(2,1)}, bf16[128,896]{1,0:T(8,128)(2,1)S(1)}, u32[]{:S(2)}) copy-start(bf16[128,896]{1,0:T(8,128)(2,1)S(1)} %get-tuple-element.88.refs_10_) | copy-start | bytes 688132
  374.2 30.3 %copy-start.27 = (bf16[128,896]{1,0:T(8,128)(2,1)}, bf16[128,896]{1,0:T(8,128)(2,1)S(1)}, u32[]{:S(2)}) copy-start(bf16[128,896]{1,0:T(8,128)(2,1)S(1)} %convert_element_type.103.refs_11_) | copy-start | bytes 688132
  376.3 2.0 copy-start.2
  404.6 4.2 copy-start.17
  404.6 4.2 copy-start.15
  431.8 2.3 copy-start.14
  434.3 14.7 %copy-start.22 = (bf16[128,896]{1,0:T(8,128)(2,1)}, bf16[128,896]{1,0:T(8,128)(2,1)S(1)}, u32[]{:S(2)}) copy-start(bf16[128,896]{1,0:T(8,128)(2,1)S(1)} %get-tuple-element.204.refs_3_) | copy-start | bytes 688132
  449.0 2.0 copy-start.10
  453.7 4.1 copy-start.38
  453.7 4.2 copy-start.37
  453.7 4.2 copy-start.32
  453.7 4.2 copy-start.28
  456.5 4.0 collective-permute-start.2
  479.7 16.9 %copy-start.39 = (f32[1,896]{1,0:T(1,128)S(1)}, f32[1,896]{1,0:T(1,128)}, u32[]{:S(2)}) copy-start(f32[1,896]{1,0:T(1,128)} %get-tuple-element.134) | copy-start | bytes 10756
  498.2 4.8 copy-start.16
  785.9 6.5 copy-start.21
  788.2 5.8 copy-start.20
  792.4 3.7 copy-start.19
  793.9 3.7 copy-start.18
  795.4 3.7 copy-start.29
  797.6 2.5 copy-start.36
  797.6 3.1 copy-start.31
  797.6 3.8 copy-start.35
  (3 other events, 2.9 us)
Sparse Core Ops, SparseCore 0:
  237.2 114.7 all-gather.2
  449.1 47.9 reduce-scatter.1
